TPU v7x, 32 devices: a whole 2x2x4 slice. The times are simulated.
32 devices in a mesh: batch: 8 (over y, x, core), group: 4 (over z).
Axes of the slice: x: 2, y: 2, z: 4, core: 2. Of those that a mesh axis runs over, the one named last changes fastest.
Arguments:
- tokens: bfloat16 [2, 8192, 1024], P(None, ('batch', 'group')), may hold values from -6 to 6
- memory: bfloat16 [2, 4096, 1024], P(None, ('batch', 'group')), may hold values from -6 to 6
- dec_segments: int32 [2, 8192], P(None, 'batch'), may hold values from 0 to 3, as said below
- enc_segments: int32 [2, 4096], P(None, 'batch'), may hold values from 0 to 3, as said below
- buckets: int32 [1024], replicated, may hold values from 0 to 31
- self_gain: float32 [1024], replicated, may hold values from 0.1 to 1.9
- self_query: bfloat16 [1024, 1024], P(None, 'group'), may hold values from -0.09375 to 0.09375
- self_key: bfloat16 [1024, 512], P(None, 'group'), may hold values from -0.09375 to 0.09375
- self_value: bfloat16 [1024, 512], P(None, 'group'), may hold values from -0.1875 to 0.1875
- self_output: bfloat16 [1024, 1024], P('group'), may hold values from -0.75 to 0.75
- rel_bias: float32 [32, 16], P(None, 'group'), may hold values from -4 to 4
- cross_gain: float32 [1024], replicated, may hold values from 0.1 to 1.9
- cross_query: bfloat16 [1024, 1024], P(None, 'group'), may hold values from -0.09375 to 0.09375
- cross_key: bfloat16 [1024, 512], P(None, 'group'), may hold values from -0.09375 to 0.09375
- cross_value: bfloat16 [1024, 512], P(None, 'group'), may hold values from -0.1875 to 0.1875
- cross_output: bfloat16 [1024, 1024], P('group'), may hold values from -0.75 to 0.75
- ffn_gain: float32 [1024], replicated, may hold values from 0.1 to 1.9
- ffn_gate: bfloat16 [1024, 2816], P(None, 'group'), may hold values from -0.1875 to 0.1875
- ffn_up: bfloat16 [1024, 2816], P(None, 'group'), may hold values from -0.1875 to 0.1875
- ffn_down: bfloat16 [2816, 1024], P('group'), may hold values from -0.109375 to 0.109375
- out_grad: bfloat16 [2, 8192, 1024], P(None, ('batch', 'group')), may hold values from -6 to 6
Outputs:
- block_out: bfloat16 [2, 8192, 1024], P(None, ('batch', 'group'))
- tokens_grad: float32 [2, 8192, 1024], P(None, ('batch', 'group'))
- memory_grad: float32 [2, 4096, 1024], P(None, ('batch', 'group'))
- self_gain_grad: float32 [1024], replicated
- self_query_grad: float32 [1024, 1024], P(None, 'group')
- self_key_grad: float32 [1024, 512], P(None, 'group')
- self_value_grad: float32 [1024, 512], P(None, 'group')
- self_output_grad: float32 [1024, 1024], P('group')
- rel_bias_grad: float32 [32, 16], P(None, 'group')
- cross_gain_grad: float32 [1024], replicated
- cross_query_grad: float32 [1024, 1024], P(None, 'group')
- cross_key_grad: float32 [1024, 512], P(None, 'group')
- cross_value_grad: float32 [1024, 512], P(None, 'group')
- cross_output_grad: float32 [1024, 1024], P('group')
- ffn_gain_grad: float32 [1024], replicated
- ffn_gate_grad: float32 [1024, 2816], P(None, 'group')
- ffn_up_grad: float32 [1024, 2816], P(None, 'group')
- ffn_down_grad: float32 [2816, 1024], P('group')
Inputs may be any that keep to these rules, and one draw needn't show every extreme that they name: `dec_segments`: within each aligned block of 1024 entries (one sequence) the ids never fall, start at 0 and take every value up to 3. `enc_segments`: within each aligned block of 512 entries (one sequence) the ids never fall, start at 0 and take every value up to 3.
All inputs are finite; a program needn't handle non-finite values.
Results may differ from a plain program's by a relative error of at most 0.028.
The roundings to bfloat16 on the way count: a program that leaves them out, or rounds other values in their place, can miss the bound.
Values may be sent and summed in bfloat16 or wider, within the bound.
No kernel may reach another device: no remote copies, remote signals or barrier semaphores. Data moves between devices by JAX's collectives and lax.ppermute only.
A program may use at most 320 MiB of HBM per device.

v0:
```python
import jax
import jax.numpy as jnp
from jax import lax
from jax.sharding import PartitionSpec as P

HEAD_DIM = 64


EPSILON = 1e-06
HIGHEST = lax.Precision.HIGHEST
CONTRACT_ROWS = (((0,), (0,)), ((), ()))
CONTRACT_COLS = (((1,), (1,)), ((), ()))


def for_sending(array):

    def short(part):
        return part.astype(jnp.bfloat16) if part.dtype == jnp.float32 else part

    return jax.tree.map(short, array)


def rms_scale(values, gain):
    return values * lax.rsqrt(jnp.mean(values * values, axis=-1, keepdims=True) + EPSILON) * gain


def norm_backward(values, gain, gradient):
    _, pull = jax.vjp(rms_scale, values, gain)
    return pull(gradient)


def gated_gelu(gate, upval):
    return jax.nn.gelu(gate, approximate=True) * upval


def multiply(left, right):
    return jnp.dot(left, right, preferred_element_type=jnp.float32)


def outer_rows(left, right):
    return lax.dot_general(left, right, CONTRACT_ROWS, preferred_element_type=jnp.float32)


def times_transpose(left, right):
    return lax.dot_general(left, right, CONTRACT_COLS, preferred_element_type=jnp.float32)


def take_rows(values, first_row, row_count):
    return lax.dynamic_slice_in_dim(values, first_row, row_count, 0)


def block_bias(distance_bias, first_row, block_rows):
    head_count, key_count = distance_bias.shape
    width = key_count + block_rows
    reversed_bias = jnp.concatenate(
        [distance_bias[:, ::-1], jnp.zeros((head_count, width), jnp.float32)], axis=1
    )
    along = lax.dynamic_slice_in_dim(reversed_bias, key_count - block_rows - first_row, width, 1)
    wrapped = jnp.roll(along, -(block_rows - 1), axis=1)
    tiled = jnp.tile(wrapped, (1, block_rows))[:, : block_rows * (width - 1)]
    return tiled.reshape(head_count, block_rows, width - 1)[:, :, :key_count]


def block_bias_grad(grad_rows, first_row):
    head_count, block_rows, key_count = grad_rows.shape
    width = key_count + block_rows
    padded = jnp.pad(grad_rows, ((0, 0), (0, 0), (0, width - 1 - key_count)))
    flat = jnp.pad(padded.reshape(head_count, -1), ((0, 0), (0, block_rows)))
    folded = jnp.sum(flat.reshape(head_count, block_rows, width), axis=1)
    along = jnp.roll(folded, block_rows - 1, axis=1)
    placed = lax.dynamic_update_slice_in_dim(
        jnp.zeros((head_count, 2 * key_count + block_rows), jnp.float32),
        along,
        key_count - block_rows - first_row,
        1,
    )
    return placed[:, :key_count][:, ::-1]


def block_scores(query_block, keys, first_row, query_seg, key_seg, distance_bias):
    block_rows = query_block.shape[0]
    key_count = keys.shape[0]
    scores = jnp.einsum("qgrd,kgd->grqk", query_block, keys, preferred_element_type=jnp.float32)
    seg_block = lax.dynamic_slice_in_dim(query_seg, first_row, block_rows, 0)
    allowed = seg_block[:, None] == key_seg[None, :]
    if distance_bias is not None:
        positions = first_row + jnp.arange(block_rows)
        distance = positions[:, None] - jnp.arange(key_count)[None, :]
        allowed = allowed & (distance >= 0)
        bias_rows = block_bias(distance_bias, first_row, block_rows)
        scores = scores + bias_rows.reshape(scores.shape)
    return (jnp.where(allowed, scores, -1e30), allowed)


def attend(query, keys, values, query_seg, key_seg, distance_bias):
    length = query.shape[0]
    block_rows = min(512, length)

    def one_block(block_index):
        first_row = block_index * block_rows
        query_block = take_rows(query, first_row, block_rows)
        scores, allowed = block_scores(
            query_block, keys, first_row, query_seg, key_seg, distance_bias
        )
        row_max = jnp.max(scores, axis=-1, keepdims=True)
        exponent = jnp.exp(scores - row_max)
        row_total = jnp.sum(exponent, axis=-1, keepdims=True)
        attn_probs = (exponent / row_total).astype(jnp.bfloat16)
        attended = jnp.einsum(
            "grqk,kgd->qgrd", attn_probs, values, preferred_element_type=jnp.float32
        )
        return (attended.astype(jnp.bfloat16), (row_max + jnp.log(row_total))[..., 0])

    attended, log_totals = lax.map(one_block, jnp.arange(length // block_rows))
    return (attended.reshape(length, -1), log_totals)


def attend_back(query, keys, values, grad_attended, log_totals, query_seg, key_seg, distance_bias):
    length = query.shape[0]
    key_count = keys.shape[0]
    block_rows = min(512, length)
    head_count = query.shape[1] * query.shape[2]

    def one_block(carry, block_index):
        grad_keys, grad_values, grad_distance = carry
        first_row = block_index * block_rows
        query_block = take_rows(query, first_row, block_rows)
        grad_block = take_rows(grad_attended, first_row, block_rows)
        scores, allowed = block_scores(
            query_block, keys, first_row, query_seg, key_seg, distance_bias
        )
        attn_probs = jnp.where(allowed, jnp.exp(scores - log_totals[block_index][..., None]), 0.0)
        grad_values = grad_values + jnp.einsum(
            "grqk,qgrd->kgd",
            attn_probs.astype(jnp.bfloat16),
            grad_block,
            preferred_element_type=jnp.float32,
        )
        grad_probs = jnp.einsum(
            "qgrd,kgd->grqk", grad_block, values, preferred_element_type=jnp.float32
        )
        inner_sum = jnp.sum(attn_probs * grad_probs, axis=-1, keepdims=True)
        grad_scores = attn_probs * (grad_probs - inner_sum)
        low_scores = grad_scores.astype(jnp.bfloat16)
        grad_query = jnp.einsum(
            "grqk,kgd->qgrd", low_scores, keys, preferred_element_type=jnp.float32
        )
        grad_keys = grad_keys + jnp.einsum(
            "grqk,qgrd->kgd", low_scores, query_block, preferred_element_type=jnp.float32
        )
        if distance_bias is not None:
            grad_distance = grad_distance + block_bias_grad(
                grad_scores.reshape(head_count, block_rows, key_count), first_row
            )
        return ((grad_keys, grad_values, grad_distance), grad_query.astype(jnp.bfloat16))

    initial = (
        jnp.zeros(keys.shape, jnp.float32),
        jnp.zeros(values.shape, jnp.float32),
        jnp.zeros((head_count, key_count), jnp.float32),
    )
    (grad_keys, grad_values, grad_distance), grad_query = lax.scan(
        one_block, initial, jnp.arange(length // block_rows)
    )
    return (
        grad_query.reshape(length, -1),
        grad_keys.astype(jnp.bfloat16).reshape(key_count, -1),
        grad_values.astype(jnp.bfloat16).reshape(key_count, -1),
        grad_distance,
    )


def batch_sum(parts):
    return jax.tree.map(
        lambda part: part.astype(jnp.float32), lax.psum(for_sending(parts), "batch")
    )


def per_device(
    tokens,
    memory,
    dec_segments,
    enc_segments,
    buckets,
    self_gain,
    self_query,
    self_key,
    self_value,
    self_output,
    rel_bias,
    cross_gain,
    cross_query,
    cross_key,
    cross_value,
    cross_output,
    ffn_gain,
    ffn_gate,
    ffn_up,
    ffn_down,
    out_grad,
):
    micro_count, shard_rows, model_width = tokens.shape
    enc_shard = memory.shape[1]
    groups = self_key.shape[1] // HEAD_DIM
    bucket_count = rel_bias.shape[0]
    onehot = (buckets[:, None] == jnp.arange(bucket_count)[None, :]).astype(jnp.float32)
    distance_bias = lax.dot_general(
        rel_bias,
        onehot,
        (((0,), (1,)), ((), ())),
        precision=HIGHEST,
        preferred_element_type=jnp.float32,
    )
    weight_list = {
        "self_query": self_query,
        "self_key": self_key,
        "self_value": self_value,
        "self_output": self_output,
        "rel_bias": rel_bias,
        "cross_query": cross_query,
        "cross_key": cross_key,
        "cross_value": cross_value,
        "cross_output": cross_output,
        "ffn_gate": ffn_gate,
        "ffn_up": ffn_up,
        "ffn_down": ffn_down,
    }
    grads = {name: jnp.zeros(weight.shape, jnp.float32) for name, weight in weight_list.items()}
    ffn_names = ("ffn_gate", "ffn_up", "ffn_down")
    cross_names = ("cross_query", "cross_key", "cross_value", "cross_output")
    self_names = ("self_query", "self_key", "self_value", "self_output", "rel_bias")
    summed = {}
    gain_one = jnp.zeros((model_width,), jnp.float32)
    gain_two = jnp.zeros((model_width,), jnp.float32)
    gain_three = jnp.zeros((model_width,), jnp.float32)
    results, token_grads, memory_grads = ([], [], [])
    for micro_index in range(micro_count):
        dec_seg = dec_segments[micro_index]
        enc_seg = enc_segments[micro_index]
        stream = tokens[micro_index].astype(jnp.float32)
        normed_one = rms_scale(stream, self_gain).astype(jnp.bfloat16)
        full_one, full_memory = (
            lax.all_gather(normed_one, "group", axis=0, tiled=True),
            lax.all_gather(memory[micro_index], "group", axis=0, tiled=True),
        )
        length = full_one.shape[0]
        enc_length = full_memory.shape[0]
        query_one = (
            multiply(full_one, self_query)
            .astype(jnp.bfloat16)
            .reshape(length, groups, -1, HEAD_DIM)
        )
        keys_one = (
            multiply(full_one, self_key).astype(jnp.bfloat16).reshape(length, groups, HEAD_DIM)
        )
        values_one = (
            multiply(full_one, self_value).astype(jnp.bfloat16).reshape(length, groups, HEAD_DIM)
        )
        attended_one, totals_one = attend(
            query_one, keys_one, values_one, dec_seg, dec_seg, distance_bias
        )
        stream_one = stream + lax.psum_scatter(
            multiply(
                take_rows(attended_one, jnp.int32(0), shard_rows * lax.axis_size("group")),
                self_output,
            ),
            "group",
            scatter_dimension=0,
            tiled=True,
        )
        normed_two = rms_scale(stream_one, cross_gain).astype(jnp.bfloat16)
        full_two = lax.all_gather(normed_two, "group", axis=0, tiled=True)
        query_two = (
            multiply(full_two, cross_query)
            .astype(jnp.bfloat16)
            .reshape(length, groups, -1, HEAD_DIM)
        )
        keys_two = (
            multiply(full_memory, cross_key)
            .astype(jnp.bfloat16)
            .reshape(enc_length, groups, HEAD_DIM)
        )
        values_two = (
            multiply(full_memory, cross_value)
            .astype(jnp.bfloat16)
            .reshape(enc_length, groups, HEAD_DIM)
        )
        attended_two, totals_two = attend(query_two, keys_two, values_two, dec_seg, enc_seg, None)
        stream_two = stream_one + lax.psum_scatter(
            multiply(
                take_rows(attended_two, jnp.int32(0), shard_rows * lax.axis_size("group")),
                cross_output,
            ).astype(jnp.bfloat16),
            "group",
            scatter_dimension=0,
            tiled=True,
        ).astype(jnp.float32)
        normed_three = rms_scale(stream_two, ffn_gain).astype(jnp.bfloat16)
        full_three = lax.all_gather(normed_three, "group", axis=0, tiled=True)
        gate = multiply(full_three, ffn_gate)
        upval = multiply(full_three, ffn_up)
        hidden = gated_gelu(gate, upval).astype(jnp.bfloat16)
        block_out = stream_two + lax.psum_scatter(
            multiply(
                take_rows(hidden, jnp.int32(0), shard_rows * lax.axis_size("group")), ffn_down
            ).astype(jnp.bfloat16),
            "group",
            scatter_dimension=0,
            tiled=True,
        ).astype(jnp.float32)
        results.append(block_out.astype(jnp.bfloat16))
        cotangent = out_grad[micro_index].astype(jnp.float32)
        full_grad = lax.all_gather(cotangent.astype(jnp.bfloat16), "group", axis=0, tiled=True)
        grads["ffn_down"] = grads["ffn_down"] + outer_rows(hidden, full_grad)
        grad_hidden = times_transpose(full_grad, ffn_down).astype(jnp.bfloat16)
        grad_hidden = lax.optimization_barrier(grad_hidden).astype(jnp.float32)
        _, pull = jax.vjp(gated_gelu, gate, upval)
        grad_gate, grad_up = pull(grad_hidden)
        grad_gate = grad_gate.astype(jnp.bfloat16)
        grad_up = grad_up.astype(jnp.bfloat16)
        grads["ffn_gate"] = grads["ffn_gate"] + outer_rows(full_three, grad_gate)
        grads["ffn_up"] = grads["ffn_up"] + outer_rows(full_three, grad_up)
        first_row = jnp.int32(0)
        row_count = shard_rows * lax.axis_size("group")
        grad_normed = lax.psum_scatter(
            (
                times_transpose(take_rows(grad_gate, first_row, row_count), ffn_gate)
                + times_transpose(take_rows(grad_up, first_row, row_count), ffn_up)
            ).astype(jnp.bfloat16),
            "group",
            scatter_dimension=0,
            tiled=True,
        ).astype(jnp.float32)
        grad_stream, grad_gain = norm_backward(stream_two, ffn_gain, grad_normed)
        gain_three = gain_three + grad_gain
        cotangent = cotangent + grad_stream
        full_grad = lax.all_gather(cotangent.astype(jnp.bfloat16), "group", axis=0, tiled=True)
        grads["cross_output"] = grads["cross_output"] + outer_rows(attended_two, full_grad)
        grad_attended = (
            times_transpose(full_grad, cross_output)
            .astype(jnp.bfloat16)
            .reshape(length, groups, -1, HEAD_DIM)
        )
        grad_query_two, grad_keys_two, grad_values_two, _ = attend_back(
            query_two, keys_two, values_two, grad_attended, totals_two, dec_seg, enc_seg, None
        )
        grads["cross_query"] = grads["cross_query"] + outer_rows(full_two, grad_query_two)
        grads["cross_key"] = grads["cross_key"] + outer_rows(full_memory, grad_keys_two)
        grads["cross_value"] = grads["cross_value"] + outer_rows(full_memory, grad_values_two)
        cross_first_row = jnp.int32(0)
        cross_row_count = shard_rows * lax.axis_size("group")
        token_part = times_transpose(
            take_rows(grad_query_two, cross_first_row, cross_row_count), cross_query
        )
        enc_first = cross_first_row * enc_length // length
        enc_count = cross_row_count * enc_length // length
        memory_part = times_transpose(
            take_rows(grad_keys_two, enc_first, enc_count), cross_key
        ) + times_transpose(take_rows(grad_values_two, enc_first, enc_count), cross_value)
        combined = lax.psum_scatter(
            jnp.concatenate([token_part, memory_part.reshape(cross_row_count, -1)], axis=1).astype(
                jnp.bfloat16
            ),
            "group",
            scatter_dimension=0,
            tiled=True,
        ).astype(jnp.float32)
        memory_grads.append(combined[:, model_width:].reshape(enc_shard, model_width))
        grad_stream, grad_gain = norm_backward(stream_one, cross_gain, combined[:, :model_width])
        gain_two = gain_two + grad_gain
        cotangent = cotangent + grad_stream
        full_grad = lax.all_gather(cotangent.astype(jnp.bfloat16), "group", axis=0, tiled=True)
        grads["self_output"] = grads["self_output"] + outer_rows(attended_one, full_grad)
        grad_attended = (
            times_transpose(full_grad, self_output)
            .astype(jnp.bfloat16)
            .reshape(length, groups, -1, HEAD_DIM)
        )
        grad_query_one, grad_keys_one, grad_values_one, grad_distance = attend_back(
            query_one,
            keys_one,
            values_one,
            grad_attended,
            totals_one,
            dec_seg,
            dec_seg,
            distance_bias,
        )
        grads["rel_bias"] = grads["rel_bias"] + lax.dot_general(
            onehot,
            grad_distance,
            (((0,), (1,)), ((), ())),
            precision=HIGHEST,
            preferred_element_type=jnp.float32,
        )
        grads["self_query"] = grads["self_query"] + outer_rows(full_one, grad_query_one)
        grads["self_key"] = grads["self_key"] + outer_rows(full_one, grad_keys_one)
        grads["self_value"] = grads["self_value"] + outer_rows(full_one, grad_values_one)
        self_first_row = jnp.int32(0)
        self_row_count = shard_rows * lax.axis_size("group")
        grad_normed = lax.psum_scatter(
            (
                times_transpose(
                    take_rows(grad_query_one, self_first_row, self_row_count), self_query
                )
                + times_transpose(
                    take_rows(grad_keys_one, self_first_row, self_row_count), self_key
                )
                + times_transpose(
                    take_rows(grad_values_one, self_first_row, self_row_count), self_value
                )
            ).astype(jnp.bfloat16),
            "group",
            scatter_dimension=0,
            tiled=True,
        ).astype(jnp.float32)
        grad_stream, grad_gain = norm_backward(stream, self_gain, grad_normed)
        gain_one = gain_one + grad_gain
        token_grads.append(cotangent + grad_stream)
    all_names = self_names + cross_names + ffn_names
    summed.update(zip(all_names, batch_sum(tuple((grads[name] for name in all_names)))))
    gain_one, gain_two, gain_three = lax.psum((gain_one, gain_two, gain_three), ("batch", "group"))
    return (
        jnp.stack(results),
        jnp.stack(token_grads),
        jnp.stack(memory_grads),
        gain_one,
        summed["self_query"],
        summed["self_key"],
        summed["self_value"],
        summed["self_output"],
        summed["rel_bias"],
        gain_two,
        summed["cross_query"],
        summed["cross_key"],
        summed["cross_value"],
        summed["cross_output"],
        gain_three,
        summed["ffn_gate"],
        summed["ffn_up"],
        summed["ffn_down"],
    )


def solution(mesh):
    return jax.shard_map(
        per_device,
        mesh=mesh,
        in_specs=(
            P(None, ("batch", "group"), None),
            P(None, ("batch", "group"), None),
            P(None, "batch"),
            P(None, "batch"),
            P(),
            P(),
            P(None, "group"),
            P(None, "group"),
            P(None, "group"),
            P("group", None),
            P(None, "group"),
            P(),
            P(None, "group"),
            P(None, "group"),
            P(None, "group"),
            P("group", None),
            P(),
            P(None, "group"),
            P(None, "group"),
            P("group", None),
            P(None, ("batch", "group"), None),
        ),
        out_specs=(
            P(None, ("batch", "group"), None),
            P(None, ("batch", "group"), None),
            P(None, ("batch", "group"), None),
            P(),
            P(None, "group"),
            P(None, "group"),
            P(None, "group"),
            P("group", None),
            P(None, "group"),
            P(),
            P(None, "group"),
            P(None, "group"),
            P(None, "group"),
            P("group", None),
            P(),
            P(None, "group"),
            P(None, "group"),
            P("group", None),
        ),
        check_vma=False,
    )
```

profile of v0, /device:TPU:0, one launch (start us, length us, event | category | flops | bytes accessed | tf_op | source)
XLA Modules:
  0.0 2401.4 jit_solution(11724922568362944052)
XLA Ops:
  13.9 46.7 %all-gather.19.cloned.1.call-done = bf16[1024,1024]{1,0:T(8,128)(2,1)} async-done(((bf16[256,1024]{1,0:T(8,128)(2,1)}), bf16[1024,1024]{1,0:T(8,128)(2,1)}) %all-gather.19.cloned.1.call-update) | async-done | bytes 2097168 | tf_op jit(solution)/shard_map/all_gather | solution.py:243
  66.3 166.3 %while.120 = (s32[]{:T(128)}, bf16[2,512,2,2,64]{1,4,3,2,0:T(8,128)(2,1)}, f32[2,2,2,512]{3,2,1,0:T(2,128)}, s32[2]{0:T(128)S(1)}, s32[1024]{0:T(1024)}, /*index...) while((s32[]{:T(128)}, ...), condition=%wide.region_4.5_spmd, body=%wide.region_1.4_spmd.sunk | while | flops 555880960 | bytes 178584112 | solution.py:114
  73.7 19.9 copy.127
  244.8 154.2 %while.122 = (s32[]{:T(128)}, bf16[2,512,2,2,64]{1,4,3,2,0:T(8,128)(2,1)}, f32[2,2,2,512]{3,2,1,0:T(2,128)}, s32[2]{0:T(128)S(1)}, s32[1024]{0:T(1024)}, /*index...) while((s32[]{:T(128)}, ...), condition=%wide.region_18.19_spmd, body=%wide.region_15.18_spmd.sunk | while | flops 555880960 | bytes 178584112 | solution.py:114
  251.8 19.9 copy.128
  406.6 73.7 %reduce-scatter.19.cloned.1.call-done = f32[256,1024]{1,0:T(8,128)} async-done(((f32[1024,1024]{1,0:T(8,128)}), f32[256,1024]{1,0:T(8,128)}) %reduce-scatter.19.cloned.1.call-update) | async-done | bytes 1048592 | tf_op jit(solution)/shard_map/reduce_scatter | solution.py:262
  485.3 25.6 %all-gather.39.cloned.1.call-done = bf16[1,512,1024]{2,1,0:T(8,128)(2,1)} async-done(((bf16[1,128,1024]{2,1,0:T(8,128)(2,1)}), bf16[1,512,1024]{2,1,0:T(8,128)(2,1)}) %all-gather.39.cloned.1.call-update) | async-done | bytes 1048592 | tf_op jit(solution)/shard_map/all_gather | solution.py:244
  515.7 42.2 %all-gather.21.cloned.1.call-done = bf16[1024,1024]{1,0:T(8,128)(2,1)} async-done(((bf16[256,1024]{1,0:T(8,128)(2,1)}), bf16[1024,1024]{1,0:T(8,128)(2,1)}) %all-gather.21.cloned.1.call-update) | async-done | bytes 2097168 | tf_op jit(solution)/shard_map/all_gather | solution.py:272
  584.6 40.2 %reduce-scatter.15.cloned.1.call-done = bf16[256,1024]{1,0:T(8,128)(2,1)} async-done(((bf16[1024,1024]{1,0:T(8,128)(2,1)}), bf16[256,1024]{1,0:T(8,128)(2,1)}) %reduce-scatter.15.cloned.1.call-update) | async-done | bytes 524304 | tf_op jit(solution)/shard_map/reduce_scatter | solution.py:289
  629.2 42.6 %all-gather.43.cloned.1.call-done = bf16[1,1024,1024]{2,1,0:T(8,128)(2,1)} async-done(((bf16[1,256,1024]{2,1,0:T(8,128)(2,1)}), bf16[1,1024,1024]{2,1,0:T(8,128)(2,1)}) %all-gather.43.cloned.1.call-update) | async-done | bytes 2097168 | tf_op jit(solution)/shard_map/all_gather | solution.py:313
  676.6 41.8 %all-gather.23.cloned.1.call-done = bf16[1024,1024]{1,0:T(8,128)(2,1)} async-done(((bf16[256,1024]{1,0:T(8,128)(2,1)}), bf16[1024,1024]{1,0:T(8,128)(2,1)}) %all-gather.23.cloned.1.call-update) | async-done | bytes 2097168 | tf_op jit(solution)/shard_map/all_gather | solution.py:299
  733.5 42.5 %reduce-scatter.25.cloned.1.call-done = bf16[256,1024]{1,0:T(8,128)(2,1)} async-done(((bf16[1024,1024]{1,0:T(8,128)(2,1)}), bf16[256,1024]{1,0:T(8,128)(2,1)}) %reduce-scatter.25.cloned.1.call-update) | async-done | bytes 524304 | tf_op jit(solution)/shard_map/reduce_scatter | solution.py:325
  782.2 44.9 %all-gather.31.cloned.1.call-done = bf16[1024,1024]{1,0:T(8,128)(2,1)} async-done(((bf16[256,1024]{1,0:T(8,128)(2,1)}), bf16[1024,1024]{1,0:T(8,128)(2,1)}) %all-gather.31.cloned.1.call-update) | async-done | bytes 2097168 | tf_op jit(solution)/shard_map/all_gather | solution.py:337
  831.7 27.2 %while.124 = (s32[]{:T(128)}, f32[512,2,64]{0,2,1:T(8,128)}, f32[512,2,64]{0,2,1:T(8,128)}, bf16[2,512,2,2,64]{1,4,3,2,0:T(8,128)(2,1)}, s32[2]{0:T(128)}, /*ind...) while((s32[]{:T(128)}, f32[512,2,64]{0,2,1:T(8,128)}, ...), condition=%wide.region_32.33_spmd.clone, body=%wide.region_30.32_spmd.clone.sunk | while | flops 687470592 | bytes 49480252 | solution.py:162
  875.0 57.3 %reduce-scatter.27.cloned.1.call-done = bf16[256,1536]{1,0:T(8,128)(2,1)} async-done(((bf16[1024,1536]{1,0:T(8,128)(2,1)}), bf16[256,1536]{1,0:T(8,128)(2,1)}) %reduce-scatter.27.cloned.1.call-update) | async-done | bytes 786448 | tf_op jit(solution)/shard_map/reduce_scatter | solution.py:360
  937.3 25.1 %all-gather.41.cloned.1.call-done = bf16[1,512,1024]{2,1,0:T(8,128)(2,1)} async-done(((bf16[1,128,1024]{2,1,0:T(8,128)(2,1)}), bf16[1,512,1024]{2,1,0:T(8,128)(2,1)}) %all-gather.41.cloned.1.call-update) | async-done | bytes 1048592 | tf_op jit(solution)/shard_map/all_gather | solution.py:244
  967.2 42.2 %all-gather.27.cloned.1.call-done = bf16[1024,1024]{1,0:T(8,128)(2,1)} async-done(((bf16[256,1024]{1,0:T(8,128)(2,1)}), bf16[1024,1024]{1,0:T(8,128)(2,1)}) %all-gather.27.cloned.1.call-update) | async-done | bytes 2097168 | tf_op jit(solution)/shard_map/all_gather | solution.py:272
  1036.4 42.0 %reduce-scatter.21.cloned.1.call-done = bf16[256,1024]{1,0:T(8,128)(2,1)} async-done(((bf16[1024,1024]{1,0:T(8,128)(2,1)}), bf16[256,1024]{1,0:T(8,128)(2,1)}) %reduce-scatter.21.cloned.1.call-update) | async-done | bytes 524304 | tf_op jit(solution)/shard_map/reduce_scatter | solution.py:289
  1082.9 42.4 %all-gather.45.cloned.1.call-done = bf16[1,1024,1024]{2,1,0:T(8,128)(2,1)} async-done(((bf16[1,256,1024]{2,1,0:T(8,128)(2,1)}), bf16[1,1024,1024]{2,1,0:T(8,128)(2,1)}) %all-gather.45.cloned.1.call-update) | async-done | bytes 2097168 | tf_op jit(solution)/shard_map/all_gather | solution.py:313
  1130.1 41.7 %all-gather.29.cloned.1.call-done = bf16[1024,1024]{1,0:T(8,128)(2,1)} async-done(((bf16[256,1024]{1,0:T(8,128)(2,1)}), bf16[1024,1024]{1,0:T(8,128)(2,1)}) %all-gather.29.cloned.1.call-update) | async-done | bytes 2097168 | tf_op jit(solution)/shard_map/all_gather | solution.py:299
  1192.3 37.3 %reduce-scatter.31.cloned.1.call-done = bf16[256,1024]{1,0:T(8,128)(2,1)} async-done(((bf16[1024,1024]{1,0:T(8,128)(2,1)}), bf16[256,1024]{1,0:T(8,128)(2,1)}) %reduce-scatter.31.cloned.1.call-update) | async-done | bytes 524304 | tf_op jit(solution)/shard_map/reduce_scatter | solution.py:325
  1231.7 43.6 %reduce-scatter.17.cloned.1.call-done = bf16[256,1024]{1,0:T(8,128)(2,1)} async-done(((bf16[1024,1024]{1,0:T(8,128)(2,1)}), bf16[256,1024]{1,0:T(8,128)(2,1)}) %reduce-scatter.17.cloned.1.call-update) | async-done | bytes 524304 | tf_op jit(solution)/shard_map/reduce_scatter | solution.py:303
  1280.7 44.2 %all-gather.35.cloned.1.call-done = bf16[1024,1024]{1,0:T(8,128)(2,1)} async-done(((bf16[256,1024]{1,0:T(8,128)(2,1)}), bf16[1024,1024]{1,0:T(8,128)(2,1)}) %all-gather.35.cloned.1.call-update) | async-done | bytes 2097168 | tf_op jit(solution)/shard_map/all_gather | solution.py:337
  1390.1 42.9 %reduce-scatter.33.cloned.1.call-done = bf16[256,1536]{1,0:T(8,128)(2,1)} async-done(((bf16[1024,1536]{1,0:T(8,128)(2,1)}), bf16[256,1536]{1,0:T(8,128)(2,1)}) %reduce-scatter.33.cloned.1.call-update) | async-done | bytes 786448 | tf_op jit(solution)/shard_map/reduce_scatter | solution.py:360
  1435.6 43.9 %reduce-scatter.23.cloned.1.call-done = bf16[256,1024]{1,0:T(8,128)(2,1)} async-done(((bf16[1024,1024]{1,0:T(8,128)(2,1)}), bf16[256,1024]{1,0:T(8,128)(2,1)}) %reduce-scatter.23.cloned.1.call-update) | async-done | bytes 524304 | tf_op jit(solution)/shard_map/reduce_scatter | solution.py:303
  1483.3 314.6 %while.125 = (s32[]{:T(128)}, f32[1024,2,64]{0,2,1:T(8,128)S(1)}, f32[1024,2,64]{0,2,1:T(8,128)S(1)}, f32[4,1024]{1,0:T(4,128)S(1)}, bf16[2,512,2,2,64]{1,4,3,2,...) while((s32[]{:T(128)}, f32[1024,2,64]{0,2,1:T(8,128)S(1)}, ...), condition=%wide.region_38.39_spmd.clone, body=%wide.region_35.38_spmd.clone.sunk | while | flops 1371156992 | bytes 364257792 | solution.py:162
  1660.4 19.9 copy.130
  1816.1 314.4 %while.127 = (s32[]{:T(128)}, f32[1024,2,64]{0,2,1:T(8,128)S(1)}, f32[1024,2,64]{0,2,1:T(8,128)S(1)}, f32[4,1024]{1,0:T(4,128)S(1)}, bf16[2,512,2,2,64]{1,4,3,2,...) while((s32[]{:T(128)}, f32[1024,2,64]{0,2,1:T(8,128)S(1)}, ...), condition=%wide.region_51.52_spmd.clone, body=%wide.region_48.51_spmd.clone.sunk | while | flops 1371156992 | bytes 366355008 | solution.py:162
  2166.8 89.1 %all-reduce.12.cloned.1.call-done = (bf16[1024,128]{0,1:T(8,128)(2,1)}, bf16[1024,128]{0,1:T(8,128)(2,1)}, bf16[1024,256]{1,0:T(8,128)(2,1)}, bf16[1024,128]{1,0...) async-done(((bf16[1024,128]{0,1:T(8,128)(2,1)}, ...) | async-done | bytes 7471120 | tf_op jit(solution)/shard_map/psum | solution.py:175
  2273.7 29.0 %reduce-scatter.29.cloned.1.call-done = bf16[256,1024]{1,0:T(8,128)(2,1)} async-done(((bf16[1024,1024]{1,0:T(8,128)(2,1)}), bf16[256,1024]{1,0:T(8,128)(2,1)}) %reduce-scatter.29.cloned.1.call-update) | async-done | bytes 524304 | tf_op jit(solution)/shard_map/reduce_scatter | solution.py:401
  2302.6 45.0 %reduce-scatter.35.cloned.1.call-done = bf16[256,1024]{1,0:T(8,128)(2,1)} async-done(((bf16[1024,1024]{1,0:T(8,128)(2,1)}), bf16[256,1024]{1,0:T(8,128)(2,1)}) %reduce-scatter.35.cloned.1.call-update) | async-done | bytes 524304 | tf_op jit(solution)/shard_map/reduce_scatter | solution.py:401
  2354.8 39.5 %all-reduce.8 = (f32[1024]{0:T(1024)}, f32[1024]{0:T(1024)}, f32[1024]{0:T(1024)}) all-reduce(f32[1024]{0:T(1024)S(1)} %copy-done.160, f32[1024]{0:T(1024)S(1)} %copy-done.159, f32[1024]{0:T(1024)S(1)} %add.625), channel_id=1, replica_groups=mesh['batch'=8,'group'=4] {'batch','group'}, use_global_device_ids=true, to_apply=%region_56.57 | all-reduce | flops 3072 | bytes 24576 | tf_op jit(solution)/shard_map/psum | solution.py:422
  (1038 shorter events, 1214.9 us)
Async XLA Ops:
  7.2 715.1 %copy-start = (bf16[1024,704]{0,1:T(8,128)(2,1)S(1)}, bf16[1024,704]{0,1:T(8,128)(2,1)}, u32[]{:S(2)}) copy-start(bf16[1024,704]{0,1:T(8,128)(2,1)} %param.54) | copy-start | bytes 4325380
  7.3 53.3 %all-gather.19.cloned.1.call-start = ((), (), s32[]{:S(2)}) async-start(), calls=%async_computation.12 | async-start | bytes 2621440 | tf_op jit(solution)/shard_map/all_gather | solution.py:243
  12.1 226.3 %all-gather.25.cloned.1.call-start = ((), (), s32[]{:S(2)}) async-start(), calls=%async_computation.18 | async-start | bytes 2621440 | tf_op jit(solution)/shard_map/all_gather | solution.py:243
  12.8 393.8 %reduce-scatter.13.cloned.1.call-start = ((), (), s32[]{:S(2)}) async-start(), calls=%async_computation.13 | async-start | bytes 5242880 | tf_op jit(solution)/shard_map/reduce_scatter | solution.py:262
  66.3 169.2 %copy-start.72 = (bf16[256,1024]{1,0:T(8,128)(2,1)S(1)}, bf16[256,1024]{1,0:T(8,128)(2,1)}, u32[]{:S(2)}) copy-start(bf16[256,1024]{1,0:T(8,128)(2,1)} %param.46) | copy-start | bytes 1572868
  238.3 242.0 %reduce-scatter.19.cloned.1.call-start = ((), (), s32[]{:S(2)}) async-start(), calls=%async_computation.19 | async-start | bytes 5242880 | tf_op jit(solution)/shard_map/reduce_scatter | solution.py:262
  244.8 157.1 %copy-start.73 = (bf16[256,1024]{1,0:T(8,128)(2,1)S(1)}, bf16[256,1024]{1,0:T(8,128)(2,1)}, u32[]{:S(2)}) copy-start(bf16[256,1024]{1,0:T(8,128)(2,1)} %param.46) | copy-start | bytes 1572868
  404.7 106.1 %all-gather.39.cloned.1.call-start = ((), (), s32[]{:S(2)}) async-start(), calls=%async_computation.34 | async-start | bytes 1310720 | tf_op jit(solution)/shard_map/all_gather | solution.py:244
  406.6 151.3 %all-gather.21.cloned.1.call-start = ((), (), s32[]{:S(2)}) async-start(), calls=%async_computation.14 | async-start | bytes 2621440 | tf_op jit(solution)/shard_map/all_gather | solution.py:272
  485.2 139.6 %reduce-scatter.15.cloned.1.call-start = ((), (), s32[]{:S(2)}) async-start(), calls=%async_computation.15 | async-start | bytes 2621440 | tf_op jit(solution)/shard_map/reduce_scatter | solution.py:289
  582.2 89.6 %all-gather.43.cloned.1.call-start = ((), (), s32[]{:S(2)}) async-start(), calls=%async_computation.36 | async-start | bytes 2621440 | tf_op jit(solution)/shard_map/all_gather | solution.py:313
  584.5 133.9 %all-gather.23.cloned.1.call-start = ((), (), s32[]{:S(2)}) async-start(), calls=%async_computation.16 | async-start | bytes 2621440 | tf_op jit(solution)/shard_map/all_gather | solution.py:299
  629.2 146.9 %reduce-scatter.25.cloned.1.call-start = ((), (), s32[]{:S(2)}) async-start(), calls=%async_computation.24 | async-start | bytes 2621440 | tf_op jit(solution)/shard_map/reduce_scatter | solution.py:325
  733.5 93.6 %all-gather.31.cloned.1.call-start = ((), (), s32[]{:S(2)}) async-start(), calls=%async_computation.25 | async-start | bytes 2621440 | tf_op jit(solution)/shard_map/all_gather | solution.py:337
  782.1 150.1 %reduce-scatter.27.cloned.1.call-start = ((), (), s32[]{:S(2)}) async-start(), calls=%async_computation.26 | async-start | bytes 3932160 | tf_op jit(solution)/shard_map/reduce_scatter | solution.py:360
  872.9 89.4 %all-gather.41.cloned.1.call-start = ((), (), s32[]{:S(2)}) async-start(), calls=%async_computation.35 | async-start | bytes 1310720 | tf_op jit(solution)/shard_map/all_gather | solution.py:244
  873.7 135.7 %all-gather.27.cloned.1.call-start = ((), (), s32[]{:S(2)}) async-start(), calls=%async_computation.20 | async-start | bytes 2621440 | tf_op jit(solution)/shard_map/all_gather | solution.py:272
  937.2 141.2 %reduce-scatter.21.cloned.1.call-start = ((), (), s32[]{:S(2)}) async-start(), calls=%async_computation.21 | async-start | bytes 2621440 | tf_op jit(solution)/shard_map/reduce_scatter | solution.py:289
  1035.8 89.5 %all-gather.45.cloned.1.call-start = ((), (), s32[]{:S(2)}) async-start(), calls=%async_computation.37 | async-start | bytes 2621440 | tf_op jit(solution)/shard_map/all_gather | solution.py:313
  1036.4 135.4 %all-gather.29.cloned.1.call-start = ((), (), s32[]{:S(2)}) async-start(), calls=%async_computation.22 | async-start | bytes 2621440 | tf_op jit(solution)/shard_map/all_gather | solution.py:299
  1082.9 146.8 %reduce-scatter.31.cloned.1.call-start = ((), (), s32[]{:S(2)}) async-start(), calls=%async_computation.29 | async-start | bytes 2621440 | tf_op jit(solution)/shard_map/reduce_scatter | solution.py:325
  1187.0 88.3 %reduce-scatter.17.cloned.1.call-start = ((), (), s32[]{:S(2)}) async-start(), calls=%async_computation.17 | async-start | bytes 2621440 | tf_op jit(solution)/shard_map/reduce_scatter | solution.py:303
  1192.2 132.7 %all-gather.35.cloned.1.call-start = ((), (), s32[]{:S(2)}) async-start(), calls=%async_computation.30 | async-start | bytes 2621440 | tf_op jit(solution)/shard_map/all_gather | solution.py:337
  1279.8 107.1 %all-gather.33.cloned.1.call-start = ((), (), s32[]{:S(2)}) async-start(), calls=%async_computation.27 | async-start | bytes 2621440 | tf_op jit(solution)/shard_map/all_gather | solution.py:372
  1280.6 152.4 %reduce-scatter.33.cloned.1.call-start = ((), (), s32[]{:S(2)}) async-start(), calls=%async_computation.31 | async-start | bytes 3932160 | tf_op jit(solution)/shard_map/reduce_scatter | solution.py:360
  1354.7 124.7 %reduce-scatter.23.cloned.1.call-start = ((), (), s32[]{:S(2)}) async-start(), calls=%async_computation.23 | async-start | bytes 2621440 | tf_op jit(solution)/shard_map/reduce_scatter | solution.py:303
  1364.8 447.9 %all-gather.37.cloned.1.call-start = ((), (), s32[]{:S(2)}) async-start(), calls=%async_computation.32 | async-start | bytes 2621440 | tf_op jit(solution)/shard_map/all_gather | solution.py:372
  1390.1 89.4 %copy-start.151 = (f32[256]{0:T(256)S(1)}, f32[256]{0:T(256)}, u32[]{:S(2)}) copy-start(f32[256]{0:T(256)} %copy-done.149) | copy-start | bytes 3076
  1390.1 89.4 %copy-start.177 = (f32[256]{0:T(256)S(1)}, f32[256]{0:T(256)}, u32[]{:S(2)}) copy-start(f32[256]{0:T(256)} %copy-done.176) | copy-start | bytes 3076
  1483.2 772.8 %all-reduce.12.cloned.1.call-start = ((), (), s32[]{:S(2)}) async-start(), calls=%async_computation.38 | async-start | bytes 14942208 | tf_op jit(solution)/shard_map/psum | solution.py:175
  2138.9 163.8 %reduce-scatter.29.cloned.1.call-start = ((), (), s32[]{:S(2)}) async-start(), calls=%async_computation.28 | async-start | bytes 2621440 | tf_op jit(solution)/shard_map/reduce_scatter | solution.py:401
  2143.7 203.9 %reduce-scatter.35.cloned.1.call-start = ((), (), s32[]{:S(2)}) async-start(), calls=%async_computation.33 | async-start | bytes 2621440 | tf_op jit(solution)/shard_map/reduce_scatter | solution.py:401
  (259 other events, 2724.5 us)
Sparse Core Ops, SparseCore 0:
  12.2 48.3 all-gather.18
  62.7 44.4 all-gather.24
  238.4 75.5 reduce-scatter.12
  404.8 75.4 reduce-scatter.18
  482.3 28.4 all-gather.38
  512.8 45.0 all-gather.20
  582.3 42.4 reduce-scatter.14
  626.9 44.8 all-gather.42
  674.0 44.4 all-gather.22
  733.6 42.4 reduce-scatter.24
  782.2 44.8 all-gather.30
  873.0 59.1 reduce-scatter.26
  934.4 27.8 all-gather.40
  964.3 45.0 all-gather.26
  1035.9 42.4 reduce-scatter.20
  1080.4 44.8 all-gather.44
  1127.3 44.4 all-gather.28
  1187.2 42.4 reduce-scatter.30
  1232.5 42.8 reduce-scatter.16
  1280.0 44.8 all-gather.34
  1327.0 44.4 all-gather.32
  1373.8 59.2 reduce-scatter.32
  1435.9 43.5 reduce-scatter.22
  1483.3 44.8 all-gather.36
  2139.0 116.9 all-reduce.11
  2258.7 43.8 reduce-scatter.28
  2304.8 42.8 reduce-scatter.34
where the time goes:
time: 2410 us; the launch traced here: 2400 us
  waiting for transfers between devices  1030 us (43%)
  local copies, waits for them, and re-layouts  796 us (33%)
  matrix products  284 us (12%)
  other arithmetic  127 us (5%)
  loops' own time  94.1 us (4%)
  blocking collectives  53.8 us (2%)
    while x188, local copies, waits for them, and re-layouts  376 us
    all_gather x6, waiting for transfers between devices, per_device(): lax.all_gather(cotangent.astype(jnp.bfloat16), 'group', axis=0, tiled=True)  174 us
    reshape x8, local copies, waits for them, and re-layouts, block_bias(): return tiled.reshape(head_count, block_rows, width - 1)[:, :, :key_count]  157 us
    reduce_scatter x2, waiting for transfers between devices, per_device(): lax.psum_scatter(jnp.concatenate([token_part, memory_part.reshape(cross_r...  100 us
    psum x1, waiting for transfers between devices, batch_sum(): lax.psum(for_sending(parts), 'batch')  89.1 us
    reduce_scatter x2, waiting for transfers between devices, per_device(): lax.psum_scatter(multiply(take_rows(hidden, jnp.int32(0), shard_rows * la...  87.5 us
    all_gather x2, waiting for transfers between devices, per_device(): full_two = lax.all_gather(normed_two, 'group', axis=0, tiled=True)  84.5 us
    all_gather x2, waiting for transfers between devices, per_device(): full_three = lax.all_gather(normed_three, 'group', axis=0, tiled=True)  83.5 us
  transfers between devices with their start and end apart: 27, of which 23 were waited for; matrix products, arithmetic and copies ran while one was open for 30% of the time, Pallas kernels for 0%

commit v1 on v0

v1 whole, which is shorter than its diff:
```python
import functools

import jax
import jax.numpy as jnp
from jax import lax
from jax.experimental import pallas as pl
from jax.experimental.pallas import tpu as pltpu
from jax.sharding import PartitionSpec as P

HEAD_DIM = 64
PAIR = 2 * HEAD_DIM
EPSILON = 1e-06
MASKED = -1e30
HIGHEST = lax.Precision.HIGHEST
BF16 = jnp.bfloat16
F32 = jnp.float32


def dot_nn(left, right):
    return lax.dot_general(left, right, (((1,), (0,)), ((), ())), preferred_element_type=F32)


def dot_nt(left, right):
    return lax.dot_general(left, right, (((1,), (1,)), ((), ())), preferred_element_type=F32)


def dot_tn(left, right):
    return lax.dot_general(left, right, (((0,), (0,)), ((), ())), preferred_element_type=F32)


def call(kernel, outs, grid, in_specs, out_specs, scratch=(), prefetch=0):
    return pl.pallas_call(
        kernel,
        out_shape=outs,
        grid_spec=pltpu.PrefetchScalarGridSpec(
            num_scalar_prefetch=prefetch,
            grid=grid,
            in_specs=in_specs,
            out_specs=out_specs,
            scratch_shapes=list(scratch),
        ),
        compiler_params=pltpu.CompilerParams(
            dimension_semantics=("arbitrary",) * len(grid),
        ),
    )


def shape(*dims, dtype=BF16):
    return jax.ShapeDtypeStruct(dims, dtype)


def whole(array):
    dims = array.shape
    return pl.BlockSpec(dims, lambda *ids: (0,) * len(dims))


def fixed(*dims):
    return pl.BlockSpec(dims, lambda *ids: (0,) * len(dims))


def rows_of(ref):
    block = ref[...]
    return block.reshape(block.shape[0] * block.shape[2], block.shape[3])


def store_rows(ref, value):
    ref[...] = value.reshape(ref.shape).astype(ref.dtype)


def weight_spec(weights, columns, index):
    cols, _, blk, _ = weights.shape
    return pl.BlockSpec((cols, 1, blk, columns), index)


def norm(values, gain):
    return values * lax.rsqrt(jnp.mean(values * values, axis=-1, keepdims=True) + EPSILON) * gain


def norm_back(values, gain, grad):
    scale = lax.rsqrt(jnp.mean(values * values, axis=-1, keepdims=True) + EPSILON)
    scaled = grad * gain
    inner = jnp.mean(scaled * values, axis=-1, keepdims=True)
    grad_values = scale * scaled - values * (scale * scale * scale * inner)
    grad_gain = jnp.sum(grad * values * scale, axis=0, keepdims=True)
    return grad_values, grad_gain


def qkv_kernel(x_ref, gain_ref, own_ref, oth_ref, n_ref, q_ref, kv_ref):
    half = x_ref.shape[1] // 2
    qcols = q_ref.shape[1]

    @pl.when(pl.program_id(0) == 0)
    def _():
        n_ref[...] = norm(x_ref[...].astype(F32), gain_ref[...]).astype(BF16)

    out = dot_nn(n_ref[:, :half], rows_of(own_ref)) + dot_nn(n_ref[:, half:], rows_of(oth_ref))
    q_ref[...] = out[:, :qcols].astype(BF16)
    kv_ref[...] = out[:, qcols:].astype(BF16)


def project_qkv(x, gain, own, oth, qcols):
    rows, width = x.shape
    shards = own.shape[1]
    spec = weight_spec(own, 2 * qcols, lambda z: (0, z, 0, 0))
    out = pl.BlockSpec((rows, qcols), lambda z: (0, z))
    return call(
        qkv_kernel,
        (shape(rows, width), shape(rows, shards * qcols), shape(rows, shards * qcols)),
        (shards,),
        [whole(x), whole(gain), spec, spec],
        (fixed(rows, width), out, out),
    )(x, gain, own, oth)


def kv_kernel(x_ref, own_ref, oth_ref, kv_ref):
    half = x_ref.shape[1] // 2
    out = dot_nn(x_ref[:, :half], rows_of(own_ref)) + dot_nn(x_ref[:, half:], rows_of(oth_ref))
    kv_ref[...] = out.astype(BF16)


def project_kv(x, own, oth, qcols):
    rows, width = x.shape
    shards = own.shape[1]
    spec = weight_spec(own, qcols, lambda z: (0, z, 0, 1))
    return call(
        kv_kernel,
        shape(rows, shards * qcols),
        (shards,),
        [whole(x), spec, spec],
        pl.BlockSpec((rows, qcols), lambda z: (0, z)),
    )(x, own, oth)


def mid_kernel(shards, x_ref, att_ref, gain_ref, wo_own, wo_oth, wq_own, wq_oth, s_ref, n_ref, q_ref):
    step = pl.program_id(0)
    half = x_ref.shape[1] // 2

    @pl.when(step == 0)
    def _():
        s_ref[...] = x_ref[...].astype(F32)

    @pl.when(step < shards)
    def _():
        att = att_ref[...]
        s_ref[:, :half] += dot_nt(att, rows_of(wo_own))
        s_ref[:, half:] += dot_nt(att, rows_of(wo_oth))

    @pl.when(step == shards - 1)
    def _():
        n_ref[...] = norm(s_ref[...], gain_ref[...]).astype(BF16)

    @pl.when(step >= shards)
    def _():
        out = dot_nn(n_ref[:, :half], rows_of(wq_own)) + dot_nn(n_ref[:, half:], rows_of(wq_oth))
        q_ref[...] = out.astype(BF16)


def output_and_query(x, att, gain, own, oth, next_own, next_oth, qcols):
    rows, width = x.shape
    shards = own.shape[1]
    first = lambda i: jnp.minimum(i, shards - 1)
    second = lambda i: jnp.maximum(i - shards, 0)
    wo = weight_spec(own, qcols, lambda i: (0, first(i), 0, 2))
    wq = weight_spec(own, qcols, lambda i: (0, second(i), 0, 0))
    return call(
        functools.partial(mid_kernel, shards),
        (shape(rows, width, dtype=F32), shape(rows, width), shape(rows, shards * qcols)),
        (2 * shards,),
        [
            whole(x),
            pl.BlockSpec((rows, qcols), lambda i: (0, first(i))),
            whole(gain),
            wo,
            wo,
            wq,
            wq,
        ],
        (
            fixed(rows, width),
            fixed(rows, width),
            pl.BlockSpec((rows, qcols), lambda i: (0, second(i))),
        ),
    )(x, att, gain, own, oth, next_own, next_oth)


def out_kernel(x_ref, att_ref, gain_ref, wo_own, wo_oth, s_ref, n_ref):
    half = x_ref.shape[1] // 2

    @pl.when(pl.program_id(0) == 0)
    def _():
        s_ref[...] = x_ref[...]

    att = att_ref[...]
    s_ref[:, :half] += dot_nt(att, rows_of(wo_own))
    s_ref[:, half:] += dot_nt(att, rows_of(wo_oth))

    @pl.when(pl.program_id(0) == pl.num_programs(0) - 1)
    def _():
        n_ref[...] = norm(s_ref[...], gain_ref[...]).astype(BF16)


def output_and_norm(x, att, gain, own, oth, qcols):
    rows, width = x.shape
    shards = own.shape[1]
    wo = weight_spec(own, qcols, lambda z: (0, z, 0, 2))
    return call(
        out_kernel,
        (shape(rows, width, dtype=F32), shape(rows, width)),
        (shards,),
        [whole(x), pl.BlockSpec((rows, qcols), lambda z: (0, z)), whole(gain), wo, wo],
        (fixed(rows, width), fixed(rows, width)),
    )(x, att, gain, own, oth)


def ffn_kernel(n_ref, r_ref, own_ref, oth_ref, y_ref, dn_ref, gown_ref, goth_ref, nt_ref, rt_ref):
    half = n_ref.shape[1] // 2
    ff = own_ref.shape[3] // 3

    @pl.when(pl.program_id(0) == 0)
    def _():
        y_ref[...] = jnp.zeros_like(y_ref)
        dn_ref[...] = jnp.zeros_like(dn_ref)
        nt_ref[...] = n_ref[...].T
        rt_ref[...] = r_ref[...].T

    own, oth = rows_of(own_ref), rows_of(oth_ref)
    up_own, up_oth = own[:, : 2 * ff], oth[:, : 2 * ff]
    down_own, down_oth = own[:, 2 * ff :], oth[:, 2 * ff :]
    both = dot_nn(n_ref[:, :half], up_own) + dot_nn(n_ref[:, half:], up_oth)
    gate, upval = both[:, :ff], both[:, ff:]
    grad_hidden = dot_nn(r_ref[:, :half], down_own) + dot_nn(r_ref[:, half:], down_oth)
    grad_hidden = grad_hidden.astype(BF16).astype(F32)
    root = 0.7978845608028654
    square = gate * gate
    tanh = jnp.tanh(root * gate * (1.0 + 0.044715 * square))
    cdf = 0.5 * (1.0 + tanh)
    gelu = gate * cdf
    slope = cdf + 0.5 * gate * (1.0 - tanh * tanh) * root * (1.0 + 3 * 0.044715 * square)
    hidden = (gelu * upval).astype(BF16)
    grad_gate = (grad_hidden * upval * slope).astype(BF16)
    grad_up = (grad_hidden * gelu).astype(BF16)
    grad_both = jnp.concatenate([grad_gate, grad_up], axis=1)
    y_ref[:, :half] += dot_nt(hidden, down_own)
    y_ref[:, half:] += dot_nt(hidden, down_oth)
    dn_ref[:, :half] += dot_nt(grad_both, up_own)
    dn_ref[:, half:] += dot_nt(grad_both, up_oth)
    cols, _, blk, _ = gown_ref.shape
    for ref, first in ((gown_ref, 0), (goth_ref, half)):
        grad = dot_nn(nt_ref[first : first + half, :], grad_both).astype(BF16)
        ref[:, 0, :, : 2 * ff] = grad.reshape(cols, blk, 2 * ff)
        grad = dot_nn(rt_ref[first : first + half, :], hidden).astype(BF16)
        ref[:, 0, :, 2 * ff :] = grad.reshape(cols, blk, ff)


def feed_forward(n, r, own, oth):
    rows, width = n.shape
    cols, shards, blk, packed = own.shape
    spec = weight_spec(own, packed, lambda z: (0, z, 0, 0))
    return call(
        ffn_kernel,
        (
            shape(rows, width, dtype=F32),
            shape(rows, width, dtype=F32),
            shape(*own.shape),
            shape(*own.shape),
        ),
        (shards,),
        [whole(n), whole(r), spec, spec],
        (fixed(rows, width), fixed(rows, width), spec, spec),
        [pltpu.VMEM((width, rows), BF16), pltpu.VMEM((width, rows), BF16)],
    )(n, r, own, oth)


def after_ffn_kernel(
    s_ref, ya_ref, yb_ref, da_ref, db_ref, cot_ref, gain_ref, wo_own, wo_oth,
    out_ref, new_ref, round_ref, gg_ref, ga_ref,
):
    half = s_ref.shape[1] // 2

    @pl.when(pl.program_id(0) == 0)
    def _():
        s = s_ref[...]
        out_ref[...] = (s + ya_ref[...] + yb_ref[...]).astype(BF16)
        dv, gg = norm_back(s, gain_ref[...], da_ref[...] + db_ref[...])
        gg_ref[...] = gg
        new = cot_ref[...].astype(F32) + dv
        new_ref[...] = new
        round_ref[...] = new.astype(BF16)

    out = dot_nn(round_ref[:, :half], rows_of(wo_own)) + dot_nn(round_ref[:, half:], rows_of(wo_oth))
    ga_ref[...] = out.astype(BF16)


def after_ffn(s, ya, yb, da, db, cot, gain, own, oth, qcols):
    rows, width = s.shape
    shards = own.shape[1]
    wo = weight_spec(own, qcols, lambda z: (0, z, 0, 2))
    full = fixed(rows, width)
    return call(
        after_ffn_kernel,
        (
            shape(rows, width),
            shape(rows, width, dtype=F32),
            shape(rows, width),
            shape(1, width, dtype=F32),
            shape(rows, shards * qcols),
        ),
        (shards,),
        [full] * 6 + [whole(gain), wo, wo],
        (full, full, full, fixed(1, width), pl.BlockSpec((rows, qcols), lambda z: (0, z))),
    )(s, ya, yb, da, db, cot, gain, own, oth)


def slab_kernel(base_ref, out_ref):
    base = base_ref[0]
    eight = jnp.concatenate([base] + [pltpu.roll(base, i, 1) for i in range(1, 8)], axis=0)
    for block in range(out_ref.shape[1] // 8):
        moved = eight if block == 0 else pltpu.roll(eight, 8 * block, 1)
        out_ref[0, 8 * block : 8 * block + 8, :] = moved


def bias_slabs(distance_bias):
    heads, length = distance_bias.shape
    width = length + 128
    base = jnp.pad(distance_bias, ((0, 0), (128, 0))).reshape(heads, 1, width)
    return call(
        slab_kernel,
        shape(heads, 128, width, dtype=F32),
        (heads,),
        [pl.BlockSpec((1, 1, width), lambda h: (h, 0, 0))],
        pl.BlockSpec((1, 128, width), lambda h: (h, 0, 0)),
    )(base)


def stack_heads(block, low_lanes):
    lanes = lax.broadcasted_iota(jnp.int32, block.shape, 1) < HEAD_DIM
    wide = block.astype(F32)
    moved = pltpu.roll(wide, HEAD_DIM, 1)
    if low_lanes:
        parts = [jnp.where(lanes, wide, 0.0), jnp.where(lanes, moved, 0.0)]
    else:
        parts = [jnp.where(lanes, 0.0, moved), jnp.where(lanes, 0.0, wide)]
    return jnp.concatenate(parts, axis=0).astype(BF16)


def join_heads(transposed, rows, first):
    parts = [transposed[first : first + HEAD_DIM, :rows], transposed[first : first + HEAD_DIM, rows:]]
    return jnp.concatenate(parts, axis=0).T


def allowed_mask(kseg, qseg, causal):
    allowed = kseg == qseg
    if causal:
        keys, rows = allowed.shape
        key_at = lax.broadcasted_iota(jnp.int32, allowed.shape, 0) - (keys - rows)
        row_at = lax.broadcasted_iota(jnp.int32, allowed.shape, 1)
        allowed = allowed & (key_at <= row_at)
    return allowed


def head_bias(slab_ref, head, keys, rows):
    blocks = keys // 128
    last = keys - rows
    parts = []
    for block in range(blocks):
        at = last - 128 * block + 128
        parts.append(slab_ref[head, :, at : at + rows])
    return jnp.concatenate(parts, axis=0)


def attend_block(keys, rows, kv, q_ref, kseg, qseg, slab_ref, att_ref, lse_ref):
    stacked = stack_heads(q_ref[...], True)
    scores = dot_nt(kv, stacked)
    allowed = allowed_mask(kseg, qseg, slab_ref is not None)
    outs = []
    for head in range(2):
        part = scores[:, head * rows : (head + 1) * rows]
        if slab_ref is not None:
            part = part + head_bias(slab_ref, head, keys, rows)
        part = jnp.where(allowed, part, MASKED)
        top = jnp.max(part, axis=0, keepdims=True)
        grown = jnp.exp(part - top)
        total = jnp.sum(grown, axis=0, keepdims=True)
        probs = (grown * (1.0 / total)).astype(BF16)
        outs.append(dot_tn(kv, probs))
        lse_ref[0, :, head * rows : (head + 1) * rows] = top + jnp.log(total)
    att_ref[...] = join_heads(jnp.concatenate(outs, axis=1), rows, HEAD_DIM).astype(BF16)


def sort_keys(ids_ref, own_ref, oth_ref, sorted_ref):
    rows = sorted_ref.shape[1]
    for slot in range(4):
        source = own_ref if slot < 2 else oth_ref
        at = (slot % 2) * rows
        sorted_ref[ids_ref[slot]] = source[at : at + rows, :]


def self_kernel(ids_ref, q_ref, own_ref, oth_ref, slab_ref, kseg_ref, qseg_ref, att_ref, lse_ref, sorted_ref):
    rows = q_ref.shape[0]

    @pl.when(pl.program_id(1) == 0)
    def _():
        sort_keys(ids_ref, own_ref, oth_ref, sorted_ref)

    mine = ids_ref[pl.program_id(1)]
    for count in range(1, 5):

        @pl.when(mine == count - 1)
        def _(count=count):
            keys = count * rows
            kv = sorted_ref[0:count].reshape(keys, PAIR)
            attend_block(
                keys, rows, kv, q_ref, kseg_ref[0:keys, :], qseg_ref[0], slab_ref, att_ref, lse_ref
            )


def attention_specs(rows, groups):
    block = pl.BlockSpec((rows, PAIR), lambda g, s, *_: (s, g))
    lse = pl.BlockSpec((1, 1, 2 * rows), lambda g, s, *_: (2 * g + s, 0, 0))
    qseg = pl.BlockSpec((1, 1, rows), lambda g, s, *_: (s, 0, 0))
    return block, lse, qseg


def group_spec(array):
    return pl.BlockSpec((array.shape[0], PAIR), lambda g, s, *_: (0, g))


def self_attention(ids, q, own, oth, slabs, kseg, qseg):
    rows, groups = q.shape[0] // 2, q.shape[1] // PAIR
    block, lse, qs = attention_specs(rows, groups)
    slab = pl.BlockSpec((2,) + slabs.shape[1:], lambda g, s, *_: (g, 0, 0))
    return call(
        self_kernel,
        (shape(*q.shape), shape(2 * groups, 1, 2 * rows, dtype=F32)),
        (groups, 2),
        [block, group_spec(own), group_spec(oth), slab, whole(kseg), qs],
        (block, lse),
        [pltpu.VMEM((4, rows, PAIR), BF16)],
        1,
    )(ids, q, own, oth, slabs, kseg, qseg)


def cross_kernel(q_ref, own_ref, oth_ref, kseg_ref, qseg_ref, att_ref, lse_ref):
    kv = jnp.concatenate([own_ref[...], oth_ref[...]], axis=0)
    attend_block(
        kv.shape[0], q_ref.shape[0], kv, q_ref, kseg_ref[...], qseg_ref[0], None, att_ref, lse_ref
    )


def cross_attention(q, own, oth, kseg, qseg):
    rows, groups = q.shape[0] // 2, q.shape[1] // PAIR
    block, lse, qs = attention_specs(rows, groups)
    return call(
        cross_kernel,
        (shape(*q.shape), shape(2 * groups, 1, 2 * rows, dtype=F32)),
        (groups, 2),
        [block, group_spec(own), group_spec(oth), whole(kseg), qs],
        (block, lse),
    )(q, own, oth, kseg, qseg)


def back_block(keys, rows, kv, q_ref, ga_ref, lse_ref, kseg, qseg, slab_ref, dslab_ref, dq_ref):
    stacked = stack_heads(q_ref[...], True)
    stacked_grad = stack_heads(ga_ref[...], False)
    scores = dot_nt(kv, stacked)
    grad_probs = dot_nt(kv, stacked_grad)
    allowed = allowed_mask(kseg, qseg, slab_ref is not None)
    queries, grad_kv = [], 0.0
    for head in range(2):
        span = slice(head * rows, (head + 1) * rows)
        part = scores[:, span]
        if slab_ref is not None:
            part = part + head_bias(slab_ref, head, keys, rows)
        part = jnp.where(allowed, part, MASKED)
        probs = jnp.exp(part - lse_ref[0, :, span])
        grad = grad_probs[:, span]
        inner = jnp.sum(probs * grad, axis=0, keepdims=True)
        grad_scores = probs * (grad - inner)
        low = grad_scores.astype(BF16)
        grad_kv = grad_kv + dot_nn(low, stacked[span, :])
        grad_kv = grad_kv + dot_nn(probs.astype(BF16), stacked_grad[span, :])
        queries.append(dot_tn(kv, low))
        if slab_ref is not None:
            last = keys - rows
            for block in range(keys // 128):
                at = last - 128 * block + 128
                dslab_ref[head, :, at : at + rows] += grad_scores[128 * block : 128 * block + 128, :]
    dq_ref[...] = join_heads(jnp.concatenate(queries, axis=1), rows, 0).astype(BF16)
    return grad_kv


def self_back_kernel(
    ids_ref, q_ref, ga_ref, lse_ref, own_ref, oth_ref, slab_ref, kseg_ref, qseg_ref,
    dq_ref, down_ref, doth_ref, fold_ref, sorted_ref, dsorted_ref, dslab_ref,
):
    rows = q_ref.shape[0]

    @pl.when(pl.program_id(1) == 0)
    def _():
        sort_keys(ids_ref, own_ref, oth_ref, sorted_ref)
        dsorted_ref[...] = jnp.zeros_like(dsorted_ref)
        dslab_ref[...] = jnp.zeros_like(dslab_ref)

    mine = ids_ref[pl.program_id(1)]
    for count in range(1, 5):

        @pl.when(mine == count - 1)
        def _(count=count):
            keys = count * rows
            kv = sorted_ref[0:count].reshape(keys, PAIR)
            grad_kv = back_block(
                keys, rows, kv, q_ref, ga_ref, lse_ref, kseg_ref[0:keys, :], qseg_ref[0],
                slab_ref, dslab_ref, dq_ref,
            )
            dsorted_ref[0:count] += grad_kv.reshape(count, rows, PAIR)

    @pl.when(pl.program_id(1) == 1)
    def _():
        for slot in range(4):
            at = (slot % 2) * rows
            value = dsorted_ref[ids_ref[slot]]
            target = down_ref if slot < 2 else doth_ref
            target[at : at + rows, :] = value.astype(target.dtype)
        width = dslab_ref.shape[2]
        for head in range(2):
            folded = dslab_ref[head]
            count = folded.shape[0] // 2
            while count >= 8:
                folded = folded[:count] + pltpu.roll(folded[count:], width - count, 1)
                count //= 2
            fold_ref[head] = folded


def self_attention_back(ids, q, ga, lses, own, oth, slabs, kseg, qseg):
    rows, groups = q.shape[0] // 2, q.shape[1] // PAIR
    block, lse, qs = attention_specs(rows, groups)
    heads, _, width = slabs.shape
    slab = pl.BlockSpec((2,) + slabs.shape[1:], lambda g, s, *_: (g, 0, 0))
    return call(
        self_back_kernel,
        (
            shape(*q.shape),
            shape(*own.shape, dtype=F32),
            shape(*own.shape),
            shape(heads, 8, width, dtype=F32),
        ),
        (groups, 2),
        [block, block, lse, group_spec(own), group_spec(oth), slab, whole(kseg), qs],
        (
            block,
            group_spec(own),
            group_spec(own),
            pl.BlockSpec((2, 8, width), lambda g, s, *_: (g, 0, 0)),
        ),
        [
            pltpu.VMEM((4, rows, PAIR), BF16),
            pltpu.VMEM((4, rows, PAIR), F32),
            pltpu.VMEM((2, 128, width), F32),
        ],
        1,
    )(ids, q, ga, lses, own, oth, slabs, kseg, qseg)


def cross_back_kernel(
    q_ref, ga_ref, lse_ref, own_ref, oth_ref, kseg_ref, qseg_ref, dq_ref, down_ref, doth_ref, acc_ref
):
    kv = jnp.concatenate([own_ref[...], oth_ref[...]], axis=0)
    grad_kv = back_block(
        kv.shape[0], q_ref.shape[0], kv, q_ref, ga_ref, lse_ref, kseg_ref[...], qseg_ref[0],
        None, None, dq_ref,
    )
    half = own_ref.shape[0]

    @pl.when(pl.program_id(1) == 0)
    def _():
        acc_ref[...] = grad_kv

    @pl.when(pl.program_id(1) == 1)
    def _():
        total = acc_ref[...] + grad_kv
        down_ref[...] = total[:half]
        doth_ref[...] = total[half:].astype(BF16)


def cross_attention_back(q, ga, lses, own, oth, kseg, qseg):
    rows, groups = q.shape[0] // 2, q.shape[1] // PAIR
    block, lse, qs = attention_specs(rows, groups)
    return call(
        cross_back_kernel,
        (shape(*q.shape), shape(*own.shape, dtype=F32), shape(*own.shape)),
        (groups, 2),
        [block, block, lse, group_spec(own), group_spec(oth), whole(kseg), qs],
        (block, group_spec(own), group_spec(own)),
        [pltpu.VMEM((2 * own.shape[0], PAIR), F32)],
    )(q, ga, lses, own, oth, kseg, qseg)


def weight_grads(half, parts, own_ref, oth_ref):
    for ref, first in ((own_ref, 0), (oth_ref, half)):
        for left, right, at in parts:
            grad = dot_nn(left[first : first + half, :], right).astype(BF16)
            cols, _, blk, _ = ref.shape
            ref[:, 0, :, at : at + right.shape[1]] = grad.reshape(cols, blk, right.shape[1])


def cross_post_kernel(
    shards, dq_ref, dko_ref, dkr_ref, n_ref, mem_ref, r_ref, att_ref, s_ref, cot_ref, gain_ref,
    own_ref, oth_ref, wo_own, wo_oth,
    gown_ref, goth_ref, new_ref, round_ref, gg_ref, dmem_ref, ga_ref,
    dn_ref, dmo_ref, nt_ref, mt_ref, rt_ref,
):
    step = pl.program_id(0)
    half = n_ref.shape[1] // 2
    qcols = dq_ref.shape[1]

    @pl.when(step == 0)
    def _():
        dn_ref[...] = jnp.zeros_like(dn_ref)
        dmo_ref[...] = jnp.zeros_like(dmo_ref)
        nt_ref[...] = n_ref[...].T
        mt_ref[...] = mem_ref[...].T
        rt_ref[...] = r_ref[...].T

    @pl.when(step < shards)
    def _():
        dq = dq_ref[...]
        dkv = (dko_ref[...] + dkr_ref[...].astype(F32)).astype(BF16)
        own, oth = rows_of(own_ref), rows_of(oth_ref)
        parts = ((nt_ref, dq, 0), (mt_ref, dkv, qcols), (rt_ref, att_ref[...], 2 * qcols))
        weight_grads(half, parts, gown_ref, goth_ref)
        for w, span in ((own, slice(0, half)), (oth, slice(half, 2 * half))):
            dn_ref[:, span] += dot_nt(dq, w[:, :qcols])
            dmo_ref[:, span] += dot_nt(dkv, w[:, qcols : 2 * qcols])

    @pl.when(step == shards - 1)
    def _():
        dmem_ref[...] = dmo_ref[...].astype(BF16)
        dv, gg = norm_back(s_ref[...], gain_ref[...], dn_ref[...])
        gg_ref[...] = gg
        new = cot_ref[...] + dv
        new_ref[...] = new
        round_ref[...] = new.astype(BF16)

    @pl.when(step >= shards)
    def _():
        r = round_ref[...]
        out = dot_nn(r[:, :half], rows_of(wo_own)) + dot_nn(r[:, half:], rows_of(wo_oth))
        ga_ref[...] = out.astype(BF16)


def cross_post(dq, dko, dkr, n, mem, r, att, s, cot, gain, own, oth, next_own, next_oth, qcols):
    rows, width = n.shape
    cols, shards, blk, packed = own.shape
    first = lambda i: jnp.minimum(i, shards - 1)
    second = lambda i: jnp.maximum(i - shards, 0)
    spec = weight_spec(own, packed, lambda i: (0, first(i), 0, 0))
    wo = weight_spec(own, qcols, lambda i: (0, second(i), 0, 2))
    enc_rows = mem.shape[0]
    by_shard = pl.BlockSpec((rows, qcols), lambda i: (0, first(i)))
    enc_by_shard = pl.BlockSpec((enc_rows, qcols), lambda i: (0, first(i)))
    full = fixed(rows, width)
    return call(
        functools.partial(cross_post_kernel, shards),
        (
            shape(*own.shape),
            shape(*own.shape),
            shape(rows, width, dtype=F32),
            shape(rows, width),
            shape(1, width, dtype=F32),
            shape(enc_rows, width),
            shape(rows, shards * qcols),
        ),
        (2 * shards,),
        [by_shard, enc_by_shard, enc_by_shard, full, whole(mem), full, by_shard, full, full]
        + [whole(gain), spec, spec, wo, wo],
        (
            spec,
            spec,
            full,
            full,
            fixed(1, width),
            fixed(enc_rows, width),
            pl.BlockSpec((rows, qcols), lambda i: (0, second(i))),
        ),
        [
            pltpu.VMEM((rows, width), F32),
            pltpu.VMEM((enc_rows, width), F32),
            pltpu.VMEM((width, rows), BF16),
            pltpu.VMEM((width, enc_rows), BF16),
            pltpu.VMEM((width, rows), BF16),
        ],
    )(dq, dko, dkr, n, mem, r, att, s, cot, gain, own, oth, next_own, next_oth)


def self_post_kernel(
    dq_ref, dko_ref, dkr_ref, n_ref, r_ref, att_ref, x_ref, cot_ref, gain_ref, own_ref, oth_ref,
    gown_ref, goth_ref, out_ref, gg_ref, dn_ref, nt_ref, rt_ref,
):
    step = pl.program_id(0)
    half = n_ref.shape[1] // 2
    qcols = dq_ref.shape[1]

    @pl.when(step == 0)
    def _():
        dn_ref[...] = jnp.zeros_like(dn_ref)
        nt_ref[...] = n_ref[...].T
        rt_ref[...] = r_ref[...].T

    dkv = (dko_ref[...] + dkr_ref[...].astype(F32)).astype(BF16)
    grad = jnp.concatenate([dq_ref[...], dkv], axis=1)
    own, oth = rows_of(own_ref), rows_of(oth_ref)
    parts = ((nt_ref, grad, 0), (rt_ref, att_ref[...], 2 * qcols))
    weight_grads(half, parts, gown_ref, goth_ref)
    dn_ref[:, :half] += dot_nt(grad, own[:, : 2 * qcols])
    dn_ref[:, half:] += dot_nt(grad, oth[:, : 2 * qcols])

    @pl.when(step == pl.num_programs(0) - 1)
    def _():
        dv, gg = norm_back(x_ref[...].astype(F32), gain_ref[...], dn_ref[...])
        gg_ref[...] = gg
        out_ref[...] = (cot_ref[...] + dv).astype(BF16)


def self_post(dq, dko, dkr, n, r, att, x, cot, gain, own, oth, qcols):
    rows, width = n.shape
    cols, shards, blk, packed = own.shape
    spec = weight_spec(own, packed, lambda i: (0, i, 0, 0))
    by_shard = pl.BlockSpec((rows, qcols), lambda i: (0, i))
    full = fixed(rows, width)
    return call(
        self_post_kernel,
        (shape(*own.shape), shape(*own.shape), shape(rows, width), shape(1, width, dtype=F32)),
        (shards,),
        [by_shard, by_shard, by_shard, full, full, by_shard, full, full, whole(gain), spec, spec],
        (spec, spec, full, fixed(1, width)),
        [
            pltpu.VMEM((rows, width), F32),
            pltpu.VMEM((width, rows), BF16),
            pltpu.VMEM((width, rows), BF16),
        ],
    )(dq, dko, dkr, n, r, att, x, cot, gain, own, oth)


def make_per_device(batch, shards):
    cols = batch // 2
    bits = cols.bit_length() - 1
    assert batch == 2 * (1 << bits) and shards == 4

    def swap(array, mask):
        return lax.ppermute(array, "batch", [(b, b ^ mask) for b in range(batch)])

    def in_order(position):
        return ((position % cols) << 1) | (position // cols)

    def place_of(difference):
        return (difference >> 1) | ((difference & 1) * cols)

    def to_relative(array):
        me = lax.axis_index("batch")
        blk = array.shape[-1] // batch
        parts = [
            lax.dynamic_slice_in_dim(array, (me ^ in_order(p)) * blk, blk, array.ndim - 1)
            for p in range(batch)
        ]
        return jnp.concatenate(parts, axis=-1)

    def to_absolute(array):
        me = lax.axis_index("batch")
        blk = array.shape[-1] // batch
        parts = [
            lax.dynamic_slice_in_dim(array, place_of(me ^ p) * blk, blk, array.ndim - 1)
            for p in range(batch)
        ]
        return jnp.concatenate(parts, axis=-1)

    def core_of(z):
        return 0 if z in (0, 3) else 1

    routes = []
    for second in (0, 1):
        route = []
        for b in range(batch):
            for z in range(shards):
                micro = (z // 2) ^ second
                target = ((b - b % 2) + core_of(z)) * shards + 2 * micro + b % 2
                route.append((b * shards + z, target))
        routes.append(route)
    both = ("batch", "group")

    def to_sequence(array):
        first = lax.axis_index("group") // 2
        received = []
        for second, route in enumerate(routes):
            part = lax.dynamic_index_in_dim(array, first ^ second, 0, keepdims=False)
            received.append(lax.ppermute(part, both, route))
        return to_relative(jnp.concatenate(received, axis=0))

    def from_sequence(array):
        array = to_absolute(array)
        rows = array.shape[0] // 2
        back = [
            lax.ppermute(array[i * rows : (i + 1) * rows], both, [(t, s) for s, t in route])
            for i, route in enumerate(routes)
        ]
        first = lax.axis_index("group") // 2
        return jnp.where(first == 0, jnp.stack(back), jnp.stack(back[::-1]))

    def spread(piece, order):
        array = piece.reshape((1,) * bits + piece.shape)
        for bit in order:
            axis = bits - 1 - bit
            array = jnp.concatenate([array, swap(array, 2 << bit)], axis=axis)
        own = array.reshape((cols,) + piece.shape)
        return own, swap(own, 1)

    def collect(own, oth, order):
        total = own.astype(F32) + swap(oth, 1).astype(F32)
        piece = total.shape[1:]
        total = total.reshape((2,) * bits + piece)
        for bit in order:
            axis = bits - 1 - bit
            keep = lax.slice_in_dim(total, 0, 1, axis=axis)
            send = lax.slice_in_dim(total, 1, 2, axis=axis).astype(BF16)
            total = keep + swap(send, 2 << bit).astype(F32)
        return total.reshape(piece).astype(BF16)

    def per_device(
        tokens, memory, dec_segments, enc_segments, buckets,
        self_gain, self_query, self_key, self_value, self_output, rel_bias,
        cross_gain, cross_query, cross_key, cross_value, cross_output,
        ffn_gain, ffn_gate, ffn_up, ffn_down, out_grad,
    ):
        me, z = lax.axis_index("batch"), lax.axis_index("group")
        core, micro, owner = me % 2, z // 2, z % 2
        width = tokens.shape[2]
        blk = width // batch
        qcols = self_query.shape[1]
        chunk, enc_chunk = tokens.shape[1], memory.shape[1]
        up = tuple(range(bits))
        down = up[::-1]

        def interleaved(keys, values):
            parts = []
            for at in range(0, keys.shape[1], HEAD_DIM):
                parts += [keys[:, at : at + HEAD_DIM], values[:, at : at + HEAD_DIM]]
            return jnp.concatenate(parts, axis=1)

        def my_rows(weight):
            return lax.dynamic_slice_in_dim(weight, me * blk, blk, 0)

        def my_cols(weight):
            return lax.dynamic_slice_in_dim(weight, me * blk, blk, 1).T

        def gathered(parts):
            return lax.all_gather(jnp.concatenate(parts, axis=1), "group", axis=0, tiled=False)

        stream = to_sequence(tokens)
        self_piece = gathered(
            [my_rows(self_query), interleaved(my_rows(self_key), my_rows(self_value)), my_cols(self_output)]
        )
        self_own, self_oth = spread(self_piece, up)
        encoder = to_sequence(memory)
        cross_piece = gathered(
            [my_rows(cross_query), interleaved(my_rows(cross_key), my_rows(cross_value)), my_cols(cross_output)]
        )
        cross_own, cross_oth = spread(cross_piece, down)
        ffn_piece = gathered([my_rows(ffn_gate), my_rows(ffn_up), my_cols(ffn_down)])
        ffn_parts = [spread(ffn_piece[:2], up), spread(ffn_piece[2:], down)]
        cot = to_sequence(out_grad)

        segments = jnp.concatenate([dec_segments, enc_segments], axis=1)
        length = dec_segments.shape[1]
        chosen = jnp.where(owner == core, segments, swap(segments, 1))
        chosen = lax.dynamic_index_in_dim(chosen, micro, 0, keepdims=False)
        dec_seg, enc_seg = chosen[:length], chosen[length:]

        def ids_of(which):
            first = jnp.where(micro == 0, which, 3 - which)
            return [first, 3 - first]

        ids = jnp.stack(ids_of(core) + ids_of(1 - core)).astype(jnp.int32)

        def pieces_of(seg, size, count):
            return [lax.dynamic_slice_in_dim(seg, ids[i] * size, size, 0) for i in range(count)]

        qseg = jnp.stack(pieces_of(dec_seg, chunk, 2)).reshape(2, 1, chunk)
        kseg = dec_seg.reshape(length, 1)
        enc_kseg = jnp.concatenate(pieces_of(enc_seg, enc_chunk, 4)).reshape(-1, 1)

        all_bias = lax.all_gather(rel_bias, "group", axis=1, tiled=True)
        bucket_count = rel_bias.shape[0]
        onehot = (buckets[:, None] == jnp.arange(bucket_count)[None, :]).astype(F32)
        distance_bias = lax.dot_general(
            all_bias, onehot, (((0,), (1,)), ((), ())), precision=HIGHEST, preferred_element_type=F32
        )
        slabs = bias_slabs(distance_bias)
        gain_one, gain_two, gain_three = (
            to_relative(gain.reshape(1, width)) for gain in (self_gain, cross_gain, ffn_gain)
        )

        n_one, q_one, kv_one = project_qkv(stream, gain_one, self_own, self_oth, qcols)
        kv_one_oth = swap(kv_one, 1)
        att_one, lse_one = self_attention(ids, q_one, kv_one, kv_one_oth, slabs, kseg, qseg)
        kv_two = project_kv(encoder, cross_own, cross_oth, qcols)
        kv_two_oth = swap(kv_two, 1)
        stream_one, n_two, q_two = output_and_query(
            stream, att_one, gain_two, self_own, self_oth, cross_own, cross_oth, qcols
        )
        att_two, lse_two = cross_attention(q_two, kv_two, kv_two_oth, enc_kseg, qseg)
        stream_two, n_three = output_and_norm(stream_one, att_two, gain_three, cross_own, cross_oth, qcols)

        ffn_sums, ffn_grads = [], []
        for (own, oth), order in zip(ffn_parts, (down, up)):
            y, dn, grad_own, grad_oth = feed_forward(n_three, cot, own, oth)
            ffn_sums.append((y, dn))
            ffn_grads.append(collect(grad_own, grad_oth, order))
        (ya, da), (yb, db) = ffn_sums
        block_out, cot_two, round_two, grad_gain_three, ga_two = after_ffn(
            stream_two, ya, yb, da, db, cot, gain_three, cross_own, cross_oth, qcols
        )
        block_out = from_sequence(block_out)

        dq_two, dkv_two, dkv_two_send = cross_attention_back(
            q_two, ga_two, lse_two, kv_two, kv_two_oth, enc_kseg, qseg
        )
        grad_own, grad_oth, cot_one, round_one, grad_gain_two, memory_grad, ga_one = cross_post(
            dq_two, dkv_two, swap(dkv_two_send, 1), n_two, encoder, round_two, att_two, stream_one,
            cot_two, gain_two, cross_own, cross_oth, self_own, self_oth, qcols,
        )
        cross_grads = collect(grad_own, grad_oth, down)
        memory_grad = from_sequence(memory_grad).astype(F32)
        dq_one, dkv_one, dkv_one_send, folded = self_attention_back(
            ids, q_one, ga_one, lse_one, kv_one, kv_one_oth, slabs, kseg, qseg
        )
        grad_own, grad_oth, tokens_grad, grad_gain_one = self_post(
            dq_one, dkv_one, swap(dkv_one_send, 1), n_one, round_one, att_one, stream, cot_one,
            gain_one, self_own, self_oth, qcols,
        )
        self_grads = collect(grad_own, grad_oth, up)
        tokens_grad = from_sequence(tokens_grad).astype(F32)

        def finish(piece):
            mine = lax.psum_scatter(piece, "group", scatter_dimension=0, tiled=False)
            return lax.all_gather(mine, "batch", axis=0, tiled=True)

        ffn_final = finish(jnp.concatenate(ffn_grads, axis=0))
        cross_final = finish(cross_grads)
        self_final = finish(self_grads)

        padded = jnp.pad(folded, ((0, 0), (0, 0), (0, 8)))
        distance_grad = sum(padded[:, i, 128 + i : 128 + i + length] for i in range(8))
        bucket_grad = lax.dot_general(
            onehot, distance_grad, (((0,), (1,)), ((), ())), precision=HIGHEST, preferred_element_type=F32
        )
        small = [to_absolute(g).reshape(width) for g in (grad_gain_one, grad_gain_two, grad_gain_three)]
        small = lax.psum(jnp.concatenate(small + [bucket_grad.reshape(-1)]), both)
        gains = [small[i * width : (i + 1) * width] for i in range(3)]
        bucket_grad = small[3 * width :].reshape(bucket_grad.shape)
        heads_here = rel_bias.shape[1]
        bucket_grad = lax.dynamic_slice_in_dim(bucket_grad, z * heads_here, heads_here, 1)

        def unpack(final):
            final = final.astype(F32)
            kv = final[:, qcols : 2 * qcols].reshape(width, -1, 2, HEAD_DIM)
            return (
                final[:, :qcols],
                kv[:, :, 0, :].reshape(width, -1),
                kv[:, :, 1, :].reshape(width, -1),
                final[:, 2 * qcols :].T,
            )

        ff = ffn_gate.shape[1]
        ffn_final = ffn_final.astype(F32)
        return (
            block_out,
            tokens_grad,
            memory_grad,
            gains[0],
            *unpack(self_final),
            bucket_grad,
            gains[1],
            *unpack(cross_final),
            gains[2],
            ffn_final[:, :ff],
            ffn_final[:, ff : 2 * ff],
            ffn_final[:, 2 * ff :].T,
        )

    return per_device


def solution(mesh):
    rows, group_cols, group_rows = P(None, ("batch", "group"), None), P(None, "group"), P("group", None)
    layer = (group_cols, group_cols, group_cols, group_rows)
    return jax.shard_map(
        make_per_device(mesh.shape["batch"], mesh.shape["group"]),
        mesh=mesh,
        in_specs=(
            rows, rows, P(None, "batch"), P(None, "batch"), P(),
            P(), *layer, group_cols,
            P(), *layer,
            P(), group_cols, group_cols, group_rows, rows,
        ),
        out_specs=(
            rows, rows, rows,
            P(), *layer, group_cols,
            P(), *layer,
            P(), group_cols, group_cols, group_rows,
        ),
        check_vma=False,
    )
```

time: 2410 us -> 954 us (0.40)
  waiting for transfers between devices: 1030 us -> 243 us
  local copies, waits for them, and re-layouts: 796 us -> 198 us
  matrix products: 284 us -> 1.03 us
  Pallas kernels: 0 us -> 215 us
  loops' own time: 94.1 us -> 0 us
  starting transfers between devices: 1.43 us -> 75.5 us
  blocking collectives: 53.8 us -> 117 us
  other arithmetic: 127 us -> 75.4 us
    reduce_scatter x12 -> x3, waiting for transfers between devices: 497 us -> 57.1 us  [finish(): mine = lax.psum_scatter(piece, 'group', scatter_dimension=0, tiled=False)]
    all_gather x14 -> x4, waiting for transfers between devices: 439 us -> 10.9 us  [the longest x3 10.9 us: finish(): return lax.all_gather(mine, 'batch', axis=0, tiled=True)]
    while x196 -> x0, local copies, waits for them, and re-layouts: 388 us -> none
    dot_general x125 -> x2, matrix products: 284 us -> 1.03 us  [the longest x1 0.59 us: per_device(): lax.dot_general(onehot, distance_grad, (((0,), (1,)), ((), ())), precisio...]
    pallas_call x0 -> x14, Pallas kernels: none -> 215 us  [the longest x2 43.6 us: feed_forward(): call(ffn_kernel, (shape(rows, width, dtype=F32), shape(rows, width, dtype...]
    reshape x14 -> x12, local copies, waits for them, and re-layouts: 220 us -> 21.2 us  [the longest x2 12.8 us: spread(): own = array.reshape((cols,) + piece.shape)]
    ppermute x0 -> x41, waiting for transfers between devices: none -> 174 us  [the longest x29 145 us: swap(): return lax.ppermute(array, 'batch', [(b, b ^ mask) for b in range(batch)])]
    another operation x8 -> x0, loops' own time: 94.1 us -> none  [the longest x4 74.9 us: attend_back(): lax.scan(one_block, initial, jnp.arange(length // block_rows))]
  transfers between devices with their start and end apart: 27 -> 48, of which waited for: 23 -> 14; matrix products, arithmetic and copies ran while one was open for 30% -> 25% of each run, Pallas kernels for 0% -> 17%
where the time goes in v1:
time: 954 us; the launch traced here: 939 us
  waiting for transfers between devices  243 us (25%)
  Pallas kernels  215 us (23%)
  local copies, waits for them, and re-layouts  198 us (21%)
  blocking collectives  117 us (12%)
  starting transfers between devices  75.5 us (8%)
  other arithmetic  75.4 us (8%)
  between operations  15.5 us (2%)
    ppermute x29, waiting for transfers between devices, swap(): return lax.ppermute(array, 'batch', [(b, b ^ mask) for b in range(batch)])  145 us
    all_gather x2, blocking collectives, gathered(): lax.all_gather(jnp.concatenate(parts, axis=1), 'group', axis=0, tiled=False)  62.2 us
    unnamed x202, local copies, waits for them, and re-layouts  60.1 us
    reduce_scatter x3, waiting for transfers between devices, finish(): mine = lax.psum_scatter(piece, 'group', scatter_dimension=0, tiled=False)  57.1 us
    ppermute x12, local copies, waits for them, and re-layouts, swap(): return lax.ppermute(array, 'batch', [(b, b ^ mask) for b in range(batch)])  47.1 us
    pallas_call x2, Pallas kernels, feed_forward(): call(ffn_kernel, (shape(rows, width, dtype=F32), shape(rows, width, dtype...  43.6 us
    psum x1, blocking collectives, per_device(): small = lax.psum(jnp.concatenate(small + [bucket_grad.reshape(-1)]), both)  43 us
    ppermute x29, starting transfers between devices, swap(): return lax.ppermute(array, 'batch', [(b, b ^ mask) for b in range(batch)])  31.9 us
  transfers between devices with their start and end apart: 48, of which 14 were waited for; matrix products, arithmetic and copies ran while one was open for 25% of the time, Pallas kernels for 17%

profile of v1, /device:TPU:0, one launch (start us, length us, event | category | flops | bytes accessed | tf_op | source)
XLA Modules:
  0.0 939.3 jit_solution(3484897307949034329)
XLA Ops:
  18.2 33.3 %all-gather.1 = bf16[512,768]{0,1:T(8,128)(2,1)S(1)} all-gather(bf16[128,768]{0,1:T(8,128)(2,1)S(1)} %constant_dynamic-update-slice_fusion.34), channel_id=3, replica_groups=mesh['batch'=8,'group'=4] {'group'}, dimensions={0}, use_global_device_ids=true | all-gather | bytes 983040 | tf_op jit(solution)/shard_map/all_gather | solution.py:855
  57.9 28.9 %all-gather = bf16[512,768]{0,1:T(8,128)(2,1)S(1)} all-gather(bf16[128,768]{0,1:T(8,128)(2,1)S(1)} %constant_dynamic-update-slice_fusion.18), channel_id=2, replica_groups=mesh['batch'=8,'group'=4] {'group'}, dimensions={0}, use_global_device_ids=true | all-gather | bytes 983040 | tf_op jit(solution)/shard_map/all_gather | solution.py:855
  89.8 11.9 %all-gather.6 = f32[4,4,32]{2,1,0:T(4,128)S(1)} all-gather(f32[1,4,32]{2,1,0:T(4,128)S(1)} %bitcast.187), channel_id=1, replica_groups=mesh['batch'=8,'group'=4] {'group'}, dimensions={0}, use_global_device_ids=true | all-gather | bytes 2560 | tf_op jit(solution)/shard_map/all_gather | solution.py:890
  111.5 19.3 %collective-permute-done.15 = bf16[1,1,2,128,2112]{3,4,2,1,0:T(8,128)(2,1)} collective-permute-done((bf16[1,1,2,128,2112]{3,4,2,1,0:T(8,128)(2,1)}, bf16[1,1,2,128,2112]{3,4,2,1,0:T(8,128)(2,1)}, u32[]{:S(2)}, u32[]{:S(2)}) %collective-permute-start.15) | collective-permute-done | bytes 1081376 | tf_op jit(solution)/shard_map/ppermute | solution.py:750
  154.8 11.2 %shard_map.341.slab_ref = f32[16,128,1152]{2,1,0:T(8,128)} custom-call(f32[16,1,1152]{2,1,0:T(1,128)} %reshape.168.base_ref), custom_call_target="tpu_custom_call" | custom-call | tf_op jit(solution)/shard_map/pallas_call | solution.py:326
  173.3 46.1 %collective-permute-done.3 = bf16[1,2,4,128,768]{4,3,2,1,0:T(8,128)(2,1)} collective-permute-done((bf16[1,2,4,128,768]{4,3,2,1,0:T(8,128)(2,1)}, bf16[1,2,4,128,768]{4,3,2,1,0:T(8,128)(2,1)}, u32[]{:S(2)}, u32[]{:S(2)}) %collective-permute-start.3) | collective-permute-done | bytes 1572896 | tf_op jit(solution)/shard_map/ppermute | solution.py:750
  264.2 9.9 %collective-permute-done.14 = bf16[256,1024]{1,0:T(8,128)(2,1)} collective-permute-done((bf16[256,1024]{1,0:T(8,128)(2,1)}, bf16[256,1024]{1,0:T(8,128)(2,1)}, u32[]{:S(2)}, u32[]{:S(2)}) %collective-permute-start.14) | collective-permute-done | bytes 524320 | tf_op jit(solution)/shard_map/ppermute | solution.py:795
  279.8 15.6 %collective-permute-start.1 = (bf16[256,1024]{1,0:T(8,128)(2,1)}, bf16[256,1024]{1,0:T(8,128)(2,1)S(1)}, u32[]{:S(2)}, u32[]{:S(2)}) collective-permute-start(bf16[256,1024]{1,0:T(8,128)(2,1)} %get-tuple-element.215), channel_id=1, source_target_pairs={{0,2},{1,6},{2,4},{3,0},{4,3},{5,7},{6,5},{7,1},{8,10},{9,14},{10,... | collective-permute-start | bytes 1572872 | tf_op jit(solution)/shard_map/ppermute | solution.py:795
  298.9 8.2 collective-permute-done.1
  319.2 10.5 %collective-permute-start.5 = (bf16[512,1024]{1,0:T(8,128)(2,1)}, bf16[512,1024]{1,0:T(8,128)(2,1)}, u32[]{:S(2)}, u32[]{:S(2)}) collective-permute-start(bf16[512,1024]{1,0:T(8,128)(2,1)} %get-tuple-element.62.own_ref), channel_id=1, source_target_pairs={{0,4},{4,0},{8,12},{12,8},{16,20},{20,16},{24,28},{28,24},{1,5},{5... | collective-permute-start | bytes 3145736 | tf_op jit(solution)/shard_map/ppermute | solution.py:750
  345.0 20.3 %shard_map.342 = (bf16[512,1024]{1,0:T(8,128)(2,1)}, f32[16,1,512]{2,1,0:T(1,128)}) custom-call(s32[4]{0:T(128)} %pad_add_fusion.2.ids_ref, bf16[512,1024]{1,0:T(8,128)(2,1)} %get-tuple-element.61.q_ref, bf16[512,1024]{1,0:T(8,128)(2,1)} %get-tuple-element.62.own_ref, bf16[512,1024]{1,0:T(8,128)(2,1)} %collective-permute-done.5.oth_ref, ...), custom_call_target="tpu_custom_call" | custom-call | tf_op jit(solution)/shard_map/pallas_call | solution.py:432
  365.2 9.9 %shard_map.343 = (f32[512,1024]{1,0:T(8,128)}, bf16[512,1024]{1,0:T(8,128)(2,1)}, bf16[512,1024]{1,0:T(8,128)(2,1)}) custom-call(bf16[512,1024]{1,0:T(8,128)(2,1)} %constant_dynamic-update-slice_fusion.2.x_ref, bf16[512,1024]{1,0:T(8,128)(2,1)} %get-tuple-element.63.att_ref, f32[1,1024]{1,0:T(1,128)} %copy-done.28, ...), custom_call_target="tpu_custom_call" | custom-call | tf_op jit(solution)/shard_map/pallas_call | solution.py:165
  375.9 16.0 %shard_map.345 = (bf16[512,1024]{1,0:T(8,128)(2,1)}, f32[16,1,512]{2,1,0:T(1,128)}) custom-call(bf16[512,1024]{1,0:T(8,128)(2,1)} %get-tuple-element.65.q_ref, bf16[256,1024]{1,0:T(8,128)(2,1)} %shard_map.344.own_ref, bf16[256,1024]{1,0:T(8,128)(2,1)} %copy-done.17, s32[512,1]{1,0:T(8,128)} %copy.183.kseg_ref, s32[2,1,256]{2,1,0:T(1,128)} %reshape.170.qseg_ref), custom_call_target="tpu_custom_call" | custom-call | tf_op jit(solution)/shard_map/pallas_call | solution.py:453
  391.8 6.7 shard_map.346
  404.9 21.9 %shard_map.347 = (f32[512,1024]{1,0:T(8,128)}, f32[512,1024]{1,0:T(8,128)}, bf16[4,2,128,2112]{3,2,1,0:T(8,128)(2,1)}, bf16[4,2,128,2112]{3,2,1,0:T(8,128)(2,1)}) custom-call(bf16[512,1024]{1,0:T(8,128)(2,1)} %get-tuple-element.68.n_ref, bf16[512,1024]{1,0:T(8,128)(2,1)} %constant_dynamic-update-slice_fusion.60.r_ref.cot_ref, ...), custom_call_target="tpu_custom_call" | custom-call | tf_op jit(solution)/shard_map/pallas_call | solution.py:259
  433.3 21.6 %shard_map.348 = (f32[512,1024]{1,0:T(8,128)}, f32[512,1024]{1,0:T(8,128)}, bf16[4,2,128,2112]{3,2,1,0:T(8,128)(2,1)}, bf16[4,2,128,2112]{3,2,1,0:T(8,128)(2,1)}) custom-call(bf16[512,1024]{1,0:T(8,128)(2,1)} %get-tuple-element.68.n_ref, bf16[512,1024]{1,0:T(8,128)(2,1)} %constant_dynamic-update-slice_fusion.60.r_ref.cot_ref, ...), custom_call_target="tpu_custom_call" | custom-call | tf_op jit(solution)/shard_map/pallas_call | solution.py:259
  454.9 10.2 %shard_map.349 = (bf16[512,1024]{1,0:T(8,128)(2,1)}, f32[512,1024]{1,0:T(8,128)}, bf16[512,1024]{1,0:T(8,128)(2,1)}, f32[1,1024]{1,0:T(1,128)}, bf16[512,1024]{1,0:T(8,128)(2,1)}) custom-call(f32[512,1024]{1,0:T(8,128)} %get-tuple-element.67.s_ref, f32[512,1024]{1,0:T(8,128)} %get-tuple-element.69.ya_ref, f32[512,1024]{1,0:T(8,128)} %get-tuple-element.70.yb_ref, ...), custom_call_target="tpu_custom_call" | custom-call | tf_op jit(solution)/shard_map/pallas_call | solution.py:299
  465.1 21.5 %shard_map.350 = (bf16[512,1024]{1,0:T(8,128)(2,1)}, f32[256,1024]{1,0:T(8,128)}, bf16[256,1024]{1,0:T(8,128)(2,1)}) custom-call(bf16[512,1024]{1,0:T(8,128)(2,1)} %get-tuple-element.65.q_ref, bf16[512,1024]{1,0:T(8,128)(2,1)} %get-tuple-element.74.ga_ref, f32[16,1,512]{2,1,0:T(1,128)} %get-tuple-element.75.lse_ref, bf16[256,1024]{1,0:T(8,128)(2,1)} %shard_map.344.own_ref, ...), custom_call_target="tpu_custom_call" | custom-call | tf_op jit(solution)/shard_map/pallas_call | solution.py:588
  494.8 18.2 %shard_map.351 = (bf16[4,4,128,768]{3,2,1,0:T(8,128)(2,1)}, bf16[4,4,128,768]{3,2,1,0:T(8,128)(2,1)}, f32[512,1024]{1,0:T(8,128)}, bf16[512,1024]{1,0:T(8,128)(2...) custom-call(bf16[512,1024]{1,0:T(8,128)(2,1)} %get-tuple-element.76.dq_ref, ...), custom_call_target="tpu_custom_call" | custom-call | tf_op jit(solution)/shard_map/pallas_call | solution.py:662
  520.0 31.8 %shard_map.352 = (bf16[512,1024]{1,0:T(8,128)(2,1)}, f32[512,1024]{1,0:T(8,128)}, bf16[512,1024]{1,0:T(8,128)(2,1)}, f32[16,8,1152]{2,1,0:T(8,128)}) custom-call(s32[4]{0:T(128)} %pad_add_fusion.2.ids_ref, bf16[512,1024]{1,0:T(8,128)(2,1)} %get-tuple-element.61.q_ref, bf16[512,1024]{1,0:T(8,128)(2,1)} %get-tuple-element.82.ga_ref, ...), custom_call_target="tpu_custom_call" | custom-call | tf_op jit(solution)/shard_map/pallas_call | solution.py:539
  555.7 14.5 %shard_map.353 = (bf16[4,4,128,768]{3,2,1,0:T(8,128)(2,1)}, bf16[4,4,128,768]{3,2,1,0:T(8,128)(2,1)}, bf16[512,1024]{1,0:T(8,128)(2,1)}, f32[1,1024]{1,0:T(1,128)}) custom-call(bf16[512,1024]{1,0:T(8,128)(2,1)} %get-tuple-element.84.dq_ref, f32[512,1024]{1,0:T(8,128)} %get-tuple-element.85.dko_ref, bf16[512,1024]{1,0:T(8,128)(2,1)} %copy-done.19, ...), custom_call_target="tpu_custom_call" | custom-call | tf_op jit(solution)/shard_map/pallas_call | solution.py:730
  583.7 8.0 convert_add_fusion.1
  620.2 6.5 convert_add_fusion
  637.9 28.3 %collective-permute-done.34 = bf16[1,1,4,128,768]{4,3,2,1,0:T(8,128)(2,1)} collective-permute-done((bf16[1,1,4,128,768]{4,3,2,1,0:T(8,128)(2,1)}, bf16[1,1,4,128,768]{4,3,2,1,0:T(8,128)(2,1)}, u32[]{:S(2)}, u32[]{:S(2)}) %collective-permute-start.34) | collective-permute-done | bytes 786464 | tf_op jit(solution)/shard_map/ppermute | solution.py:750
  684.0 28.5 %collective-permute-done.39 = bf16[2,1,2,128,2112]{3,4,2,1,0:T(8,128)(2,1)} collective-permute-done((bf16[2,1,2,128,2112]{3,4,2,1,0:T(8,128)(2,1)}, bf16[2,1,2,128,2112]{3,4,2,1,0:T(8,128)(2,1)}, u32[]{:S(2)}, u32[]{:S(2)}) %collective-permute-start.39) | collective-permute-done | bytes 2162720 | tf_op jit(solution)/shard_map/ppermute | solution.py:750
  726.5 8.0 collective-permute-done.37
  738.0 9.7 %collective-permute-done.40 = bf16[1,1,2,128,2112]{3,4,2,1,0:T(8,128)(2,1)} collective-permute-done((bf16[1,1,2,128,2112]{3,4,2,1,0:T(8,128)(2,1)}, bf16[1,1,2,128,2112]{3,4,2,1,0:T(8,128)(2,1)}, u32[]{:S(2)}, u32[]{:S(2)}) %collective-permute-start.40) | collective-permute-done | bytes 1081376 | tf_op jit(solution)/shard_map/ppermute | solution.py:750
  757.4 7.4 collective-permute-start.22
  764.9 56.8 %reduce-scatter.8.cloned.1.call-done = bf16[1,128,2112]{2,1,0:T(8,128)(2,1)} async-done(((bf16[4,128,2112]{2,1,0:T(8,128)(2,1)}), bf16[1,128,2112]{2,1,0:T(8,128)(2,1)}) %reduce-scatter.8.cloned.1.call-update) | async-done | bytes 540688 | tf_op jit(solution)/shard_map/reduce_scatter | solution.py:943
  828.3 10.4 %collective-permute-done.28 = bf16[128,1024]{1,0:T(8,128)(2,1)} collective-permute-done((bf16[128,1024]{1,0:T(8,128)(2,1)S(1)}, bf16[128,1024]{1,0:T(8,128)(2,1)}, u32[]{:S(2)}, u32[]{:S(2)}) %collective-permute-start.28) | collective-permute-done | bytes 262176 | tf_op jit(solution)/shard_map/ppermute | solution.py:802
  846.4 43.0 %psum.7 = f32[3584]{0:T(1024)S(1)} all-reduce(f32[3584]{0:T(1024)S(1)} %pad_maximum_fusion.10), channel_id=1, replica_groups=mesh['batch'=8,'group'=4] {'batch','group'}, use_global_device_ids=true, to_apply=%region_0.1 | all-reduce | flops 3584 | bytes 28672 | tf_op jit(solution)/shard_map/psum | solution.py:956
  905.4 10.9 %all-gather.18.cloned.1.call-done = bf16[1,1024,2112]{2,1,0:T(8,128)(2,1)} async-done(((bf16[1,128,2112]{2,1,0:T(8,128)(2,1)}), bf16[1,1024,2112]{2,1,0:T(8,128)(2,1)}) %all-gather.18.cloned.1.call-update) | async-done | bytes 4325392 | tf_op jit(solution)/shard_map/all_gather | solution.py:944
  (416 shorter events, 318.9 us)
Async XLA Ops:
  7.2 94.9 %all-gather.12.cloned.1.call-start = ((), (), s32[]{:S(2)}) async-start(), calls=%async_computation.6 | async-start | bytes 2703360 | tf_op jit(solution)/shard_map/all_gather | solution.py:855
  10.5 742.3 %reduce-scatter.6.cloned.1.call-start = ((), (), s32[]{:S(2)}) async-start(), calls=%async_computation.4 | async-start | bytes 983040 | tf_op jit(solution)/shard_map/reduce_scatter | solution.py:943
  11.4 247.2 %collective-permute-start.10 = (bf16[128,1024]{1,0:T(8,128)(2,1)}, bf16[128,1024]{1,0:T(8,128)(2,1)}, u32[]{:S(2)}, u32[]{:S(2)}) collective-permute-start(bf16[128,1024]{1,0:T(8,128)(2,1)} %get-tuple-element.220), channel_id=1, source_target_pairs={{0,0},{1,4},{2,6},{3,2},{4,1},{5,5},{6,7},{7,3},{8,8},{9,12},{10,1... | collective-permute-start | bytes 786440 | tf_op jit(solution)/shard_map/ppermute | solution.py:795
  52.7 117.9 %collective-permute-start.7 = (bf16[1,1,4,128,768]{4,3,2,1,0:T(8,128)(2,1)}, bf16[1,1,4,128,768]{4,3,2,1,0:T(8,128)(2,1)}, u32[]{:S(2)}, u32[]{:S(2)}) collective-permute-start(bf16[1,1,4,128,768]{4,3,2,1,0:T(8,128)(2,1)} %bitcast.89), channel_id=1, source_target_pairs={{0,16},{4,20},{8,24},{12,28},{16,0},{20,4},{24,8},{28,12},{1,17},{... | collective-permute-start | bytes 2359304 | tf_op jit(solution)/shard_map/ppermute | solution.py:750
  87.9 61.5 %collective-permute-start.2 = (bf16[1,1,4,128,768]{4,3,2,1,0:T(8,128)(2,1)}, bf16[1,1,4,128,768]{4,3,2,1,0:T(8,128)(2,1)}, u32[]{:S(2)}, u32[]{:S(2)}) collective-permute-start(bf16[1,1,4,128,768]{4,3,2,1,0:T(8,128)(2,1)} %bitcast.87), channel_id=1, source_target_pairs={{0,8},{4,12},{8,0},{12,4},{16,24},{20,28},{24,16},{28,20},{1,9},{5... | collective-permute-start | bytes 2359304 | tf_op jit(solution)/shard_map/ppermute | solution.py:750
  138.2 87.5 %collective-permute-start.16 = (bf16[1,2,2,128,2112]{3,4,2,1,0:T(8,128)(2,1)}, bf16[1,2,2,128,2112]{3,4,2,1,0:T(8,128)(2,1)}, u32[]{:S(2)}, u32[]{:S(2)}) collective-permute-start(bf16[1,2,2,128,2112]{3,4,2,1,0:T(8,128)(2,1)} %copy.187), channel_id=1, source_target_pairs={{0,16},{4,20},{8,24},{12,28},{16,0},{20,4},{24,8},{28,12},{1,17},{... | collective-permute-start | bytes 6488072 | tf_op jit(solution)/shard_map/ppermute | solution.py:750
  148.7 86.4 %collective-permute-start.19 = (bf16[2,1,2,128,2112]{3,4,2,1,0:T(8,128)(2,1)}, bf16[2,1,2,128,2112]{3,4,2,1,0:T(8,128)(2,1)}, u32[]{:S(2)}, u32[]{:S(2)}) collective-permute-start(bf16[2,1,2,128,2112]{3,4,2,1,0:T(8,128)(2,1)} %copy.194), channel_id=1, source_target_pairs={{0,8},{4,12},{8,0},{12,4},{16,24},{20,28},{24,16},{28,20},{1,9},{5... | collective-permute-start | bytes 6488072 | tf_op jit(solution)/shard_map/ppermute | solution.py:750
  152.0 67.3 %collective-permute-start.3 = (bf16[1,2,4,128,768]{4,3,2,1,0:T(8,128)(2,1)}, bf16[1,2,4,128,768]{4,3,2,1,0:T(8,128)(2,1)}, u32[]{:S(2)}, u32[]{:S(2)}) collective-permute-start(bf16[1,2,4,128,768]{4,3,2,1,0:T(8,128)(2,1)} %pad_maximum_fusion.7), channel_id=1, source_target_pairs={{0,16},{4,20},{8,24},{12,28},{16,0},{20,4},{24,8},{28,12},{1,17},{... | collective-permute-start | bytes 4718600 | tf_op jit(solution)/shard_map/ppermute | solution.py:750
  170.6 88.1 %collective-permute-start.11 = (bf16[128,1024]{1,0:T(8,128)(2,1)}, bf16[128,1024]{1,0:T(8,128)(2,1)}, u32[]{:S(2)}, u32[]{:S(2)}) collective-permute-start(bf16[128,1024]{1,0:T(8,128)(2,1)} %get-tuple-element.219), channel_id=1, source_target_pairs={{0,2},{1,6},{2,4},{3,0},{4,3},{5,7},{6,5},{7,1},{8,10},{9,14},{10,... | collective-permute-start | bytes 786440 | tf_op jit(solution)/shard_map/ppermute | solution.py:795
  219.4 39.8 %collective-permute-start.8 = (bf16[2,1,4,128,768]{4,3,2,1,0:T(8,128)(2,1)}, bf16[2,1,4,128,768]{4,3,2,1,0:T(8,128)(2,1)}, u32[]{:S(2)}, u32[]{:S(2)}) collective-permute-start(bf16[2,1,4,128,768]{4,3,2,1,0:T(8,128)(2,1)} %pad_maximum_fusion.8), channel_id=1, source_target_pairs={{0,8},{4,12},{8,0},{12,4},{16,24},{20,28},{24,16},{28,20},{1,9},{5... | collective-permute-start | bytes 4718600 | tf_op jit(solution)/shard_map/ppermute | solution.py:750
  258.1 54.6 %collective-permute-start.4 = (bf16[4,4,128,768]{3,2,1,0:T(8,128)(2,1)}, bf16[4,4,128,768]{3,2,1,0:T(8,128)(2,1)}, u32[]{:S(2)}, u32[]{:S(2)}) collective-permute-start(bf16[4,4,128,768]{3,2,1,0:T(8,128)(2,1)} %bitcast.15.own_ref.wo_own), channel_id=1, source_target_pairs={{0,4},{4,0},{8,12},{12,8},{16,20},{20,16},{24,28},{28,24},{1,5},{5... | collective-permute-start | bytes 9437192 | tf_op jit(solution)/shard_map/ppermute | solution.py:750
  258.6 139.9 %collective-permute-start.17 = (bf16[4,2,128,2112]{2,3,1,0:T(8,128)(2,1)}, bf16[4,2,128,2112]{2,3,1,0:T(8,128)(2,1)}, u32[]{:S(2)}, u32[]{:S(2)}) collective-permute-start(bf16[4,2,128,2112]{2,3,1,0:T(8,128)(2,1)} %copy.189), channel_id=1, source_target_pairs={{0,4},{4,0},{8,12},{12,8},{16,20},{20,16},{24,28},{28,24},{1,5},{5... | collective-permute-start | bytes 12976136 | tf_op jit(solution)/shard_map/ppermute | solution.py:750
  258.7 168.2 %collective-permute-start.20 = (bf16[4,2,128,2112]{2,3,1,0:T(8,128)(2,1)}, bf16[4,2,128,2112]{2,3,1,0:T(8,128)(2,1)}, u32[]{:S(2)}, u32[]{:S(2)}) collective-permute-start(bf16[4,2,128,2112]{2,3,1,0:T(8,128)(2,1)} %copy.196), channel_id=1, source_target_pairs={{0,4},{4,0},{8,12},{12,8},{16,20},{20,16},{24,28},{28,24},{1,5},{5... | collective-permute-start | bytes 12976136 | tf_op jit(solution)/shard_map/ppermute | solution.py:750
  261.4 75.7 %collective-permute-start.9 = (bf16[4,4,128,768]{3,2,1,0:T(8,128)(2,1)S(1)}, bf16[4,4,128,768]{3,2,1,0:T(8,128)(2,1)}, u32[]{:S(2)}, u32[]{:S(2)}) collective-permute-start(bf16[4,4,128,768]{3,2,1,0:T(8,128)(2,1)S(1)} %bitcast.151), channel_id=1, source_target_pairs={{0,4},{4,0},{8,12},{12,8},{16,20},{20,16},{24,28},{28,24},{1,5},{5... | collective-permute-start | bytes 9437192 | tf_op jit(solution)/shard_map/ppermute | solution.py:750
  494.0 83.3 %collective-permute-start.35 = (bf16[4,2,128,2112]{2,3,1,0:T(8,128)(2,1)}, bf16[4,2,128,2112]{2,3,1,0:T(8,128)(2,1)}, u32[]{:S(2)}, u32[]{:S(2)}) collective-permute-start(bf16[4,2,128,2112]{2,3,1,0:T(8,128)(2,1)} %copy.204), channel_id=1, source_target_pairs={{0,4},{4,0},{8,12},{12,8},{16,20},{20,16},{24,28},{28,24},{1,5},{5... | collective-permute-start | bytes 12976136 | tf_op jit(solution)/shard_map/ppermute | solution.py:750
  513.0 57.4 %collective-permute-start.32 = (bf16[4,4,128,768]{3,2,1,0:T(8,128)(2,1)}, bf16[4,4,128,768]{3,2,1,0:T(8,128)(2,1)}, u32[]{:S(2)}, u32[]{:S(2)}) collective-permute-start(bf16[4,4,128,768]{3,2,1,0:T(8,128)(2,1)} %get-tuple-element.99), channel_id=1, source_target_pairs={{0,4},{4,0},{8,12},{12,8},{16,20},{20,16},{24,28},{28,24},{1,5},{5... | collective-permute-start | bytes 9437192 | tf_op jit(solution)/shard_map/ppermute | solution.py:750
  520.0 78.4 %collective-permute-start.38 = (bf16[4,2,128,2112]{2,3,1,0:T(8,128)(2,1)}, bf16[4,2,128,2112]{2,3,1,0:T(8,128)(2,1)}, u32[]{:S(2)}, u32[]{:S(2)}) collective-permute-start(bf16[4,2,128,2112]{2,3,1,0:T(8,128)(2,1)} %copy.210), channel_id=1, source_target_pairs={{0,4},{4,0},{8,12},{12,8},{16,20},{20,16},{24,28},{28,24},{1,5},{5... | collective-permute-start | bytes 12976136 | tf_op jit(solution)/shard_map/ppermute | solution.py:750
  596.6 77.1 %collective-permute-start.36 = (bf16[1,2,2,128,2112]{3,4,2,1,0:T(8,128)(2,1)}, bf16[1,2,2,128,2112]{3,4,2,1,0:T(8,128)(2,1)}, u32[]{:S(2)}, u32[]{:S(2)}) collective-permute-start(bf16[1,2,2,128,2112]{3,4,2,1,0:T(8,128)(2,1)} %copy.206), channel_id=1, source_target_pairs={{0,16},{4,20},{8,24},{12,28},{16,0},{20,4},{24,8},{28,12},{1,17},{... | collective-permute-start | bytes 6488072 | tf_op jit(solution)/shard_map/ppermute | solution.py:750
  611.7 57.2 %collective-permute-start.30 = (bf16[2,1,4,128,768]{3,4,2,1,0:T(8,128)(2,1)}, bf16[2,1,4,128,768]{3,4,2,1,0:T(8,128)(2,1)}, u32[]{:S(2)}, u32[]{:S(2)}) collective-permute-start(bf16[2,1,4,128,768]{3,4,2,1,0:T(8,128)(2,1)} %copy.245), channel_id=1, source_target_pairs={{0,8},{4,12},{8,0},{12,4},{16,24},{20,28},{24,16},{28,20},{1,9},{5... | collective-permute-start | bytes 4718600 | tf_op jit(solution)/shard_map/ppermute | solution.py:750
  619.8 46.3 %collective-permute-start.34 = (bf16[1,1,4,128,768]{4,3,2,1,0:T(8,128)(2,1)}, bf16[1,1,4,128,768]{4,3,2,1,0:T(8,128)(2,1)}, u32[]{:S(2)}, u32[]{:S(2)}) collective-permute-start(bf16[1,1,4,128,768]{4,3,2,1,0:T(8,128)(2,1)} %slice.389), channel_id=1, source_target_pairs={{0,8},{4,12},{8,0},{12,4},{16,24},{20,28},{24,16},{28,20},{1,9},{5... | collective-permute-start | bytes 2359304 | tf_op jit(solution)/shard_map/ppermute | solution.py:750
  631.7 80.9 %collective-permute-start.39 = (bf16[2,1,2,128,2112]{3,4,2,1,0:T(8,128)(2,1)}, bf16[2,1,2,128,2112]{3,4,2,1,0:T(8,128)(2,1)}, u32[]{:S(2)}, u32[]{:S(2)}) collective-permute-start(bf16[2,1,2,128,2112]{3,4,2,1,0:T(8,128)(2,1)} %copy.212), channel_id=1, source_target_pairs={{0,8},{4,12},{8,0},{12,4},{16,24},{20,28},{24,16},{28,20},{1,9},{5... | collective-permute-start | bytes 6488072 | tf_op jit(solution)/shard_map/ppermute | solution.py:750
  668.9 84.8 %reduce-scatter.4.cloned.1.call-start = ((), (), s32[]{:S(2)}) async-start(), calls=%async_computation.3 | async-start | bytes 983040 | tf_op jit(solution)/shard_map/reduce_scatter | solution.py:943
  673.3 51.0 %collective-permute-start.31 = (bf16[1,1,4,128,768]{3,4,2,1,0:T(8,128)(2,1)}, bf16[1,1,4,128,768]{3,4,2,1,0:T(8,128)(2,1)}, u32[]{:S(2)}, u32[]{:S(2)}) collective-permute-start(bf16[1,1,4,128,768]{3,4,2,1,0:T(8,128)(2,1)} %slice.390), channel_id=1, source_target_pairs={{0,16},{4,20},{8,24},{12,28},{16,0},{20,4},{24,8},{28,12},{1,17},{... | collective-permute-start | bytes 2359304 | tf_op jit(solution)/shard_map/ppermute | solution.py:750
  683.3 51.2 %collective-permute-start.37 = (bf16[1,1,2,128,2112]{3,4,2,1,0:T(8,128)(2,1)}, bf16[1,1,2,128,2112]{3,4,2,1,0:T(8,128)(2,1)}, u32[]{:S(2)}, u32[]{:S(2)}) collective-permute-start(bf16[1,1,2,128,2112]{3,4,2,1,0:T(8,128)(2,1)} %copy.208), channel_id=1, source_target_pairs={{0,8},{4,12},{8,0},{12,4},{16,24},{20,28},{24,16},{28,20},{1,9},{5... | collective-permute-start | bytes 3244040 | tf_op jit(solution)/shard_map/ppermute | solution.py:750
  726.5 95.3 %reduce-scatter.8.cloned.1.call-start = ((), (), s32[]{:S(2)}) async-start(), calls=%async_computation.5 | async-start | bytes 2785280 | tf_op jit(solution)/shard_map/reduce_scatter | solution.py:943
  752.8 139.5 %all-gather.16.cloned.1.call-start = ((), (), s32[]{:S(2)}) async-start(), calls=%async_computation.8 | async-start | bytes 1769472 | tf_op jit(solution)/shard_map/all_gather | solution.py:944
  753.4 145.6 %all-gather.14.cloned.1.call-start = ((), (), s32[]{:S(2)}) async-start(), calls=%async_computation.7 | async-start | bytes 1769472 | tf_op jit(solution)/shard_map/all_gather | solution.py:944
  754.0 162.3 %all-gather.18.cloned.1.call-start = ((), (), s32[]{:S(2)}) async-start(), calls=%async_computation.9 | async-start | bytes 5013504 | tf_op jit(solution)/shard_map/all_gather | solution.py:944
  755.7 71.5 %collective-permute-start.21 = (bf16[256,1024]{1,0:T(8,128)(2,1)}, bf16[256,1024]{1,0:T(8,128)(2,1)S(1)}, u32[]{:S(2)}, u32[]{:S(2)}) collective-permute-start(bf16[256,1024]{1,0:T(8,128)(2,1)} %get-tuple-element.211), channel_id=1, source_target_pairs={{0,0},{4,1},{6,2},{2,3},{1,4},{5,5},{7,6},{3,7},{8,8},{12,9},{14,1... | collective-permute-start | bytes 1572872 | tf_op jit(solution)/shard_map/ppermute | solution.py:802
  757.4 69.8 %collective-permute-start.22 = (bf16[256,1024]{1,0:T(8,128)(2,1)}, bf16[256,1024]{1,0:T(8,128)(2,1)S(1)}, u32[]{:S(2)}, u32[]{:S(2)}) collective-permute-start(bf16[256,1024]{1,0:T(8,128)(2,1)} %get-tuple-element.212), channel_id=1, source_target_pairs={{2,0},{6,1},{4,2},{0,3},{3,4},{7,5},{5,6},{1,7},{10,8},{14,9},{12,... | collective-permute-start | bytes 1572872 | tf_op jit(solution)/shard_map/ppermute | solution.py:802
  841.4 49.4 %collective-permute-start.25 = (bf16[256,1024]{1,0:T(8,128)(2,1)S(1)}, bf16[256,1024]{1,0:T(8,128)(2,1)S(1)}, u32[]{:S(2)}, u32[]{:S(2)}) collective-permute-start(bf16[256,1024]{1,0:T(8,128)(2,1)S(1)} %get-tuple-element.209), channel_id=1, source_target_pairs={{0,0},{4,1},{6,2},{2,3},{1,4},{5,5},{7,6},{3,7},{8,8},{12,9},{14,1... | collective-permute-start | bytes 1572872 | tf_op jit(solution)/shard_map/ppermute | solution.py:802
  842.1 48.7 %collective-permute-start.26 = (bf16[256,1024]{1,0:T(8,128)(2,1)S(1)}, bf16[256,1024]{1,0:T(8,128)(2,1)S(1)}, u32[]{:S(2)}, u32[]{:S(2)}) collective-permute-start(bf16[256,1024]{1,0:T(8,128)(2,1)S(1)} %get-tuple-element.210), channel_id=1, source_target_pairs={{2,0},{6,1},{4,2},{0,3},{3,4},{7,5},{5,6},{1,7},{10,8},{14,9},{12,... | collective-permute-start | bytes 1572872 | tf_op jit(solution)/shard_map/ppermute | solution.py:802
  (58 other events, 987.2 us)
Sparse Core Ops, SparseCore 0:
  10.6 68.1 all-gather.11
  669.0 26.3 reduce-scatter.5
  726.6 27.0 reduce-scatter.3
  756.5 65.2 reduce-scatter.7
  823.5 25.5 all-gather.15
  850.8 25.7 all-gather.13
  878.5 37.7 all-gather.17

commit v2 on v1

--- a/solution.py
+++ b/solution.py
@@ -14,6 +14,8 @@
 HIGHEST = lax.Precision.HIGHEST
 BF16 = jnp.bfloat16
 F32 = jnp.float32
+FLOPS_PER_MICRO = 1_000_000_000
+BYTES_PER_MICRO = 3_000_000
 
 
 def dot_nn(left, right):
@@ -28,10 +30,13 @@
     return lax.dot_general(left, right, (((0,), (0,)), ((), ())), preferred_element_type=F32)
 
 
-def call(kernel, outs, grid, in_specs, out_specs, scratch=(), prefetch=0):
+def call(kernel, outs, grid, in_specs, out_specs, scratch=(), prefetch=0, micros=5):
     return pl.pallas_call(
         kernel,
         out_shape=outs,
+        cost_estimate=pl.CostEstimate(
+            flops=micros * FLOPS_PER_MICRO, transcendentals=0, bytes_accessed=micros * BYTES_PER_MICRO
+        ),
         grid_spec=pltpu.PrefetchScalarGridSpec(
             num_scalar_prefetch=prefetch,
             grid=grid,
@@ -109,6 +114,7 @@
         (shards,),
         [whole(x), whole(gain), spec, spec],
         (fixed(rows, width), out, out),
+        micros=7,
     )(x, gain, own, oth)
 
 
@@ -128,6 +134,7 @@
         (shards,),
         [whole(x), spec, spec],
         pl.BlockSpec((rows, qcols), lambda z: (0, z)),
+        micros=4,
     )(x, own, oth)
 
 
@@ -180,6 +187,7 @@
             fixed(rows, width),
             pl.BlockSpec((rows, qcols), lambda i: (0, second(i))),
         ),
+        micros=10,
     )(x, att, gain, own, oth, next_own, next_oth)
 
 
@@ -209,12 +217,12 @@
         (shards,),
         [whole(x), pl.BlockSpec((rows, qcols), lambda z: (0, z)), whole(gain), wo, wo],
         (fixed(rows, width), fixed(rows, width)),
+        micros=7,
     )(x, att, gain, own, oth)
 
 
-def ffn_kernel(n_ref, r_ref, own_ref, oth_ref, y_ref, dn_ref, gown_ref, goth_ref, nt_ref, rt_ref):
+def ffn_kernel(ff, n_ref, r_ref, own_ref, oth_ref, y_ref, dn_ref, gown_ref, goth_ref, nt_ref, rt_ref):
     half = n_ref.shape[1] // 2
-    ff = own_ref.shape[3] // 3
 
     @pl.when(pl.program_id(0) == 0)
     def _():
@@ -225,7 +233,7 @@
 
     own, oth = rows_of(own_ref), rows_of(oth_ref)
     up_own, up_oth = own[:, : 2 * ff], oth[:, : 2 * ff]
-    down_own, down_oth = own[:, 2 * ff :], oth[:, 2 * ff :]
+    down_own, down_oth = own[:, 2 * ff : 3 * ff], oth[:, 2 * ff : 3 * ff]
     both = dot_nn(n_ref[:, :half], up_own) + dot_nn(n_ref[:, half:], up_oth)
     gate, upval = both[:, :ff], both[:, ff:]
     grad_hidden = dot_nn(r_ref[:, :half], down_own) + dot_nn(r_ref[:, half:], down_oth)
@@ -244,20 +252,23 @@
     y_ref[:, half:] += dot_nt(hidden, down_oth)
     dn_ref[:, :half] += dot_nt(grad_both, up_own)
     dn_ref[:, half:] += dot_nt(grad_both, up_oth)
-    cols, _, blk, _ = gown_ref.shape
+    cols, _, blk, packed = gown_ref.shape
     for ref, first in ((gown_ref, 0), (goth_ref, half)):
         grad = dot_nn(nt_ref[first : first + half, :], grad_both).astype(BF16)
         ref[:, 0, :, : 2 * ff] = grad.reshape(cols, blk, 2 * ff)
         grad = dot_nn(rt_ref[first : first + half, :], hidden).astype(BF16)
-        ref[:, 0, :, 2 * ff :] = grad.reshape(cols, blk, ff)
-
-
-def feed_forward(n, r, own, oth):
+        ref[:, 0, :, 2 * ff : 3 * ff] = grad.reshape(cols, blk, ff)
+        spare = packed - 3 * ff
+        if spare:
+            ref[:, 0, :, 3 * ff :] = jnp.zeros((cols, blk, spare), BF16)
+
+
+def feed_forward(n, r, own, oth, ff):
     rows, width = n.shape
     cols, shards, blk, packed = own.shape
     spec = weight_spec(own, packed, lambda z: (0, z, 0, 0))
     return call(
-        ffn_kernel,
+        functools.partial(ffn_kernel, ff),
         (
             shape(rows, width, dtype=F32),
             shape(rows, width, dtype=F32),
@@ -268,6 +279,7 @@
         [whole(n), whole(r), spec, spec],
         (fixed(rows, width), fixed(rows, width), spec, spec),
         [pltpu.VMEM((width, rows), BF16), pltpu.VMEM((width, rows), BF16)],
+        micros=22,
     )(n, r, own, oth)
 
 
@@ -308,6 +320,7 @@
         (shards,),
         [full] * 6 + [whole(gain), wo, wo],
         (full, full, full, fixed(1, width), pl.BlockSpec((rows, qcols), lambda z: (0, z))),
+        micros=10,
     )(s, ya, yb, da, db, cot, gain, own, oth)
 
 
@@ -329,6 +342,7 @@
         (heads,),
         [pl.BlockSpec((1, 1, width), lambda h: (h, 0, 0))],
         pl.BlockSpec((1, 128, width), lambda h: (h, 0, 0)),
+        micros=11,
     )(base)
 
 
@@ -436,7 +450,8 @@
         [block, group_spec(own), group_spec(oth), slab, whole(kseg), qs],
         (block, lse),
         [pltpu.VMEM((4, rows, PAIR), BF16)],
-        1,
+        prefetch=1,
+        micros=20,
     )(ids, q, own, oth, slabs, kseg, qseg)
 
 
@@ -456,6 +471,7 @@
         (groups, 2),
         [block, group_spec(own), group_spec(oth), whole(kseg), qs],
         (block, lse),
+        micros=16,
     )(q, own, oth, kseg, qseg)
 
 
@@ -557,7 +573,8 @@
             pltpu.VMEM((4, rows, PAIR), F32),
             pltpu.VMEM((2, 128, width), F32),
         ],
-        1,
+        prefetch=1,
+        micros=32,
     )(ids, q, ga, lses, own, oth, slabs, kseg, qseg)
 
 
@@ -592,6 +609,7 @@
         [block, block, lse, group_spec(own), group_spec(oth), whole(kseg), qs],
         (block, group_spec(own), group_spec(own)),
         [pltpu.VMEM((2 * own.shape[0], PAIR), F32)],
+        micros=21,
     )(q, ga, lses, own, oth, kseg, qseg)
 
 
@@ -605,8 +623,8 @@
 
 def cross_post_kernel(
     shards, dq_ref, dko_ref, dkr_ref, n_ref, mem_ref, r_ref, att_ref, s_ref, cot_ref, gain_ref,
-    own_ref, oth_ref, wo_own, wo_oth,
-    gown_ref, goth_ref, new_ref, round_ref, gg_ref, dmem_ref, ga_ref,
+    own_ref, oth_ref, wo_own, wo_oth, att_one_ref,
+    gown_ref, goth_ref, oown_ref, ooth_ref, new_ref, round_ref, gg_ref, dmem_ref, ga_ref,
     dn_ref, dmo_ref, nt_ref, mt_ref, rt_ref,
 ):
     step = pl.program_id(0)
@@ -640,15 +658,19 @@
         new = cot_ref[...] + dv
         new_ref[...] = new
         round_ref[...] = new.astype(BF16)
+        rt_ref[...] = new.astype(BF16).T
 
     @pl.when(step >= shards)
     def _():
         r = round_ref[...]
+        weight_grads(half, ((rt_ref, att_one_ref[...], 0),), oown_ref, ooth_ref)
         out = dot_nn(r[:, :half], rows_of(wo_own)) + dot_nn(r[:, half:], rows_of(wo_oth))
         ga_ref[...] = out.astype(BF16)
 
 
-def cross_post(dq, dko, dkr, n, mem, r, att, s, cot, gain, own, oth, next_own, next_oth, qcols):
+def cross_post(
+    dq, dko, dkr, n, mem, r, att, s, cot, gain, own, oth, next_own, next_oth, next_att, qcols
+):
     rows, width = n.shape
     cols, shards, blk, packed = own.shape
     first = lambda i: jnp.minimum(i, shards - 1)
@@ -664,6 +686,8 @@
         (
             shape(*own.shape),
             shape(*own.shape),
+            shape(cols, shards, blk, qcols),
+            shape(cols, shards, blk, qcols),
             shape(rows, width, dtype=F32),
             shape(rows, width),
             shape(1, width, dtype=F32),
@@ -672,10 +696,12 @@
         ),
         (2 * shards,),
         [by_shard, enc_by_shard, enc_by_shard, full, whole(mem), full, by_shard, full, full]
-        + [whole(gain), spec, spec, wo, wo],
+        + [whole(gain), spec, spec, wo, wo, pl.BlockSpec((rows, qcols), lambda i: (0, second(i)))],
         (
             spec,
             spec,
+            weight_spec(own, qcols, lambda i: (0, second(i), 0, 0)),
+            weight_spec(own, qcols, lambda i: (0, second(i), 0, 0)),
             full,
             full,
             fixed(1, width),
@@ -689,12 +715,13 @@
             pltpu.VMEM((width, enc_rows), BF16),
             pltpu.VMEM((width, rows), BF16),
         ],
-    )(dq, dko, dkr, n, mem, r, att, s, cot, gain, own, oth, next_own, next_oth)
+        micros=18,
+    )(dq, dko, dkr, n, mem, r, att, s, cot, gain, own, oth, next_own, next_oth, next_att)
 
 
 def self_post_kernel(
-    dq_ref, dko_ref, dkr_ref, n_ref, r_ref, att_ref, x_ref, cot_ref, gain_ref, own_ref, oth_ref,
-    gown_ref, goth_ref, out_ref, gg_ref, dn_ref, nt_ref, rt_ref,
+    dq_ref, dko_ref, dkr_ref, n_ref, x_ref, cot_ref, gain_ref, own_ref, oth_ref,
+    gown_ref, goth_ref, out_ref, gg_ref, dn_ref, nt_ref,
 ):
     step = pl.program_id(0)
     half = n_ref.shape[1] // 2
@@ -704,15 +731,13 @@
     def _():
         dn_ref[...] = jnp.zeros_like(dn_ref)
         nt_ref[...] = n_ref[...].T
-        rt_ref[...] = r_ref[...].T
 
     dkv = (dko_ref[...] + dkr_ref[...].astype(F32)).astype(BF16)
     grad = jnp.concatenate([dq_ref[...], dkv], axis=1)
     own, oth = rows_of(own_ref), rows_of(oth_ref)
-    parts = ((nt_ref, grad, 0), (rt_ref, att_ref[...], 2 * qcols))
-    weight_grads(half, parts, gown_ref, goth_ref)
-    dn_ref[:, :half] += dot_nt(grad, own[:, : 2 * qcols])
-    dn_ref[:, half:] += dot_nt(grad, oth[:, : 2 * qcols])
+    weight_grads(half, ((nt_ref, grad, 0),), gown_ref, goth_ref)
+    dn_ref[:, :half] += dot_nt(grad, own)
+    dn_ref[:, half:] += dot_nt(grad, oth)
 
     @pl.when(step == pl.num_programs(0) - 1)
     def _():
@@ -721,24 +746,117 @@
         out_ref[...] = (cot_ref[...] + dv).astype(BF16)
 
 
-def self_post(dq, dko, dkr, n, r, att, x, cot, gain, own, oth, qcols):
+def self_post(dq, dko, dkr, n, x, cot, gain, own, oth, qcols):
     rows, width = n.shape
     cols, shards, blk, packed = own.shape
-    spec = weight_spec(own, packed, lambda i: (0, i, 0, 0))
+    spec = weight_spec(own, 2 * qcols, lambda i: (0, i, 0, 0))
     by_shard = pl.BlockSpec((rows, qcols), lambda i: (0, i))
     full = fixed(rows, width)
     return call(
         self_post_kernel,
-        (shape(*own.shape), shape(*own.shape), shape(rows, width), shape(1, width, dtype=F32)),
+        (
+            shape(cols, shards, blk, 2 * qcols),
+            shape(cols, shards, blk, 2 * qcols),
+            shape(rows, width),
+            shape(1, width, dtype=F32),
+        ),
         (shards,),
-        [by_shard, by_shard, by_shard, full, full, by_shard, full, full, whole(gain), spec, spec],
+        [by_shard, by_shard, by_shard, full, full, full, whole(gain), spec, spec],
         (spec, spec, full, fixed(1, width)),
         [
             pltpu.VMEM((rows, width), F32),
             pltpu.VMEM((width, rows), BF16),
-            pltpu.VMEM((width, rows), BF16),
         ],
-    )(dq, dko, dkr, n, r, att, x, cot, gain, own, oth)
+        micros=14,
+    )(dq, dko, dkr, n, x, cot, gain, own, oth)
+
+
+def pack_layer_kernel(me_ref, q_ref, k_ref, v_ref, o_ref, out_ref):
+    qcols, kcols = q_ref.shape[1], k_ref.shape[1]
+    out_ref[:, :qcols] = q_ref[...]
+    for at in range(0, kcols, HEAD_DIM):
+        first = qcols + 2 * at
+        out_ref[:, first : first + HEAD_DIM] = k_ref[:, at : at + HEAD_DIM]
+        out_ref[:, first + HEAD_DIM : first + 2 * HEAD_DIM] = v_ref[:, at : at + HEAD_DIM]
+    out = o_ref[...]
+    out_ref[:, 2 * qcols :] = out if out.shape[0] == out_ref.shape[0] else out.T
+
+
+def pack_ffn_kernel(me_ref, g_ref, u_ref, d_ref, out_ref):
+    rows, packed = out_ref.shape
+    parts = [r[...] if r.shape[0] == rows else r[...].T for r in (g_ref, u_ref, d_ref)]
+    spare = packed - 3 * parts[0].shape[1]
+    if spare:
+        parts.append(jnp.zeros((rows, spare), BF16))
+    out_ref[...] = jnp.concatenate(parts, axis=1)
+
+
+def packed_rows(kernel, me, blk, by_row, by_col, packed):
+    if blk % 128:
+        by_row = by_row + [w.T for w in by_col]
+        by_col = []
+    specs = [pl.BlockSpec((blk, w.shape[1]), lambda i, at: (at[0], 0)) for w in by_row]
+    specs += [pl.BlockSpec((w.shape[0], blk), lambda i, at: (0, at[0])) for w in by_col]
+    return call(
+        kernel, shape(blk, packed), (1,), specs, fixed(blk, packed), prefetch=1, micros=2
+    )(me, *by_row, *by_col)
+
+
+def unpack_layer_kernel(pos_ref, x_ref, q_ref, k_ref, v_ref, *o_refs):
+    x = x_ref[0].astype(F32)
+    qcols, kcols = q_ref.shape[1], k_ref.shape[1]
+    q_ref[...] = x[:, :qcols]
+    for at in range(0, kcols, HEAD_DIM):
+        first = qcols + 2 * at
+        k_ref[:, at : at + HEAD_DIM] = x[:, first : first + HEAD_DIM]
+        v_ref[:, at : at + HEAD_DIM] = x[:, first + HEAD_DIM : first + 2 * HEAD_DIM]
+    for i, o_ref in enumerate(o_refs):
+        out = x[:, (2 + i) * qcols : (3 + i) * qcols]
+        o_ref[...] = out if o_ref.shape == out.shape else out.T
+
+
+def unpack_ffn_kernel(ff, pos_ref, x_ref, g_ref, u_ref, d_ref):
+    x = x_ref[0].astype(F32)
+    for i, ref in enumerate((g_ref, u_ref, d_ref)):
+        out = x[:, i * ff : (i + 1) * ff]
+        ref[...] = out if ref.shape == out.shape else out.T
+
+
+def unpacked(kernel, position, array, by_row, by_col):
+    count, blk, packed = array.shape
+    turned = blk % 128 == 0
+    outs = [shape(count * blk, c, dtype=F32) for c in by_row]
+    specs = [pl.BlockSpec((blk, c), lambda p, pos: (p, 0)) for c in by_row]
+    for c in by_col:
+        if turned:
+            outs.append(shape(c, count * blk, dtype=F32))
+            specs.append(pl.BlockSpec((c, blk), lambda p, pos: (0, p)))
+        else:
+            outs.append(shape(count * blk, c, dtype=F32))
+            specs.append(pl.BlockSpec((blk, c), lambda p, pos: (p, 0)))
+    results = call(
+        kernel,
+        tuple(outs),
+        (count,),
+        [pl.BlockSpec((1, blk, packed), lambda p, pos: (pos[p], 0, 0))],
+        tuple(specs),
+        prefetch=1,
+        micros=5,
+    )(position, array)
+    rows = len(by_row)
+    return results[:rows], [r if turned else r.T for r in results[rows:]]
+
+
+def unpack_layer(position, array, qcols, turned):
+    rows, outs = unpacked(
+        unpack_layer_kernel, position, array, (qcols, qcols // 2, qcols // 2), (qcols,) * turned
+    )
+    return (*rows, *outs)
+
+
+def unpack_ffn(position, array, ff):
+    _, turned = unpacked(functools.partial(unpack_ffn_kernel, ff), position, array, (), (ff, ff, ff))
+    return turned[0].T, turned[1].T, turned[2]
 
 
 def make_per_device(batch, shards):
@@ -787,42 +905,145 @@
         routes.append(route)
     both = ("batch", "group")
 
+    def pin(*values):
+        return lax.optimization_barrier(values)
+
+    def after(value, *others):
+        return lax.optimization_barrier((value,) + others)[0]
+
     def to_sequence(array):
         first = lax.axis_index("group") // 2
         received = []
         for second, route in enumerate(routes):
             part = lax.dynamic_index_in_dim(array, first ^ second, 0, keepdims=False)
             received.append(lax.ppermute(part, both, route))
-        return to_relative(jnp.concatenate(received, axis=0))
-
-    def from_sequence(array):
+        return jnp.concatenate(received, axis=0)
+
+    def send_back(array):
         array = to_absolute(array)
         rows = array.shape[0] // 2
-        back = [
+        return [
             lax.ppermute(array[i * rows : (i + 1) * rows], both, [(t, s) for s, t in route])
             for i, route in enumerate(routes)
         ]
+
+    def as_micros(back):
         first = lax.axis_index("group") // 2
         return jnp.where(first == 0, jnp.stack(back), jnp.stack(back[::-1]))
 
-    def spread(piece, order):
-        array = piece.reshape((1,) * bits + piece.shape)
+    def swap_z(array, mask):
+        return lax.ppermute(array, "group", [(z, z ^ mask) for z in range(shards)])
+
+    def shards_of(own):
+        far = swap_z(own, 2)
+        return [own, swap_z(own, 1), far, swap_z(far, 1)]
+
+    class Spread:
+        def __init__(self, pieces, order):
+            self.piece = (len(pieces),) + pieces[0].shape
+            self.order, self.own = list(order), None
+            self.array = jnp.stack(pieces).reshape((1,) * bits + self.piece)
+
+        def start(self):
+            self.pending = swap(self.array, 2 << self.order[0])
+
+        def land(self):
+            axis = bits - 1 - self.order.pop(0)
+            self.array = jnp.concatenate([self.array, self.pending], axis=axis)
+
+        def advance(self):
+            self.land()
+            if self.order:
+                self.start()
+            else:
+                self.own = self.array.reshape((cols,) + self.piece)
+                self.oth = swap(self.own, 1)
+
+        def finish(self):
+            while self.own is None:
+                self.advance()
+            return self.own, self.oth
+
+    def total_of(terms):
+        total = terms[0].astype(F32)
+        for term in terms[1:]:
+            total = total + term.astype(F32)
+        return total
+
+    def halves(terms, axis):
+        first = [lax.slice_in_dim(t, 0, 1, axis=axis) for t in terms]
+        second = [lax.slice_in_dim(t, 1, 2, axis=axis) for t in terms]
+        return first, second
+
+    def joined(terms):
+        return terms[0] if len(terms) == 1 else jnp.concatenate(terms, axis=-1)
+
+    def collecting(parts, order, z_masks):
+        piece = parts[0][0].shape[1:-1] + (sum(own.shape[-1] for own, _ in parts),)
+        pending = yield [swap(oth, 1) for _, oth in parts]
+        cube = (2,) * bits
+        terms = [
+            joined([own for own, _ in parts]).reshape(cube + piece),
+            joined(pending).reshape(cube + piece),
+        ]
         for bit in order:
-            axis = bits - 1 - bit
-            array = jnp.concatenate([array, swap(array, 2 << bit)], axis=axis)
-        own = array.reshape((cols,) + piece.shape)
-        return own, swap(own, 1)
-
-    def collect(own, oth, order):
-        total = own.astype(F32) + swap(oth, 1).astype(F32)
-        piece = total.shape[1:]
-        total = total.reshape((2,) * bits + piece)
-        for bit in order:
-            axis = bits - 1 - bit
-            keep = lax.slice_in_dim(total, 0, 1, axis=axis)
-            send = lax.slice_in_dim(total, 1, 2, axis=axis).astype(BF16)
-            total = keep + swap(send, 2 << bit).astype(F32)
-        return total.reshape(piece).astype(BF16)
+            terms, send = halves(terms, bits - 1 - bit)
+            terms = terms + (yield [swap(total_of(send).astype(BF16), 2 << bit)])
+        terms = [t.reshape(piece) for t in terms]
+        for mask in z_masks:
+            count = terms[0].shape[0] // 2
+            keep, send = halves([t.reshape((count, 2) + t.shape[1:]) for t in terms], 1)
+            received = yield [swap_z(total_of(send).astype(BF16), mask)]
+            terms = [t.reshape((count,) + piece[1:]) for t in keep + received]
+        return terms
+
+    def sharing(terms):
+        piece = terms[0].shape[1:]
+        array = total_of(terms).astype(BF16).reshape((1,) * bits + piece)
+        for bit in range(bits):
+            (pending,) = yield [swap(array, 2 << bit)]
+            array = jnp.concatenate([array, pending], axis=bits - 1 - bit)
+        array = array.reshape((cols,) + piece)
+        (pending,) = yield [swap(array, 1)]
+        return jnp.concatenate([array, pending], axis=0)
+
+    def whole_chain(parts, order):
+        terms = yield from collecting(parts, order, (1, 2))
+        return (yield from sharing(terms))
+
+    def ffn_chain(near, far):
+        received = yield [swap_z(total_of(far).astype(BF16), 2)]
+        return (yield from sharing(near + received))
+
+    def summing(small):
+        for mask in (1, 2):
+            (other,) = yield [swap_z(small, mask)]
+            small = small + other
+        for bit in range(bits + 1):
+            (other,) = yield [swap(small, 1 << bit)]
+            small = small + other
+        return small
+
+    class Chain:
+        def __init__(self, steps):
+            self.steps, self.result = steps, None
+            self.pending = next(steps)
+
+        def advance(self):
+            try:
+                self.pending = self.steps.send(self.pending)
+            except StopIteration as stop:
+                self.pending, self.result = [], stop.value
+
+    def land(chains, *extra):
+        chains = [c for c in chains if c.pending]
+        flat = [p for c in chains for p in c.pending]
+        flat = list(lax.optimization_barrier(tuple(flat) + extra))
+        for c in chains:
+            c.pending = [flat.pop(0) for _ in c.pending]
+        for c in chains:
+            c.advance()
+        return flat
 
     def per_device(
         tokens, memory, dec_segments, enc_segments, buckets,
@@ -839,34 +1060,46 @@
         up = tuple(range(bits))
         down = up[::-1]
 
-        def interleaved(keys, values):
-            parts = []
-            for at in range(0, keys.shape[1], HEAD_DIM):
-                parts += [keys[:, at : at + HEAD_DIM], values[:, at : at + HEAD_DIM]]
-            return jnp.concatenate(parts, axis=1)
-
-        def my_rows(weight):
-            return lax.dynamic_slice_in_dim(weight, me * blk, blk, 0)
-
-        def my_cols(weight):
-            return lax.dynamic_slice_in_dim(weight, me * blk, blk, 1).T
-
-        def gathered(parts):
-            return lax.all_gather(jnp.concatenate(parts, axis=1), "group", axis=0, tiled=False)
-
-        stream = to_sequence(tokens)
-        self_piece = gathered(
-            [my_rows(self_query), interleaved(my_rows(self_key), my_rows(self_value)), my_cols(self_output)]
+        ff = ffn_gate.shape[1]
+        at = me.reshape(1).astype(jnp.int32)
+        self_piece = packed_rows(
+            pack_layer_kernel, at, blk, [self_query, self_key, self_value], [self_output], 3 * qcols
         )
-        self_own, self_oth = spread(self_piece, up)
-        encoder = to_sequence(memory)
-        cross_piece = gathered(
-            [my_rows(cross_query), interleaved(my_rows(cross_key), my_rows(cross_value)), my_cols(cross_output)]
+        cross_piece = packed_rows(
+            pack_layer_kernel, at, blk, [cross_query, cross_key, cross_value], [cross_output], 3 * qcols
         )
-        cross_own, cross_oth = spread(cross_piece, down)
-        ffn_piece = gathered([my_rows(ffn_gate), my_rows(ffn_up), my_cols(ffn_down)])
-        ffn_parts = [spread(ffn_piece[:2], up), spread(ffn_piece[2:], down)]
-        cot = to_sequence(out_grad)
+        ffn_piece = packed_rows(
+            pack_ffn_kernel, at, blk, [], [ffn_gate.T, ffn_up.T, ffn_down], 3 * ff + -3 * ff % 128
+        )
+        self_far = swap_z(self_piece, 2)
+        self_near = swap_z(self_piece, 1)
+        cross_far = swap_z(cross_piece, 2)
+        cross_near = swap_z(cross_piece, 1)
+        self_last = swap_z(self_far, 1)
+        self_w = Spread([self_piece, self_near, self_far, self_last], up)
+        self_w.start()
+        cross_last = swap_z(cross_far, 1)
+        cross_w = Spread([cross_piece, cross_near, cross_far, cross_last], down)
+        cross_w.start()
+        stream = to_sequence(after(tokens, self_far, cross_far))
+        first = (self_w.pending, cross_w.pending)
+        self_w.advance()
+        cross_w.advance()
+        ffn_piece = after(ffn_piece, *first)
+        ffn_near = swap_z(ffn_piece, 1)
+        ffn_far = swap_z(ffn_piece, 2)
+        ffn_last = swap_z(ffn_far, 1)
+        encoder = to_sequence(after(memory, ffn_far))
+        near_w = Spread([ffn_piece, ffn_near], up)
+        far_w = Spread([ffn_far, ffn_last], down)
+        near_w.array = after(near_w.array, self_w.pending, cross_w.pending)
+        near_w.start()
+        far_w.array = after(far_w.array, self_w.pending, cross_w.pending)
+        far_w.start()
+        self_own, self_oth = self_w.finish()
+        cross_own, cross_oth = cross_w.finish()
+        cot = to_sequence(after(out_grad, encoder))
+        stream, encoder = to_relative(stream), to_relative(encoder)
 
         segments = jnp.concatenate([dec_segments, enc_segments], axis=1)
         length = dec_segments.shape[1]
@@ -887,7 +1120,7 @@
         kseg = dec_seg.reshape(length, 1)
         enc_kseg = jnp.concatenate(pieces_of(enc_seg, enc_chunk, 4)).reshape(-1, 1)
 
-        all_bias = lax.all_gather(rel_bias, "group", axis=1, tiled=True)
+        all_bias = jnp.concatenate(shards_of(rel_bias), axis=1)
         bucket_count = rel_bias.shape[0]
         onehot = (buckets[:, None] == jnp.arange(bucket_count)[None, :]).astype(F32)
         distance_bias = lax.dot_general(
@@ -900,52 +1133,54 @@
 
         n_one, q_one, kv_one = project_qkv(stream, gain_one, self_own, self_oth, qcols)
         kv_one_oth = swap(kv_one, 1)
-        att_one, lse_one = self_attention(ids, q_one, kv_one, kv_one_oth, slabs, kseg, qseg)
         kv_two = project_kv(encoder, cross_own, cross_oth, qcols)
         kv_two_oth = swap(kv_two, 1)
+        near_w.pending, far_w.pending, q_one = pin(near_w.pending, far_w.pending, q_one)
+        near_w.advance()
+        far_w.advance()
+        att_one, lse_one = self_attention(ids, q_one, kv_one, kv_one_oth, slabs, kseg, qseg)
         stream_one, n_two, q_two = output_and_query(
             stream, att_one, gain_two, self_own, self_oth, cross_own, cross_oth, qcols
         )
         att_two, lse_two = cross_attention(q_two, kv_two, kv_two_oth, enc_kseg, qseg)
+        near_w.pending, far_w.pending, att_two = pin(near_w.pending, far_w.pending, att_two)
+        near_w.finish()
+        far_w.finish()
         stream_two, n_three = output_and_norm(stream_one, att_two, gain_three, cross_own, cross_oth, qcols)
 
-        ffn_sums, ffn_grads = [], []
-        for (own, oth), order in zip(ffn_parts, (down, up)):
-            y, dn, grad_own, grad_oth = feed_forward(n_three, cot, own, oth)
-            ffn_sums.append((y, dn))
-            ffn_grads.append(collect(grad_own, grad_oth, order))
-        (ya, da), (yb, db) = ffn_sums
+        cot = to_relative(cot)
+        ya, da, grad_own, grad_oth = feed_forward(n_three, cot, near_w.own, near_w.oth, ff)
+        near_g = Chain(collecting([(grad_own, grad_oth)], down, (1,)))
+        n_three, ya = pin(n_three, ya)
+        yb, db, grad_own, grad_oth = feed_forward(n_three, cot, far_w.own, far_w.oth, ff)
+        far_g = Chain(collecting([(grad_own, grad_oth)], up, (1,)))
+        (db,) = land([near_g], db)
         block_out, cot_two, round_two, grad_gain_three, ga_two = after_ffn(
             stream_two, ya, yb, da, db, cot, gain_three, cross_own, cross_oth, qcols
         )
-        block_out = from_sequence(block_out)
+        (ga_two,) = land([far_g], ga_two)
+        block_back = send_back(block_out)
 
         dq_two, dkv_two, dkv_two_send = cross_attention_back(
             q_two, ga_two, lse_two, kv_two, kv_two_oth, enc_kseg, qseg
         )
-        grad_own, grad_oth, cot_one, round_one, grad_gain_two, memory_grad, ga_one = cross_post(
+        (dq_two,) = land([near_g], dq_two)
+        (grad_own, grad_oth, out_own, out_oth, cot_one, round_one, grad_gain_two, memory_grad, ga_one) = cross_post(
             dq_two, dkv_two, swap(dkv_two_send, 1), n_two, encoder, round_two, att_two, stream_one,
-            cot_two, gain_two, cross_own, cross_oth, self_own, self_oth, qcols,
+            cot_two, gain_two, cross_own, cross_oth, self_own, self_oth, att_one, qcols,
         )
-        cross_grads = collect(grad_own, grad_oth, down)
-        memory_grad = from_sequence(memory_grad).astype(F32)
+        cross_g = Chain(whole_chain([(grad_own, grad_oth), (out_own, out_oth)], up))
+        (ga_one,) = land([far_g, cross_g], ga_one)
         dq_one, dkv_one, dkv_one_send, folded = self_attention_back(
             ids, q_one, ga_one, lse_one, kv_one, kv_one_oth, slabs, kseg, qseg
         )
+        (dq_one,) = land([near_g, far_g], dq_one)
         grad_own, grad_oth, tokens_grad, grad_gain_one = self_post(
-            dq_one, dkv_one, swap(dkv_one_send, 1), n_one, round_one, att_one, stream, cot_one,
+            dq_one, dkv_one, swap(dkv_one_send, 1), n_one, stream, cot_one,
             gain_one, self_own, self_oth, qcols,
         )
-        self_grads = collect(grad_own, grad_oth, up)
-        tokens_grad = from_sequence(tokens_grad).astype(F32)
-
-        def finish(piece):
-            mine = lax.psum_scatter(piece, "group", scatter_dimension=0, tiled=False)
-            return lax.all_gather(mine, "batch", axis=0, tiled=True)
-
-        ffn_final = finish(jnp.concatenate(ffn_grads, axis=0))
-        cross_final = finish(cross_grads)
-        self_final = finish(self_grads)
+        self_g = Chain(whole_chain([(grad_own, grad_oth)], down))
+        tokens_back = send_back(tokens_grad)
 
         padded = jnp.pad(folded, ((0, 0), (0, 0), (0, 8)))
         distance_grad = sum(padded[:, i, 128 + i : 128 + i + length] for i in range(8))
@@ -953,37 +1188,45 @@
             onehot, distance_grad, (((0,), (1,)), ((), ())), precision=HIGHEST, preferred_element_type=F32
         )
         small = [to_absolute(g).reshape(width) for g in (grad_gain_one, grad_gain_two, grad_gain_three)]
-        small = lax.psum(jnp.concatenate(small + [bucket_grad.reshape(-1)]), both)
+        bucket_grad = bucket_grad.reshape(bucket_count, shards, -1)
+        bucket_grad = [
+            lax.dynamic_index_in_dim(bucket_grad, z ^ p, 1, keepdims=False) for p in range(shards)
+        ]
+        small = jnp.concatenate(small + [g.reshape(-1) for g in bucket_grad])
+        small_g = Chain(summing(small))
+        land([self_g, near_g, far_g, cross_g])
+        while near_g.pending or far_g.pending:
+            land([self_g, near_g, far_g, cross_g])
+        ffn_g = Chain(ffn_chain(near_g.result, far_g.result))
+        memory_back = send_back(after(memory_grad, *self_g.pending))
+        chains = [self_g, cross_g, ffn_g, small_g]
+        while any(c.pending for c in chains):
+            land(chains)
+        position = place_of(me ^ jnp.arange(batch)).astype(jnp.int32)
+        ffn_final = unpack_ffn(position, ffn_g.result, ff)
+        *cross_final, self_out_grad = unpack_layer(position, cross_g.result, qcols, 2)
+        self_final = (*unpack_layer(position, self_g.result, qcols, 0), self_out_grad)
+        late = self_g.result
+        block_out = as_micros([after(part, late) for part in block_back])
+        memory_grad = as_micros([after(part, late) for part in memory_back]).astype(F32)
+        tokens_grad = as_micros([after(part, late) for part in tokens_back]).astype(F32)
+
+        small = small_g.result
         gains = [small[i * width : (i + 1) * width] for i in range(3)]
-        bucket_grad = small[3 * width :].reshape(bucket_grad.shape)
-        heads_here = rel_bias.shape[1]
-        bucket_grad = lax.dynamic_slice_in_dim(bucket_grad, z * heads_here, heads_here, 1)
-
-        def unpack(final):
-            final = final.astype(F32)
-            kv = final[:, qcols : 2 * qcols].reshape(width, -1, 2, HEAD_DIM)
-            return (
-                final[:, :qcols],
-                kv[:, :, 0, :].reshape(width, -1),
-                kv[:, :, 1, :].reshape(width, -1),
-                final[:, 2 * qcols :].T,
-            )
-
-        ff = ffn_gate.shape[1]
-        ffn_final = ffn_final.astype(F32)
+        bucket_grad = small[3 * width :].reshape(shards, bucket_count, -1)
+        bucket_grad = lax.dynamic_index_in_dim(bucket_grad, z, 0, keepdims=False)
+
         return (
             block_out,
             tokens_grad,
             memory_grad,
             gains[0],
-            *unpack(self_final),
+            *self_final,
             bucket_grad,
             gains[1],
-            *unpack(cross_final),
+            *cross_final,
             gains[2],
-            ffn_final[:, :ff],
-            ffn_final[:, ff : 2 * ff],
-            ffn_final[:, 2 * ff :].T,
+            *ffn_final,
         )
 
     return per_device

time: 954 us -> 683 us (0.72)
  local copies, waits for them, and re-layouts: 198 us -> 56.7 us
  blocking collectives: 117 us -> 0 us
  waiting for transfers between devices: 243 us -> 216 us
  Pallas kernels: 215 us -> 241 us
  starting transfers between devices: 75.5 us -> 95.7 us
  between operations: 15.5 us -> 2.4 us
  other arithmetic: 75.4 us -> 62.7 us
    ppermute x6 -> x27, waiting for transfers between devices: 10.5 us -> 95.1 us  [the longest x21 91.5 us: swap_z(): return lax.ppermute(array, 'group', [(z, z ^ mask) for z in range(shards)])]
    all_gather x3 -> x0, blocking collectives: 74.1 us -> none  [the longest x2 62.2 us: gathered(): lax.all_gather(jnp.concatenate(parts, axis=1), 'group', axis=0, tiled=False)]
    reduce_scatter x3 -> x0, waiting for transfers between devices: 57.1 us -> none  [finish(): mine = lax.psum_scatter(piece, 'group', scatter_dimension=0, tiled=False)]
    ppermute x12 -> x0, local copies, waits for them, and re-layouts: 47.1 us -> none  [swap(): return lax.ppermute(array, 'batch', [(b, b ^ mask) for b in range(batch)])]
    psum x1 -> x0, blocking collectives: 43 us -> none  [per_device(): small = lax.psum(jnp.concatenate(small + [bucket_grad.reshape(-1)]), both)]
    ppermute x29 -> x42, waiting for transfers between devices: 145 us -> 106 us  [swap(): return lax.ppermute(array, 'batch', [(b, b ^ mask) for b in range(batch)])]
    unnamed x202 -> x200, local copies, waits for them, and re-layouts: 60.1 us -> 22.7 us
    add x8 -> x5, other arithmetic: 29.5 us -> 0.03 us  [summing(): small = small + other]
  transfers between devices with their start and end apart: 48 -> 75, of which waited for: 14 -> 29; matrix products, arithmetic and copies ran while one was open for 25% -> 15% of each run, Pallas kernels for 17% -> 36%
where the time goes in v2:
time: 683 us; the launch traced here: 675 us
  Pallas kernels  241 us (35%)
  waiting for transfers between devices  216 us (32%)
  starting transfers between devices  95.7 us (14%)
  other arithmetic  62.7 us (9%)
  local copies, waits for them, and re-layouts  56.7 us (8%)
    ppermute x42, waiting for transfers between devices, swap(): return lax.ppermute(array, 'batch', [(b, b ^ mask) for b in range(batch)])  106 us
    ppermute x21, waiting for transfers between devices, swap_z(): return lax.ppermute(array, 'group', [(z, z ^ mask) for z in range(shards)])  91.5 us
    pallas_call x2, Pallas kernels, feed_forward(): call(functools.partial(ffn_kernel, ff), (shape(rows, width, dtype=F32), s...  43.9 us
    ppermute x42, starting transfers between devices, swap(): return lax.ppermute(array, 'batch', [(b, b ^ mask) for b in range(batch)])  36.7 us
    pallas_call x1, Pallas kernels, self_attention_back(): call(self_back_kernel, (shape(*q.shape), shape(*own.shape, dtype=F32), sh...  32.1 us
    ppermute x21, starting transfers between devices, swap_z(): return lax.ppermute(array, 'group', [(z, z ^ mask) for z in range(shards)])  29.2 us
    unnamed x200, local copies, waits for them, and re-layouts  22.7 us
    pallas_call x3, Pallas kernels, unpacked(): call(kernel, tuple(outs), (count,), [pl.BlockSpec((1, blk, packed), lambd...  21.9 us
  transfers between devices with their start and end apart: 75, of which 29 were waited for; matrix products, arithmetic and copies ran while one was open for 15% of the time, Pallas kernels for 36%

profile of v2, /device:TPU:0, one launch (start us, length us, event | category | flops | bytes accessed | tf_op | source)
XLA Modules:
  0.0 674.7 jit_solution(947085342244754373)
XLA Ops:
  25.2 11.1 %shard_map.344.slab_ref = f32[16,128,1152]{2,1,0:T(8,128)} custom-call(f32[16,1,1152]{2,1,0:T(1,128)} %reshape.458.base_ref), custom_call_target="tpu_custom_call" | custom-call | flops 11000000512 | bytes 33000000 | tf_op jit(solution)/shard_map/pallas_call | solution.py:339
  49.0 9.5 %collective-permute-done.6 = bf16[1,1,4,128,768]{4,3,2,1,0:T(8,128)(2,1)S(1)} collective-permute-done((bf16[1,1,4,128,768]{4,3,2,1,0:T(8,128)(2,1)S(1)}, bf16[1,1,4,128,768]{4,3,2,1,0:T(8,128)(2,1)S(1)}, u32[]{:S(2)}, u32[]{:S(2)}) %collective-permute-start.6) | collective-permute-done | bytes 786464 | tf_op jit(solution)/shard_map/ppermute | solution.py:868
  71.8 24.1 %collective-permute-done.14 = bf16[128,2176]{1,0:T(8,128)(2,1)S(1)} collective-permute-done((bf16[128,2176]{1,0:T(8,128)(2,1)S(1)}, bf16[128,2176]{1,0:T(8,128)(2,1)S(1)}, u32[]{:S(2)}, u32[]{:S(2)}) %collective-permute-start.14) | collective-permute-done | bytes 557088 | tf_op jit(solution)/shard_map/ppermute | solution.py:935
  101.3 7.7 %collective-permute-done.27 = bf16[128,1024]{1,0:T(8,128)(2,1)S(1)} collective-permute-done((bf16[128,1024]{1,0:T(8,128)(2,1)S(1)}, bf16[128,1024]{1,0:T(8,128)(2,1)S(1)}, u32[]{:S(2)}, u32[]{:S(2)}) %collective-permute-start.27) | collective-permute-done | bytes 262176 | tf_op jit(solution)/shard_map/ppermute | solution.py:919
  127.4 6.9 %collective-permute-start.23 = (bf16[4,4,128,768]{3,2,1,0:T(8,128)(2,1)}, bf16[4,4,128,768]{3,2,1,0:T(8,128)(2,1)}, u32[]{:S(2)}, u32[]{:S(2)}) collective-permute-start(bf16[4,4,128,768]{3,2,1,0:T(8,128)(2,1)} %bitcast.43.wq_own.own_ref.wo_own), channel_id=1, source_target_pairs={{0,4},{4,0},{8,12},{12,8},{16,20},{20,16},{24,28},{28,24},{1,5},{5... | collective-permute-start | bytes 9437192 | tf_op jit(solution)/shard_map/ppermute | solution.py:868
  143.1 6.4 shard_map.343
  149.5 17.7 %collective-permute-done.13 = bf16[1,1,2,128,2176]{4,3,2,1,0:T(8,128)(2,1)} collective-permute-done((bf16[1,1,2,128,2176]{4,3,2,1,0:T(8,128)(2,1)S(1)}, bf16[1,1,2,128,2176]{4,3,2,1,0:T(8,128)(2,1)}, u32[]{:S(2)}, u32[]{:S(2)}) %collective-permute-start.13) | collective-permute-done | bytes 1114144 | tf_op jit(solution)/shard_map/ppermute | solution.py:868
  178.7 20.3 %shard_map.345 = (bf16[512,1024]{1,0:T(8,128)(2,1)}, f32[16,1,512]{2,1,0:T(1,128)}) custom-call(s32[4]{0:T(128)} %pad_add_fusion.2.ids_ref, bf16[512,1024]{1,0:T(8,128)(2,1)} %get-tuple-element.137.q_ref, bf16[512,1024]{1,0:T(8,128)(2,1)} %get-tuple-element.138.own_ref, bf16[512,1024]{1,0:T(8,128)(2,1)} %copy-done.47, f32[16,128,1152]{2,1,0:T(8,128)} %shard_map.344.slab_ref, ...), custom_call_target="tpu_custom_call" | custom-call | flops 20000000000 | bytes 60000000 | tf_op jit(solution)/shard_map/pallas_call | solution.py:446
  198.9 9.8 %shard_map.346 = (f32[512,1024]{1,0:T(8,128)}, bf16[512,1024]{1,0:T(8,128)(2,1)}, bf16[512,1024]{1,0:T(8,128)(2,1)}) custom-call(bf16[512,1024]{1,0:T(8,128)(2,1)} %copy-done.36, bf16[512,1024]{1,0:T(8,128)(2,1)} %get-tuple-element.139.att_ref.att_one_ref, f32[1,1024]{1,0:T(1,128)} %copy-done.45, bf16[4,4,128,768]{3,2,1,0:T(8,128)(2,1)} %bitcast.262, ...), custom_call_target="tpu_custom_call" | custom-call | flops 10000000000 | bytes 30000000 | tf_op jit(solution)/shard_map/pallas_call | solution.py:172
  208.8 16.0 %shard_map.348 = (bf16[512,1024]{1,0:T(8,128)(2,1)}, f32[16,1,512]{2,1,0:T(1,128)}) custom-call(bf16[512,1024]{1,0:T(8,128)(2,1)} %get-tuple-element.143.q_ref, bf16[256,1024]{1,0:T(8,128)(2,1)} %shard_map.347.own_ref, bf16[256,1024]{1,0:T(8,128)(2,1)} %collective-permute-done.28.oth_ref, s32[512,1]{1,0:T(8,128)} %copy.52.kseg_ref, ...), custom_call_target="tpu_custom_call" | custom-call | flops 16000000000 | bytes 48000000 | tf_op jit(solution)/shard_map/pallas_call | solution.py:468
  240.2 6.7 shard_map.349
  246.9 21.9 %shard_map.350 = (f32[512,1024]{1,0:T(8,128)}, f32[512,1024]{1,0:T(8,128)}, bf16[4,2,128,2176]{3,2,1,0:T(8,128)(2,1)}, bf16[4,2,128,2176]{3,2,1,0:T(8,128)(2,1)}) custom-call(bf16[512,1024]{1,0:T(8,128)(2,1)} %get-tuple-element.153.n_ref, bf16[512,1024]{1,0:T(8,128)(2,1)} %constant_dynamic-update-slice_fusion.52.r_ref.cot_ref, ...), custom_call_target="tpu_custom_call" | custom-call | flops 22000001024 | bytes 66000000 | tf_op jit(solution)/shard_map/pallas_call | solution.py:270
  269.8 22.0 %shard_map.351 = (f32[512,1024]{1,0:T(8,128)}, f32[512,1024]{1,0:T(8,128)}, bf16[4,2,128,2176]{3,2,1,0:T(8,128)(2,1)}, bf16[4,2,128,2176]{3,2,1,0:T(8,128)(2,1)}) custom-call(bf16[512,1024]{1,0:T(8,128)(2,1)} %get-tuple-element.153.n_ref, bf16[512,1024]{1,0:T(8,128)(2,1)} %constant_dynamic-update-slice_fusion.52.r_ref.cot_ref, ...), custom_call_target="tpu_custom_call" | custom-call | flops 22000001024 | bytes 66000000 | tf_op jit(solution)/shard_map/pallas_call | solution.py:270
  296.1 10.2 %shard_map.352 = (bf16[512,1024]{1,0:T(8,128)(2,1)}, f32[512,1024]{1,0:T(8,128)}, bf16[512,1024]{1,0:T(8,128)(2,1)}, f32[1,1024]{1,0:T(1,128)}, bf16[512,1024]{1,0:T(8,128)(2,1)}) custom-call(f32[512,1024]{1,0:T(8,128)} %get-tuple-element.147.s_ref, f32[512,1024]{1,0:T(8,128)} %get-tuple-element.152.ya_ref, f32[512,1024]{1,0:T(8,128)} %get-tuple-element.155.yb_ref, ...), custom_call_target="tpu_custom_call" | custom-call | flops 10000000000 | bytes 30000000 | tf_op jit(solution)/shard_map/pallas_call | solution.py:311
  314.9 6.3 collective-permute-start.70
  331.7 21.7 %shard_map.353 = (bf16[512,1024]{1,0:T(8,128)(2,1)}, f32[256,1024]{1,0:T(8,128)}, bf16[256,1024]{1,0:T(8,128)(2,1)}) custom-call(bf16[512,1024]{1,0:T(8,128)(2,1)} %get-tuple-element.143.q_ref, bf16[512,1024]{1,0:T(8,128)(2,1)} %get-tuple-element.165.ga_ref, f32[16,1,512]{2,1,0:T(1,128)} %get-tuple-element.166.lse_ref, ...), custom_call_target="tpu_custom_call" | custom-call | flops 20999999488 | bytes 63000000 | tf_op jit(solution)/shard_map/pallas_call | solution.py:605
  360.2 13.7 %collective-permute-done.35 = bf16[1,2,2,128,2176]{4,3,2,1,0:T(8,128)(2,1)} collective-permute-done((bf16[1,2,2,128,2176]{4,3,2,1,0:T(8,128)(2,1)}, bf16[1,2,2,128,2176]{4,3,2,1,0:T(8,128)(2,1)}, u32[]{:S(2)}, u32[]{:S(2)}) %collective-permute-start.35) | collective-permute-done | bytes 2228256 | tf_op jit(solution)/shard_map/ppermute | solution.py:868
  373.9 19.3 %shard_map.354 = (bf16[4,4,128,768]{3,2,1,0:T(8,128)(2,1)}, bf16[4,4,128,768]{3,2,1,0:T(8,128)(2,1)}, bf16[4,4,128,256]{3,2,1,0:T(8,128)(2,1)}, bf16[4,4,128,256...) custom-call(bf16[512,1024]{1,0:T(8,128)(2,1)} %get-tuple-element.171, ...), custom_call_target="tpu_custom_call" | custom-call | flops 17999998976 | bytes 54000000 | tf_op jit(solution)/shard_map/pallas_call | solution.py:684
  410.6 32.1 %shard_map.355 = (bf16[512,1024]{1,0:T(8,128)(2,1)}, f32[512,1024]{1,0:T(8,128)}, bf16[512,1024]{1,0:T(8,128)(2,1)}, f32[16,8,1152]{2,1,0:T(8,128)}) custom-call(s32[4]{0:T(128)} %pad_add_fusion.2.ids_ref, bf16[512,1024]{1,0:T(8,128)(2,1)} %get-tuple-element.137.q_ref, bf16[512,1024]{1,0:T(8,128)(2,1)} %get-tuple-element.181.ga_ref, ...), custom_call_target="tpu_custom_call" | custom-call | flops 32000000000 | bytes 96000000 | tf_op jit(solution)/shard_map/pallas_call | solution.py:555
  453.1 12.0 %shard_map.356 = (bf16[4,4,128,512]{3,2,1,0:T(8,128)(2,1)}, bf16[4,4,128,512]{3,2,1,0:T(8,128)(2,1)}, bf16[512,1024]{1,0:T(8,128)(2,1)}, f32[1,1024]{1,0:T(1,128)}) custom-call(bf16[512,1024]{1,0:T(8,128)(2,1)} %get-tuple-element.184.dq_ref, f32[512,1024]{1,0:T(8,128)} %get-tuple-element.185.dko_ref, bf16[512,1024]{1,0:T(8,128)(2,1)} %collective-permute-done.43.dkr_ref, ...), custom_call_target="tpu_custom_call" | custom-call | flops 14000000000 | bytes 42000000 | tf_op jit(solution)/shard_map/pallas_call | solution.py:755
  469.8 12.9 %collective-permute-done.45 = bf16[1,1,128,2176]{3,2,1,0:T(8,128)(2,1)S(1)} collective-permute-done((bf16[1,1,128,2176]{3,2,1,0:T(8,128)(2,1)S(1)}, bf16[1,1,128,2176]{3,2,1,0:T(8,128)(2,1)S(1)}, u32[]{:S(2)}, u32[]{:S(2)}) %collective-permute-start.45) | collective-permute-done | bytes 557088 | tf_op jit(solution)/shard_map/ppermute | solution.py:935
  482.7 11.4 %collective-permute-done.46 = bf16[1,1,128,2176]{3,2,1,0:T(8,128)(2,1)S(1)} collective-permute-done((bf16[1,1,128,2176]{3,2,1,0:T(8,128)(2,1)S(1)}, bf16[1,1,128,2176]{3,2,1,0:T(8,128)(2,1)S(1)}, u32[]{:S(2)}, u32[]{:S(2)}) %collective-permute-start.46) | collective-permute-done | bytes 557088 | tf_op jit(solution)/shard_map/ppermute | solution.py:935
  504.2 8.3 %collective-permute-done.51 = f32[3584]{0:T(1024)S(1)} collective-permute-done((f32[3584]{0:T(1024)S(1)}, f32[3584]{0:T(1024)S(1)}, u32[]{:S(2)}, u32[]{:S(2)}) %collective-permute-start.51) | collective-permute-done | bytes 14368 | tf_op jit(solution)/shard_map/ppermute | solution.py:935
  512.5 13.3 %collective-permute-done.50 = bf16[1,128,2176]{2,1,0:T(8,128)(2,1)S(1)} collective-permute-done((bf16[1,128,2176]{2,1,0:T(8,128)(2,1)S(1)}, bf16[1,128,2176]{2,1,0:T(8,128)(2,1)S(1)}, u32[]{:S(2)}, u32[]{:S(2)}) %collective-permute-start.50) | collective-permute-done | bytes 557088 | tf_op jit(solution)/shard_map/ppermute | solution.py:935
  525.8 15.9 %collective-permute-done.49 = bf16[1,1,4,128,1024]{4,3,2,1,0:T(8,128)(2,1)S(1)} collective-permute-done((bf16[1,1,4,128,1024]{4,3,2,1,0:T(8,128)(2,1)S(1)}, bf16[1,1,4,128,1024]{4,3,2,1,0:T(8,128)(2,1)S(1)}, u32[]{:S(2)}, u32[]{:S(2)}) %collective-permute-start.49) | collective-permute-done | bytes 1048608 | tf_op jit(solution)/shard_map/ppermute | solution.py:868
  556.8 9.7 %collective-permute-done.54 = bf16[1,1,128,2176]{3,2,1,0:T(8,128)(2,1)S(1)} collective-permute-done((bf16[1,1,128,2176]{3,2,1,0:T(8,128)(2,1)S(1)}, bf16[1,1,128,2176]{3,2,1,0:T(8,128)(2,1)S(1)}, u32[]{:S(2)}, u32[]{:S(2)}) %collective-permute-start.54) | collective-permute-done | bytes 557088 | tf_op jit(solution)/shard_map/ppermute | solution.py:868
  571.9 6.8 %collective-permute-done.56 = bf16[2,1,128,512]{3,2,0,1:T(8,128)(2,1)S(1)} collective-permute-done((bf16[2,1,128,512]{3,2,0,1:T(8,128)(2,1)S(1)}, bf16[2,1,128,512]{3,2,0,1:T(8,128)(2,1)S(1)}, u32[]{:S(2)}, u32[]{:S(2)}) %collective-permute-start.56) | collective-permute-done | bytes 262176 | tf_op jit(solution)/shard_map/ppermute | solution.py:935
  580.5 10.6 %collective-permute-done.58 = bf16[1,2,128,2176]{3,2,1,0:T(8,128)(2,1)S(1)} collective-permute-done((bf16[1,2,128,2176]{3,2,1,0:T(8,128)(2,1)S(1)}, bf16[1,2,128,2176]{3,2,1,0:T(8,128)(2,1)S(1)}, u32[]{:S(2)}, u32[]{:S(2)}) %collective-permute-start.58) | collective-permute-done | bytes 1114144 | tf_op jit(solution)/shard_map/ppermute | solution.py:868
  606.9 12.0 %collective-permute-done.66 = f32[3584]{0:T(1024)S(1)} collective-permute-done((f32[3584]{0:T(1024)S(1)}, f32[3584]{0:T(1024)S(1)}, u32[]{:S(2)}, u32[]{:S(2)}) %collective-permute-start.66) | collective-permute-done | bytes 14368 | tf_op jit(solution)/shard_map/ppermute | solution.py:868
  636.5 8.8 %shard_map.359 = (f32[704,1024]{1,0:T(8,128)}, f32[704,1024]{1,0:T(8,128)}, f32[704,1024]{1,0:T(8,128)}) custom-call(s32[8]{0:T(128)} %multiply_or_fusion.pos_ref, bf16[8,128,2176]{2,1,0:T(8,128)(2,1)} %pad_maximum_fusion.2.x_ref), custom_call_target="tpu_custom_call" | custom-call | flops 5000000000 | bytes 15000000 | tf_op jit(solution)/shard_map/pallas_call | solution.py:837
  648.2 6.9 %shard_map.358 = (f32[1024,256]{1,0:T(8,128)}, f32[1024,128]{1,0:T(8,128)}, f32[1024,128]{1,0:T(8,128)}, f32[256,1024]{1,0:T(8,128)}, f32[256,1024]{1,0:T(8,128)}) custom-call(s32[8]{0:T(128)} %multiply_or_fusion.pos_ref, bf16[8,128,1024]{2,1,0:T(8,128)(2,1)} %pad_maximum_fusion.8.x_ref), custom_call_target="tpu_custom_call" | custom-call | flops 5000000000 | bytes 15000000 | tf_op jit(solution)/shard_map/pallas_call | solution.py:837
  661.5 6.2 shard_map.357
  (466 shorter events, 254.0 us)
Async XLA Ops:
  6.5 29.9 %collective-permute-start.4 = (bf16[128,768]{1,0:T(8,128)(2,1)}, bf16[128,768]{1,0:T(8,128)(2,1)S(1)}, u32[]{:S(2)}, u32[]{:S(2)}) collective-permute-start(bf16[128,768]{1,0:T(8,128)(2,1)} %shard_map.340), channel_id=1, source_target_pairs={{0,1},{1,0},{2,3},{3,2},{4,5},{5,4},{6,7},{7,6},{8,9},{9,8},{10,11... | collective-permute-start | bytes 589832 | tf_op jit(solution)/shard_map/ppermute | solution.py:935
  60.1 35.8 %collective-permute-start.14 = (bf16[128,2176]{1,0:T(8,128)(2,1)S(1)}, bf16[128,2176]{1,0:T(8,128)(2,1)S(1)}, u32[]{:S(2)}, u32[]{:S(2)}) collective-permute-start(bf16[128,2176]{1,0:T(8,128)(2,1)S(1)} %copy-done.28), channel_id=1, source_target_pairs={{0,2},{1,3},{2,0},{3,1},{4,6},{5,7},{6,4},{7,5},{8,10},{9,11},{10,... | collective-permute-start | bytes 1671176 | tf_op jit(solution)/shard_map/ppermute | solution.py:935
  60.4 37.6 %collective-permute-start.10 = (bf16[128,2176]{1,0:T(8,128)(2,1)S(1)}, bf16[128,2176]{1,0:T(8,128)(2,1)}, u32[]{:S(2)}, u32[]{:S(2)}) collective-permute-start(bf16[128,2176]{1,0:T(8,128)(2,1)S(1)} %copy-done.28), channel_id=1, source_target_pairs={{0,1},{1,0},{2,3},{3,2},{4,5},{5,4},{6,7},{7,6},{8,9},{9,8},{10,11... | collective-permute-start | bytes 1671176 | tf_op jit(solution)/shard_map/ppermute | solution.py:935
  62.0 53.2 %collective-permute-start.11 = (bf16[1,2,4,128,768]{4,3,2,1,0:T(8,128)(2,1)}, bf16[1,2,4,128,768]{4,3,2,1,0:T(8,128)(2,1)}, u32[]{:S(2)}, u32[]{:S(2)}) collective-permute-start(bf16[1,2,4,128,768]{4,3,2,1,0:T(8,128)(2,1)} %pad_maximum_fusion.9), channel_id=1, source_target_pairs={{0,16},{4,20},{8,24},{12,28},{16,0},{20,4},{24,8},{28,12},{1,17},{... | collective-permute-start | bytes 4718600 | tf_op jit(solution)/shard_map/ppermute | solution.py:868
  71.2 54.1 %collective-permute-start.12 = (bf16[2,1,4,128,768]{4,3,2,1,0:T(8,128)(2,1)S(1)}, bf16[2,1,4,128,768]{4,3,2,1,0:T(8,128)(2,1)S(1)}, u32[]{:S(2)}, u32[]{:S(2)}) collective-permute-start(bf16[2,1,4,128,768]{4,3,2,1,0:T(8,128)(2,1)S(1)} %pad_maximum_fusion.10), channel_id=1, source_target_pairs={{0,8},{4,12},{8,0},{12,4},{16,24},{20,28},{24,16},{28,20},{1,9},{5... | collective-permute-start | bytes 4718600 | tf_op jit(solution)/shard_map/ppermute | solution.py:868
  99.3 24.9 %collective-permute-start.15 = (bf16[128,2176]{1,0:T(8,128)(2,1)S(1)}, bf16[128,2176]{1,0:T(8,128)(2,1)S(1)}, u32[]{:S(2)}, u32[]{:S(2)}) collective-permute-start(bf16[128,2176]{1,0:T(8,128)(2,1)S(1)} %copy-done.31), channel_id=1, source_target_pairs={{0,1},{1,0},{2,3},{3,2},{4,5},{5,4},{6,7},{7,6},{8,9},{9,8},{10,11... | collective-permute-start | bytes 1671176 | tf_op jit(solution)/shard_map/ppermute | solution.py:935
  109.7 28.1 %collective-permute-start.30 = (bf16[256,1024]{1,0:T(8,128)(2,1)S(1)}, bf16[256,1024]{1,0:T(8,128)(2,1)S(1)}, u32[]{:S(2)}, u32[]{:S(2)}) collective-permute-start(bf16[256,1024]{1,0:T(8,128)(2,1)S(1)} %get-tuple-element.250), channel_id=1, source_target_pairs={{0,2},{1,6},{2,4},{3,0},{4,3},{5,7},{6,5},{7,1},{8,10},{9,14},{10,... | collective-permute-start | bytes 1572872 | tf_op jit(solution)/shard_map/ppermute | solution.py:919
  117.0 26.1 %collective-permute-start.17 = (bf16[4,4,128,768]{3,2,1,0:T(8,128)(2,1)S(1)}, bf16[4,4,128,768]{3,2,1,0:T(8,128)(2,1)}, u32[]{:S(2)}, u32[]{:S(2)}) collective-permute-start(bf16[4,4,128,768]{3,2,1,0:T(8,128)(2,1)S(1)} %bitcast.260), channel_id=1, source_target_pairs={{0,4},{4,0},{8,12},{12,8},{16,20},{20,16},{24,28},{28,24},{1,5},{5... | collective-permute-start | bytes 9437192 | tf_op jit(solution)/shard_map/ppermute | solution.py:868
  127.4 46.1 %collective-permute-start.23 = (bf16[4,4,128,768]{3,2,1,0:T(8,128)(2,1)}, bf16[4,4,128,768]{3,2,1,0:T(8,128)(2,1)}, u32[]{:S(2)}, u32[]{:S(2)}) collective-permute-start(bf16[4,4,128,768]{3,2,1,0:T(8,128)(2,1)} %bitcast.43.wq_own.own_ref.wo_own), channel_id=1, source_target_pairs={{0,4},{4,0},{8,12},{12,8},{16,20},{20,16},{24,28},{28,24},{1,5},{5... | collective-permute-start | bytes 9437192 | tf_op jit(solution)/shard_map/ppermute | solution.py:868
  140.1 27.1 %collective-permute-start.13 = (bf16[1,1,2,128,2176]{4,3,2,1,0:T(8,128)(2,1)S(1)}, bf16[1,1,2,128,2176]{4,3,2,1,0:T(8,128)(2,1)}, u32[]{:S(2)}, u32[]{:S(2)}) collective-permute-start(bf16[1,1,2,128,2176]{4,3,2,1,0:T(8,128)(2,1)S(1)} %maximum_bitcast_fusion), channel_id=1, source_target_pairs={{0,8},{4,12},{8,0},{12,4},{16,24},{20,28},{24,16},{28,20},{1,9},{5... | collective-permute-start | bytes 3342344 | tf_op jit(solution)/shard_map/ppermute | solution.py:868
  140.6 27.1 %collective-permute-start.16 = (bf16[1,1,2,128,2176]{4,3,2,1,0:T(8,128)(2,1)}, bf16[1,1,2,128,2176]{4,3,2,1,0:T(8,128)(2,1)}, u32[]{:S(2)}, u32[]{:S(2)}) collective-permute-start(bf16[1,1,2,128,2176]{4,3,2,1,0:T(8,128)(2,1)} %maximum_bitcast_fusion.1), channel_id=1, source_target_pairs={{0,16},{4,20},{8,24},{12,28},{16,0},{20,4},{24,8},{28,12},{1,17},{... | collective-permute-start | bytes 3342344 | tf_op jit(solution)/shard_map/ppermute | solution.py:868
  170.0 54.7 %collective-permute-start.24 = (bf16[1,2,2,128,2176]{4,3,2,1,0:T(8,128)(2,1)}, bf16[1,2,2,128,2176]{4,3,2,1,0:T(8,128)(2,1)}, u32[]{:S(2)}, u32[]{:S(2)}) collective-permute-start(bf16[1,2,2,128,2176]{4,3,2,1,0:T(8,128)(2,1)} %constant_dynamic-update-slice_fusion.28), channel_id=1, source_target_pairs={{0,16},{4,20},{8,24},{12,28},{16,0},{20,4},{24,8},{28,12},{1,17},{... | collective-permute-start | bytes 6684680 | tf_op jit(solution)/shard_map/ppermute | solution.py:868
  171.9 52.8 %collective-permute-start.25 = (bf16[2,1,2,128,2176]{4,3,2,1,0:T(8,128)(2,1)S(1)}, bf16[2,1,2,128,2176]{4,3,2,1,0:T(8,128)(2,1)}, u32[]{:S(2)}, u32[]{:S(2)}) collective-permute-start(bf16[2,1,2,128,2176]{4,3,2,1,0:T(8,128)(2,1)S(1)} %constant_dynamic-update-slice_fusion.30), channel_id=1, source_target_pairs={{0,8},{4,12},{8,0},{12,4},{16,24},{20,28},{24,16},{28,20},{1,9},{5... | collective-permute-start | bytes 6684680 | tf_op jit(solution)/shard_map/ppermute | solution.py:868
  177.7 31.1 %collective-permute-start.28 = (bf16[256,1024]{1,0:T(8,128)(2,1)}, bf16[256,1024]{1,0:T(8,128)(2,1)}, u32[]{:S(2)}, u32[]{:S(2)}) collective-permute-start(bf16[256,1024]{1,0:T(8,128)(2,1)} %shard_map.347.own_ref), channel_id=1, source_target_pairs={{0,4},{4,0},{8,12},{12,8},{16,20},{20,16},{24,28},{28,24},{1,5},{5... | collective-permute-start | bytes 1572872 | tf_op jit(solution)/shard_map/ppermute | solution.py:868
  234.6 35.2 %collective-permute-start.32 = (bf16[4,2,128,2176]{3,2,1,0:T(8,128)(2,1)}, bf16[4,2,128,2176]{3,2,1,0:T(8,128)(2,1)}, u32[]{:S(2)}, u32[]{:S(2)}) collective-permute-start(bf16[4,2,128,2176]{3,2,1,0:T(8,128)(2,1)} %bitcast.62.own_ref), channel_id=1, source_target_pairs={{0,4},{4,0},{8,12},{12,8},{16,20},{20,16},{24,28},{28,24},{1,5},{5... | collective-permute-start | bytes 13369352 | tf_op jit(solution)/shard_map/ppermute | solution.py:868
  268.8 27.3 %collective-permute-start.33 = (bf16[4,2,128,2176]{3,2,1,0:T(8,128)(2,1)}, bf16[4,2,128,2176]{3,2,1,0:T(8,128)(2,1)}, u32[]{:S(2)}, u32[]{:S(2)}) collective-permute-start(bf16[4,2,128,2176]{3,2,1,0:T(8,128)(2,1)} %get-tuple-element.157), channel_id=1, source_target_pairs={{0,4},{4,0},{8,12},{12,8},{16,20},{20,16},{24,28},{28,24},{1,5},{5... | collective-permute-start | bytes 13369352 | tf_op jit(solution)/shard_map/ppermute | solution.py:868
  291.7 35.3 %collective-permute-start.36 = (bf16[4,2,128,2176]{3,2,1,0:T(8,128)(2,1)}, bf16[4,2,128,2176]{3,2,1,0:T(8,128)(2,1)}, u32[]{:S(2)}, u32[]{:S(2)}) collective-permute-start(bf16[4,2,128,2176]{3,2,1,0:T(8,128)(2,1)} %get-tuple-element.163), channel_id=1, source_target_pairs={{0,4},{4,0},{8,12},{12,8},{16,20},{20,16},{24,28},{28,24},{1,5},{5... | collective-permute-start | bytes 13369352 | tf_op jit(solution)/shard_map/ppermute | solution.py:868
  314.9 342.2 %collective-permute-start.70 = (bf16[256,1024]{1,0:T(8,128)(2,1)}, bf16[256,1024]{1,0:T(8,128)(2,1)}, u32[]{:S(2)}, u32[]{:S(2)}) collective-permute-start(bf16[256,1024]{1,0:T(8,128)(2,1)} %get-tuple-element.249), channel_id=1, source_target_pairs={{2,0},{6,1},{4,2},{0,3},{3,4},{7,5},{5,6},{1,7},{10,8},{14,9},{12,... | collective-permute-start | bytes 1572872 | tf_op jit(solution)/shard_map/ppermute | solution.py:926
  325.4 48.5 %collective-permute-start.35 = (bf16[1,2,2,128,2176]{4,3,2,1,0:T(8,128)(2,1)}, bf16[1,2,2,128,2176]{4,3,2,1,0:T(8,128)(2,1)}, u32[]{:S(2)}, u32[]{:S(2)}) collective-permute-start(bf16[1,2,2,128,2176]{4,3,2,1,0:T(8,128)(2,1)} %fusion), channel_id=1, source_target_pairs={{0,16},{4,20},{8,24},{12,28},{16,0},{20,4},{24,8},{28,12},{1,17},{... | collective-permute-start | bytes 6684680 | tf_op jit(solution)/shard_map/ppermute | solution.py:868
  331.2 71.7 %collective-permute-start.38 = (bf16[2,1,2,128,2176]{4,3,2,1,0:T(8,128)(2,1)}, bf16[2,1,2,128,2176]{4,3,2,1,0:T(8,128)(2,1)}, u32[]{:S(2)}, u32[]{:S(2)}) collective-permute-start(bf16[2,1,2,128,2176]{4,3,2,1,0:T(8,128)(2,1)} %add_convert_fusion), channel_id=1, source_target_pairs={{0,8},{4,12},{8,0},{12,4},{16,24},{20,28},{24,16},{28,20},{1,9},{5... | collective-permute-start | bytes 6684680 | tf_op jit(solution)/shard_map/ppermute | solution.py:868
  396.5 55.7 %collective-permute-start.37 = (bf16[1,1,2,128,2176]{4,3,2,1,0:T(8,128)(2,1)}, bf16[1,1,2,128,2176]{4,3,2,1,0:T(8,128)(2,1)}, u32[]{:S(2)}, u32[]{:S(2)}) collective-permute-start(bf16[1,1,2,128,2176]{4,3,2,1,0:T(8,128)(2,1)} %add_convert_fusion.4), channel_id=1, source_target_pairs={{0,8},{4,12},{8,0},{12,4},{16,24},{20,28},{24,16},{28,20},{1,9},{5... | collective-permute-start | bytes 3342344 | tf_op jit(solution)/shard_map/ppermute | solution.py:868
  409.8 42.3 %collective-permute-start.42 = (bf16[1,1,2,128,2176]{4,3,2,1,0:T(8,128)(2,1)}, bf16[1,1,2,128,2176]{4,3,2,1,0:T(8,128)(2,1)S(1)}, u32[]{:S(2)}, u32[]{:S(2)}) collective-permute-start(bf16[1,1,2,128,2176]{4,3,2,1,0:T(8,128)(2,1)} %add_convert_fusion.3), channel_id=1, source_target_pairs={{0,16},{4,20},{8,24},{12,28},{16,0},{20,4},{24,8},{28,12},{1,17},{... | collective-permute-start | bytes 3342344 | tf_op jit(solution)/shard_map/ppermute | solution.py:868
  442.8 51.4 %collective-permute-start.47 = (bf16[2,1,4,128,1024]{4,3,2,1,0:T(8,128)(2,1)}, bf16[2,1,4,128,1024]{4,3,2,1,0:T(8,128)(2,1)}, u32[]{:S(2)}, u32[]{:S(2)}) collective-permute-start(bf16[2,1,4,128,1024]{4,3,2,1,0:T(8,128)(2,1)} %add_convert_fusion.2), channel_id=1, source_target_pairs={{0,8},{4,12},{8,0},{12,4},{16,24},{20,28},{24,16},{28,20},{1,9},{5... | collective-permute-start | bytes 6291464 | tf_op jit(solution)/shard_map/ppermute | solution.py:868
  465.2 29.0 %collective-permute-start.44 = (bf16[4,4,128,512]{3,2,1,0:T(8,128)(2,1)}, bf16[4,4,128,512]{3,2,1,0:T(8,128)(2,1)S(1)}, u32[]{:S(2)}, u32[]{:S(2)}) collective-permute-start(bf16[4,4,128,512]{3,2,1,0:T(8,128)(2,1)} %get-tuple-element.190), channel_id=1, source_target_pairs={{0,4},{4,0},{8,12},{12,8},{16,20},{20,16},{24,28},{28,24},{1,5},{5... | collective-permute-start | bytes 6291464 | tf_op jit(solution)/shard_map/ppermute | solution.py:868
  467.8 26.4 %collective-permute-start.46 = (bf16[1,1,128,2176]{3,2,1,0:T(8,128)(2,1)S(1)}, bf16[1,1,128,2176]{3,2,1,0:T(8,128)(2,1)S(1)}, u32[]{:S(2)}, u32[]{:S(2)}) collective-permute-start(bf16[1,1,128,2176]{3,2,1,0:T(8,128)(2,1)S(1)} %add_convert_fusion.8), channel_id=1, source_target_pairs={{0,1},{1,0},{2,3},{3,2},{4,5},{5,4},{6,7},{7,6},{8,9},{9,8},{10,11... | collective-permute-start | bytes 1671176 | tf_op jit(solution)/shard_map/ppermute | solution.py:935
  494.5 31.3 %collective-permute-start.48 = (bf16[1,2,4,128,512]{4,3,2,1,0:T(8,128)(2,1)S(1)}, bf16[1,2,4,128,512]{4,3,2,1,0:T(8,128)(2,1)S(1)}, u32[]{:S(2)}, u32[]{:S(2)}) collective-permute-start(bf16[1,2,4,128,512]{4,3,2,1,0:T(8,128)(2,1)S(1)} %fusion.2), channel_id=1, source_target_pairs={{0,16},{4,20},{8,24},{12,28},{16,0},{20,4},{24,8},{28,12},{1,17},{... | collective-permute-start | bytes 3145736 | tf_op jit(solution)/shard_map/ppermute | solution.py:868
  497.6 44.1 %collective-permute-start.49 = (bf16[1,1,4,128,1024]{4,3,2,1,0:T(8,128)(2,1)S(1)}, bf16[1,1,4,128,1024]{4,3,2,1,0:T(8,128)(2,1)S(1)}, u32[]{:S(2)}, u32[]{:S(2)}) collective-permute-start(bf16[1,1,4,128,1024]{4,3,2,1,0:T(8,128)(2,1)S(1)} %add_convert_fusion.5), channel_id=1, source_target_pairs={{0,16},{4,20},{8,24},{12,28},{16,0},{20,4},{24,8},{28,12},{1,17},{... | collective-permute-start | bytes 3145736 | tf_op jit(solution)/shard_map/ppermute | solution.py:868
  499.6 26.2 %collective-permute-start.50 = (bf16[1,128,2176]{2,1,0:T(8,128)(2,1)S(1)}, bf16[1,128,2176]{2,1,0:T(8,128)(2,1)S(1)}, u32[]{:S(2)}, u32[]{:S(2)}) collective-permute-start(bf16[1,128,2176]{2,1,0:T(8,128)(2,1)S(1)} %fusion.4), channel_id=1, source_target_pairs={{0,2},{1,3},{2,0},{3,1},{4,6},{5,7},{6,4},{7,5},{8,10},{9,11},{10,... | collective-permute-start | bytes 1671176 | tf_op jit(solution)/shard_map/ppermute | solution.py:935
  566.7 24.4 %collective-permute-start.58 = (bf16[1,2,128,2176]{3,2,1,0:T(8,128)(2,1)S(1)}, bf16[1,2,128,2176]{3,2,1,0:T(8,128)(2,1)S(1)}, u32[]{:S(2)}, u32[]{:S(2)}) collective-permute-start(bf16[1,2,128,2176]{3,2,1,0:T(8,128)(2,1)S(1)} %pad_maximum_fusion.11), channel_id=1, source_target_pairs={{0,16},{4,20},{8,24},{12,28},{16,0},{20,4},{24,8},{28,12},{1,17},{... | collective-permute-start | bytes 3342344 | tf_op jit(solution)/shard_map/ppermute | solution.py:868
  602.2 55.7 %collective-permute-start.34 = (bf16[256,1024]{1,0:T(8,128)(2,1)}, bf16[256,1024]{1,0:T(8,128)(2,1)S(1)}, u32[]{:S(2)}, u32[]{:S(2)}) collective-permute-start(bf16[256,1024]{1,0:T(8,128)(2,1)} %get-tuple-element.248), channel_id=1, source_target_pairs={{0,0},{4,1},{6,2},{2,3},{1,4},{5,5},{7,6},{3,7},{8,8},{12,9},{14,1... | collective-permute-start | bytes 1572872 | tf_op jit(solution)/shard_map/ppermute | solution.py:926
  618.9 39.0 %collective-permute-start.72 = (bf16[256,1024]{1,0:T(8,128)(2,1)}, bf16[256,1024]{1,0:T(8,128)(2,1)}, u32[]{:S(2)}, u32[]{:S(2)}) collective-permute-start(bf16[256,1024]{1,0:T(8,128)(2,1)} %get-tuple-element.247), channel_id=1, source_target_pairs={{2,0},{6,1},{4,2},{0,3},{3,4},{7,5},{5,6},{1,7},{10,8},{14,9},{12,... | collective-permute-start | bytes 1572872 | tf_op jit(solution)/shard_map/ppermute | solution.py:926
  631.0 26.9 %collective-permute-start.71 = (bf16[256,1024]{1,0:T(8,128)(2,1)}, bf16[256,1024]{1,0:T(8,128)(2,1)}, u32[]{:S(2)}, u32[]{:S(2)}) collective-permute-start(bf16[256,1024]{1,0:T(8,128)(2,1)} %get-tuple-element.246), channel_id=1, source_target_pairs={{0,0},{4,1},{6,2},{2,3},{1,4},{5,5},{7,6},{3,7},{8,8},{12,9},{14,1... | collective-permute-start | bytes 1572872 | tf_op jit(solution)/shard_map/ppermute | solution.py:926
  (96 other events, 1244.8 us)

commit v3 on v2

--- a/solution.py
+++ b/solution.py
@@ -1164,13 +1164,12 @@
         dq_two, dkv_two, dkv_two_send = cross_attention_back(
             q_two, ga_two, lse_two, kv_two, kv_two_oth, enc_kseg, qseg
         )
-        (dq_two,) = land([near_g], dq_two)
         (grad_own, grad_oth, out_own, out_oth, cot_one, round_one, grad_gain_two, memory_grad, ga_one) = cross_post(
             dq_two, dkv_two, swap(dkv_two_send, 1), n_two, encoder, round_two, att_two, stream_one,
             cot_two, gain_two, cross_own, cross_oth, self_own, self_oth, att_one, qcols,
         )
         cross_g = Chain(whole_chain([(grad_own, grad_oth), (out_own, out_oth)], up))
-        (ga_one,) = land([far_g, cross_g], ga_one)
+        (ga_one,) = land([near_g, far_g, cross_g], ga_one)
         dq_one, dkv_one, dkv_one_send, folded = self_attention_back(
             ids, q_one, ga_one, lse_one, kv_one, kv_one_oth, slabs, kseg, qseg
         )
@@ -1179,7 +1178,7 @@
             dq_one, dkv_one, swap(dkv_one_send, 1), n_one, stream, cot_one,
             gain_one, self_own, self_oth, qcols,
         )
-        self_g = Chain(whole_chain([(grad_own, grad_oth)], down))
+        self_g = Chain(whole_chain([(grad_own, grad_oth)], up))
         tokens_back = send_back(tokens_grad)
 
         padded = jnp.pad(folded, ((0, 0), (0, 0), (0, 8)))
@@ -1193,23 +1192,33 @@
             lax.dynamic_index_in_dim(bucket_grad, z ^ p, 1, keepdims=False) for p in range(shards)
         ]
         small = jnp.concatenate(small + [g.reshape(-1) for g in bucket_grad])
+        position = place_of(me ^ jnp.arange(batch)).astype(jnp.int32)
         small_g = Chain(summing(small))
-        land([self_g, near_g, far_g, cross_g])
+        land([self_g])
+        land([near_g, far_g, cross_g])
         while near_g.pending or far_g.pending:
-            land([self_g, near_g, far_g, cross_g])
+            land([near_g, far_g])
         ffn_g = Chain(ffn_chain(near_g.result, far_g.result))
         memory_back = send_back(after(memory_grad, *self_g.pending))
         chains = [self_g, cross_g, ffn_g, small_g]
+        land(chains)
+        while ffn_g.pending:
+            land(chains)
+        ffn_final = land(chains, *unpack_ffn(position, ffn_g.result, ff))
+        while cross_g.pending:
+            land(chains)
+        *cross_final, self_out_grad = unpack_layer(position, cross_g.result, qcols, 2)
+        *cross_final, self_out_grad = land(chains, *cross_final, self_out_grad)
         while any(c.pending for c in chains):
             land(chains)
-        position = place_of(me ^ jnp.arange(batch)).astype(jnp.int32)
-        ffn_final = unpack_ffn(position, ffn_g.result, ff)
-        *cross_final, self_out_grad = unpack_layer(position, cross_g.result, qcols, 2)
         self_final = (*unpack_layer(position, self_g.result, qcols, 0), self_out_grad)
         late = self_g.result
-        block_out = as_micros([after(part, late) for part in block_back])
-        memory_grad = as_micros([after(part, late) for part in memory_back]).astype(F32)
-        tokens_grad = as_micros([after(part, late) for part in tokens_back]).astype(F32)
+        block_back = [after(part, late) for part in block_back]
+        memory_back = [after(part, late) for part in memory_back]
+        tokens_back = [after(part, late) for part in tokens_back]
+        block_out = as_micros(block_back)
+        memory_grad = as_micros(memory_back).astype(F32)
+        tokens_grad = as_micros(tokens_back).astype(F32)
 
         small = small_g.result
         gains = [small[i * width : (i + 1) * width] for i in range(3)]

time: 683 us -> 643 us (0.941)
  waiting for transfers between devices: 216 us -> 165 us
  starting transfers between devices: 95.7 us -> 103 us
    ppermute x42, waiting for transfers between devices: 106 us -> 56.1 us  [swap(): return lax.ppermute(array, 'batch', [(b, b ^ mask) for b in range(batch)])]
    ppermute x21, starting transfers between devices: 29.2 us -> 36.9 us  [swap_z(): return lax.ppermute(array, 'group', [(z, z ^ mask) for z in range(shards)])]
    unnamed x200 -> x214, local copies, waits for them, and re-layouts: 22.7 us -> 23.5 us
  transfers between devices with their start and end apart: 75 -> 75, of which waited for: 29 -> 29; matrix products, arithmetic and copies ran while one was open for 15% -> 16% of each run, Pallas kernels for 36% -> 38%
where the time goes in v3:
time: 643 us; the launch traced here: 633 us
  Pallas kernels  242 us (38%)
  waiting for transfers between devices  165 us (26%)
  starting transfers between devices  103 us (16%)
  other arithmetic  63.2 us (10%)
  local copies, waits for them, and re-layouts  57.9 us (9%)
    ppermute x21, waiting for transfers between devices, swap_z(): return lax.ppermute(array, 'group', [(z, z ^ mask) for z in range(shards)])  86.6 us
    ppermute x42, waiting for transfers between devices, swap(): return lax.ppermute(array, 'batch', [(b, b ^ mask) for b in range(batch)])  56.1 us
    pallas_call x2, Pallas kernels, feed_forward(): call(functools.partial(ffn_kernel, ff), (shape(rows, width, dtype=F32), s...  44 us
    ppermute x21, starting transfers between devices, swap_z(): return lax.ppermute(array, 'group', [(z, z ^ mask) for z in range(shards)])  36.9 us
    ppermute x42, starting transfers between devices, swap(): return lax.ppermute(array, 'batch', [(b, b ^ mask) for b in range(batch)])  36.4 us
    pallas_call x1, Pallas kernels, self_attention_back(): call(self_back_kernel, (shape(*q.shape), shape(*own.shape, dtype=F32), sh...  32.2 us
    unnamed x214, local copies, waits for them, and re-layouts  23.5 us
    pallas_call x3, Pallas kernels, unpacked(): call(kernel, tuple(outs), (count,), [pl.BlockSpec((1, blk, packed), lambd...  21.9 us
  transfers between devices with their start and end apart: 75, of which 29 were waited for; matrix products, arithmetic and copies ran while one was open for 16% of the time, Pallas kernels for 38%

profile of v3, /device:TPU:0, one launch (start us, length us, event | category | flops | bytes accessed | tf_op | source)
XLA Modules:
  0.0 633.4 jit_solution(5700448957763812168)
XLA Ops:
  25.2 11.2 %shard_map.344.slab_ref = f32[16,128,1152]{2,1,0:T(8,128)} custom-call(f32[16,1,1152]{2,1,0:T(1,128)} %reshape.454.base_ref), custom_call_target="tpu_custom_call" | custom-call | flops 11000000512 | bytes 33000000 | tf_op jit(solution)/shard_map/pallas_call | solution.py:339
  43.6 5.4 collective-permute-start.2
  49.0 9.5 %collective-permute-done.6 = bf16[1,1,4,128,768]{4,3,2,1,0:T(8,128)(2,1)S(1)} collective-permute-done((bf16[1,1,4,128,768]{4,3,2,1,0:T(8,128)(2,1)S(1)}, bf16[1,1,4,128,768]{4,3,2,1,0:T(8,128)(2,1)S(1)}, u32[]{:S(2)}, u32[]{:S(2)}) %collective-permute-start.6) | collective-permute-done | bytes 786464 | tf_op jit(solution)/shard_map/ppermute | solution.py:868
  71.8 24.1 %collective-permute-done.14 = bf16[128,2176]{1,0:T(8,128)(2,1)S(1)} collective-permute-done((bf16[128,2176]{1,0:T(8,128)(2,1)S(1)}, bf16[128,2176]{1,0:T(8,128)(2,1)S(1)}, u32[]{:S(2)}, u32[]{:S(2)}) %collective-permute-start.14) | collective-permute-done | bytes 557088 | tf_op jit(solution)/shard_map/ppermute | solution.py:935
  101.3 7.7 %collective-permute-done.27 = bf16[128,1024]{1,0:T(8,128)(2,1)S(1)} collective-permute-done((bf16[128,1024]{1,0:T(8,128)(2,1)S(1)}, bf16[128,1024]{1,0:T(8,128)(2,1)S(1)}, u32[]{:S(2)}, u32[]{:S(2)}) %collective-permute-start.27) | collective-permute-done | bytes 262176 | tf_op jit(solution)/shard_map/ppermute | solution.py:919
  109.8 5.4 collective-permute-start.30
  118.1 6.1 collective-permute-done.15
  127.3 6.9 %collective-permute-start.23 = (bf16[4,4,128,768]{3,2,1,0:T(8,128)(2,1)}, bf16[4,4,128,768]{3,2,1,0:T(8,128)(2,1)}, u32[]{:S(2)}, u32[]{:S(2)}) collective-permute-start(bf16[4,4,128,768]{3,2,1,0:T(8,128)(2,1)} %bitcast.43.wq_own.own_ref.wo_own), channel_id=1, source_target_pairs={{0,4},{4,0},{8,12},{12,8},{16,20},{20,16},{24,28},{28,24},{1,5},{5... | collective-permute-start | bytes 9437192 | tf_op jit(solution)/shard_map/ppermute | solution.py:868
  143.1 6.4 %shard_map.343 = (bf16[512,1024]{1,0:T(8,128)(2,1)}, bf16[512,1024]{1,0:T(8,128)(2,1)}, bf16[512,1024]{1,0:T(8,128)(2,1)}) custom-call(bf16[512,1024]{1,0:T(8,128)(2,1)} %copy-done.40, f32[1,1024]{1,0:T(1,128)} %copy-done.52, bf16[4,4,128,768]{3,2,1,0:T(8,128)(2,1)} %bitcast.241, bf16[4,4,128,768]{3,2,1,0:T(8,128)(2,1)} %collective-permute-done.17.oth_ref.wo_oth), custom_call_target="tpu_custom_call" | custom-call | flops 7000000000 | bytes 21000000 | tf_op jit(solution)/shard_map/pallas_call | solution.py:111
  149.5 17.7 %collective-permute-done.13 = bf16[1,1,2,128,2176]{4,3,2,1,0:T(8,128)(2,1)} collective-permute-done((bf16[1,1,2,128,2176]{4,3,2,1,0:T(8,128)(2,1)S(1)}, bf16[1,1,2,128,2176]{4,3,2,1,0:T(8,128)(2,1)}, u32[]{:S(2)}, u32[]{:S(2)}) %collective-permute-start.13) | collective-permute-done | bytes 1114144 | tf_op jit(solution)/shard_map/ppermute | solution.py:868
  178.7 20.3 %shard_map.345 = (bf16[512,1024]{1,0:T(8,128)(2,1)}, f32[16,1,512]{2,1,0:T(1,128)}) custom-call(s32[4]{0:T(128)} %pad_add_fusion.2.ids_ref, bf16[512,1024]{1,0:T(8,128)(2,1)} %get-tuple-element.144.q_ref, bf16[512,1024]{1,0:T(8,128)(2,1)} %get-tuple-element.145.own_ref, bf16[512,1024]{1,0:T(8,128)(2,1)} %copy-done.53, f32[16,128,1152]{2,1,0:T(8,128)} %shard_map.344.slab_ref, ...), custom_call_target="tpu_custom_call" | custom-call | flops 20000000000 | bytes 60000000 | tf_op jit(solution)/shard_map/pallas_call | solution.py:446
  199.0 9.8 %shard_map.346 = (f32[512,1024]{1,0:T(8,128)}, bf16[512,1024]{1,0:T(8,128)(2,1)}, bf16[512,1024]{1,0:T(8,128)(2,1)}) custom-call(bf16[512,1024]{1,0:T(8,128)(2,1)} %copy-done.40, bf16[512,1024]{1,0:T(8,128)(2,1)} %get-tuple-element.146.att_ref.att_one_ref, f32[1,1024]{1,0:T(1,128)} %copy-done.51, bf16[4,4,128,768]{3,2,1,0:T(8,128)(2,1)} %bitcast.242, ...), custom_call_target="tpu_custom_call" | custom-call | flops 10000000000 | bytes 30000000 | tf_op jit(solution)/shard_map/pallas_call | solution.py:172
  208.8 16.0 %shard_map.348 = (bf16[512,1024]{1,0:T(8,128)(2,1)}, f32[16,1,512]{2,1,0:T(1,128)}) custom-call(bf16[512,1024]{1,0:T(8,128)(2,1)} %get-tuple-element.150.q_ref, bf16[256,1024]{1,0:T(8,128)(2,1)} %shard_map.347.own_ref, bf16[256,1024]{1,0:T(8,128)(2,1)} %collective-permute-done.28.oth_ref, s32[512,1]{1,0:T(8,128)} %copy.44.kseg_ref, ...), custom_call_target="tpu_custom_call" | custom-call | flops 16000000000 | bytes 48000000 | tf_op jit(solution)/shard_map/pallas_call | solution.py:468
  236.0 6.9 %shard_map.349 = (f32[512,1024]{1,0:T(8,128)}, bf16[512,1024]{1,0:T(8,128)(2,1)}) custom-call(f32[512,1024]{1,0:T(8,128)} %get-tuple-element.147.x_ref.s_ref, bf16[512,1024]{1,0:T(8,128)(2,1)} %get-tuple-element.153.att_ref, f32[1,1024]{1,0:T(1,128)} %copy-done.59, bf16[4,4,128,768]{3,2,1,0:T(8,128)(2,1)} %bitcast.43.wq_own.own_ref.wo_own, ...), custom_call_target="tpu_custom_call" | custom-call | flops 7000000000 | bytes 21000000 | tf_op jit(solution)/shard_map/pallas_call | solution.py:214
  242.9 22.0 %shard_map.350 = (f32[512,1024]{1,0:T(8,128)}, f32[512,1024]{1,0:T(8,128)}, bf16[4,2,128,2176]{3,2,1,0:T(8,128)(2,1)}, bf16[4,2,128,2176]{3,2,1,0:T(8,128)(2,1)}) custom-call(bf16[512,1024]{1,0:T(8,128)(2,1)} %get-tuple-element.160.n_ref, bf16[512,1024]{1,0:T(8,128)(2,1)} %copy-done.39, bf16[4,2,128,2176]{3,2,1,0:T(8,128)(2,1)} %bitcast.61.own_ref, ...), custom_call_target="tpu_custom_call" | custom-call | flops 22000001024 | bytes 66000000 | tf_op jit(solution)/shard_map/pallas_call | solution.py:270
  265.2 22.0 %shard_map.351 = (f32[512,1024]{1,0:T(8,128)}, f32[512,1024]{1,0:T(8,128)}, bf16[4,2,128,2176]{3,2,1,0:T(8,128)(2,1)}, bf16[4,2,128,2176]{3,2,1,0:T(8,128)(2,1)}) custom-call(bf16[512,1024]{1,0:T(8,128)(2,1)} %get-tuple-element.160.n_ref, bf16[512,1024]{1,0:T(8,128)(2,1)} %copy-done.39, bf16[4,2,128,2176]{3,2,1,0:T(8,128)(2,1)} %bitcast.62.own_ref, ...), custom_call_target="tpu_custom_call" | custom-call | flops 22000001024 | bytes 66000000 | tf_op jit(solution)/shard_map/pallas_call | solution.py:270
  297.9 10.3 %shard_map.352 = (bf16[512,1024]{1,0:T(8,128)(2,1)}, f32[512,1024]{1,0:T(8,128)}, bf16[512,1024]{1,0:T(8,128)(2,1)}, f32[1,1024]{1,0:T(1,128)}, bf16[512,1024]{1,0:T(8,128)(2,1)}) custom-call(f32[512,1024]{1,0:T(8,128)} %get-tuple-element.154.s_ref, f32[512,1024]{1,0:T(8,128)} %get-tuple-element.159.ya_ref, f32[512,1024]{1,0:T(8,128)} %get-tuple-element.162.yb_ref, ...), custom_call_target="tpu_custom_call" | custom-call | flops 10000000000 | bytes 30000000 | tf_op jit(solution)/shard_map/pallas_call | solution.py:311
  312.9 21.7 %shard_map.353 = (bf16[512,1024]{1,0:T(8,128)(2,1)}, f32[256,1024]{1,0:T(8,128)}, bf16[256,1024]{1,0:T(8,128)(2,1)}) custom-call(bf16[512,1024]{1,0:T(8,128)(2,1)} %get-tuple-element.150.q_ref, bf16[512,1024]{1,0:T(8,128)(2,1)} %get-tuple-element.174.ga_ref, f32[16,1,512]{2,1,0:T(1,128)} %get-tuple-element.175.lse_ref, ...), custom_call_target="tpu_custom_call" | custom-call | flops 20999999488 | bytes 63000000 | tf_op jit(solution)/shard_map/pallas_call | solution.py:605
  343.5 19.3 %shard_map.354 = (bf16[4,4,128,768]{3,2,1,0:T(8,128)(2,1)}, bf16[4,4,128,768]{3,2,1,0:T(8,128)(2,1)}, bf16[4,4,128,256]{3,2,1,0:T(8,128)(2,1)}, bf16[4,4,128,256...) custom-call(bf16[512,1024]{1,0:T(8,128)(2,1)} %get-tuple-element.176, ...), custom_call_target="tpu_custom_call" | custom-call | flops 17999998976 | bytes 54000000 | tf_op jit(solution)/shard_map/pallas_call | solution.py:684
  385.2 32.2 %shard_map.355 = (bf16[512,1024]{1,0:T(8,128)(2,1)}, f32[512,1024]{1,0:T(8,128)}, bf16[512,1024]{1,0:T(8,128)(2,1)}, f32[16,8,1152]{2,1,0:T(8,128)}) custom-call(s32[4]{0:T(128)} %pad_add_fusion.2.ids_ref, bf16[512,1024]{1,0:T(8,128)(2,1)} %get-tuple-element.144.q_ref, bf16[512,1024]{1,0:T(8,128)(2,1)} %get-tuple-element.187.ga_ref, ...), custom_call_target="tpu_custom_call" | custom-call | flops 32000000000 | bytes 96000000 | tf_op jit(solution)/shard_map/pallas_call | solution.py:555
  428.1 12.0 %shard_map.356 = (bf16[4,4,128,512]{3,2,1,0:T(8,128)(2,1)}, bf16[4,4,128,512]{3,2,1,0:T(8,128)(2,1)}, bf16[512,1024]{1,0:T(8,128)(2,1)}, f32[1,1024]{1,0:T(1,128)}) custom-call(bf16[512,1024]{1,0:T(8,128)(2,1)} %get-tuple-element.190.dq_ref, f32[512,1024]{1,0:T(8,128)} %get-tuple-element.191.dko_ref, bf16[512,1024]{1,0:T(8,128)(2,1)} %collective-permute-done.43.dkr_ref, ...), custom_call_target="tpu_custom_call" | custom-call | flops 14000000000 | bytes 42000000 | tf_op jit(solution)/shard_map/pallas_call | solution.py:755
  445.7 11.9 %collective-permute-done.46 = bf16[1,1,128,2176]{3,2,1,0:T(8,128)(2,1)S(1)} collective-permute-done((bf16[1,1,128,2176]{3,2,1,0:T(8,128)(2,1)S(1)}, bf16[1,1,128,2176]{3,2,1,0:T(8,128)(2,1)S(1)}, u32[]{:S(2)}, u32[]{:S(2)}) %collective-permute-start.46) | collective-permute-done | bytes 557088 | tf_op jit(solution)/shard_map/ppermute | solution.py:935
  457.6 11.4 %collective-permute-done.47 = bf16[1,1,128,2176]{3,2,1,0:T(8,128)(2,1)S(1)} collective-permute-done((bf16[1,1,128,2176]{3,2,1,0:T(8,128)(2,1)S(1)}, bf16[1,1,128,2176]{3,2,1,0:T(8,128)(2,1)S(1)}, u32[]{:S(2)}, u32[]{:S(2)}) %collective-permute-start.47) | collective-permute-done | bytes 557088 | tf_op jit(solution)/shard_map/ppermute | solution.py:935
  492.1 12.3 %collective-permute-done.50 = bf16[1,128,2176]{2,1,0:T(8,128)(2,1)S(1)} collective-permute-done((bf16[1,128,2176]{2,1,0:T(8,128)(2,1)S(1)}, bf16[1,128,2176]{2,1,0:T(8,128)(2,1)S(1)}, u32[]{:S(2)}, u32[]{:S(2)}) %collective-permute-start.50) | collective-permute-done | bytes 557088 | tf_op jit(solution)/shard_map/ppermute | solution.py:935
  512.4 5.4 collective-permute-done.55
  536.2 11.0 %collective-permute-done.58 = bf16[1,2,128,2176]{3,2,1,0:T(8,128)(2,1)S(1)} collective-permute-done((bf16[1,2,128,2176]{3,2,1,0:T(8,128)(2,1)S(1)}, bf16[1,2,128,2176]{3,2,1,0:T(8,128)(2,1)S(1)}, u32[]{:S(2)}, u32[]{:S(2)}) %collective-permute-start.58) | collective-permute-done | bytes 1114144 | tf_op jit(solution)/shard_map/ppermute | solution.py:868
  557.3 5.4 collective-permute-start.34
  572.1 8.8 %shard_map.357 = (f32[704,1024]{1,0:T(8,128)}, f32[704,1024]{1,0:T(8,128)}, f32[704,1024]{1,0:T(8,128)}) custom-call(s32[8]{0:T(128)} %multiply_or_fusion.pos_ref, bf16[8,128,2176]{2,1,0:T(8,128)(2,1)} %pad_maximum_fusion.2.x_ref), custom_call_target="tpu_custom_call" | custom-call | flops 5000000000 | bytes 15000000 | tf_op jit(solution)/shard_map/pallas_call | solution.py:837
  587.2 5.7 collective-permute-done.67
  592.9 5.4 collective-permute-start.71
  602.0 6.9 %shard_map.358 = (f32[1024,256]{1,0:T(8,128)}, f32[1024,128]{1,0:T(8,128)}, f32[1024,128]{1,0:T(8,128)}, f32[256,1024]{1,0:T(8,128)}, f32[256,1024]{1,0:T(8,128)}) custom-call(s32[8]{0:T(128)} %multiply_or_fusion.pos_ref, bf16[8,128,1024]{2,1,0:T(8,128)(2,1)} %pad_maximum_fusion.8.x_ref), custom_call_target="tpu_custom_call" | custom-call | flops 5000000000 | bytes 15000000 | tf_op jit(solution)/shard_map/pallas_call | solution.py:837
  620.2 6.2 shard_map.359
  (478 shorter events, 248.1 us)
Async XLA Ops:
  6.5 29.9 %collective-permute-start.4 = (bf16[128,768]{1,0:T(8,128)(2,1)}, bf16[128,768]{1,0:T(8,128)(2,1)S(1)}, u32[]{:S(2)}, u32[]{:S(2)}) collective-permute-start(bf16[128,768]{1,0:T(8,128)(2,1)} %shard_map.340), channel_id=1, source_target_pairs={{0,1},{1,0},{2,3},{3,2},{4,5},{5,4},{6,7},{7,6},{8,9},{9,8},{10,11... | collective-permute-start | bytes 589832 | tf_op jit(solution)/shard_map/ppermute | solution.py:935
  43.6 22.4 %collective-permute-start.2 = (bf16[256,1024]{1,0:T(8,128)(2,1)}, bf16[256,1024]{1,0:T(8,128)(2,1)}, u32[]{:S(2)}, u32[]{:S(2)}) collective-permute-start(bf16[256,1024]{1,0:T(8,128)(2,1)} %get-tuple-element.267), channel_id=1, source_target_pairs={{0,0},{1,4},{2,6},{3,2},{4,1},{5,5},{6,7},{7,3},{8,8},{9,12},{10,1... | collective-permute-start | bytes 1572872 | tf_op jit(solution)/shard_map/ppermute | solution.py:919
  60.1 35.8 %collective-permute-start.14 = (bf16[128,2176]{1,0:T(8,128)(2,1)S(1)}, bf16[128,2176]{1,0:T(8,128)(2,1)S(1)}, u32[]{:S(2)}, u32[]{:S(2)}) collective-permute-start(bf16[128,2176]{1,0:T(8,128)(2,1)S(1)} %copy-done.27), channel_id=1, source_target_pairs={{0,2},{1,3},{2,0},{3,1},{4,6},{5,7},{6,4},{7,5},{8,10},{9,11},{10,... | collective-permute-start | bytes 1671176 | tf_op jit(solution)/shard_map/ppermute | solution.py:935
  60.5 37.6 %collective-permute-start.10 = (bf16[128,2176]{1,0:T(8,128)(2,1)S(1)}, bf16[128,2176]{1,0:T(8,128)(2,1)}, u32[]{:S(2)}, u32[]{:S(2)}) collective-permute-start(bf16[128,2176]{1,0:T(8,128)(2,1)S(1)} %copy-done.27), channel_id=1, source_target_pairs={{0,1},{1,0},{2,3},{3,2},{4,5},{5,4},{6,7},{7,6},{8,9},{9,8},{10,11... | collective-permute-start | bytes 1671176 | tf_op jit(solution)/shard_map/ppermute | solution.py:935
  62.0 53.2 %collective-permute-start.11 = (bf16[1,2,4,128,768]{4,3,2,1,0:T(8,128)(2,1)}, bf16[1,2,4,128,768]{4,3,2,1,0:T(8,128)(2,1)}, u32[]{:S(2)}, u32[]{:S(2)}) collective-permute-start(bf16[1,2,4,128,768]{4,3,2,1,0:T(8,128)(2,1)} %pad_maximum_fusion.9), channel_id=1, source_target_pairs={{0,16},{4,20},{8,24},{12,28},{16,0},{20,4},{24,8},{28,12},{1,17},{... | collective-permute-start | bytes 4718600 | tf_op jit(solution)/shard_map/ppermute | solution.py:868
  71.2 54.1 %collective-permute-start.12 = (bf16[2,1,4,128,768]{4,3,2,1,0:T(8,128)(2,1)S(1)}, bf16[2,1,4,128,768]{4,3,2,1,0:T(8,128)(2,1)S(1)}, u32[]{:S(2)}, u32[]{:S(2)}) collective-permute-start(bf16[2,1,4,128,768]{4,3,2,1,0:T(8,128)(2,1)S(1)} %pad_maximum_fusion.10), channel_id=1, source_target_pairs={{0,8},{4,12},{8,0},{12,4},{16,24},{20,28},{24,16},{28,20},{1,9},{5... | collective-permute-start | bytes 4718600 | tf_op jit(solution)/shard_map/ppermute | solution.py:868
  99.4 24.8 %collective-permute-start.15 = (bf16[128,2176]{1,0:T(8,128)(2,1)S(1)}, bf16[128,2176]{1,0:T(8,128)(2,1)S(1)}, u32[]{:S(2)}, u32[]{:S(2)}) collective-permute-start(bf16[128,2176]{1,0:T(8,128)(2,1)S(1)} %copy-done.30), channel_id=1, source_target_pairs={{0,1},{1,0},{2,3},{3,2},{4,5},{5,4},{6,7},{7,6},{8,9},{9,8},{10,11... | collective-permute-start | bytes 1671176 | tf_op jit(solution)/shard_map/ppermute | solution.py:935
  109.8 28.1 %collective-permute-start.30 = (bf16[256,1024]{1,0:T(8,128)(2,1)S(1)}, bf16[256,1024]{1,0:T(8,128)(2,1)S(1)}, u32[]{:S(2)}, u32[]{:S(2)}) collective-permute-start(bf16[256,1024]{1,0:T(8,128)(2,1)S(1)} %get-tuple-element.264), channel_id=1, source_target_pairs={{0,2},{1,6},{2,4},{3,0},{4,3},{5,7},{6,5},{7,1},{8,10},{9,14},{10,... | collective-permute-start | bytes 1572872 | tf_op jit(solution)/shard_map/ppermute | solution.py:919
  117.0 26.1 %collective-permute-start.17 = (bf16[4,4,128,768]{3,2,1,0:T(8,128)(2,1)S(1)}, bf16[4,4,128,768]{3,2,1,0:T(8,128)(2,1)}, u32[]{:S(2)}, u32[]{:S(2)}) collective-permute-start(bf16[4,4,128,768]{3,2,1,0:T(8,128)(2,1)S(1)} %bitcast.240), channel_id=1, source_target_pairs={{0,4},{4,0},{8,12},{12,8},{16,20},{20,16},{24,28},{28,24},{1,5},{5... | collective-permute-start | bytes 9437192 | tf_op jit(solution)/shard_map/ppermute | solution.py:868
  127.3 46.2 %collective-permute-start.23 = (bf16[4,4,128,768]{3,2,1,0:T(8,128)(2,1)}, bf16[4,4,128,768]{3,2,1,0:T(8,128)(2,1)}, u32[]{:S(2)}, u32[]{:S(2)}) collective-permute-start(bf16[4,4,128,768]{3,2,1,0:T(8,128)(2,1)} %bitcast.43.wq_own.own_ref.wo_own), channel_id=1, source_target_pairs={{0,4},{4,0},{8,12},{12,8},{16,20},{20,16},{24,28},{28,24},{1,5},{5... | collective-permute-start | bytes 9437192 | tf_op jit(solution)/shard_map/ppermute | solution.py:868
  140.1 27.1 %collective-permute-start.13 = (bf16[1,1,2,128,2176]{4,3,2,1,0:T(8,128)(2,1)S(1)}, bf16[1,1,2,128,2176]{4,3,2,1,0:T(8,128)(2,1)}, u32[]{:S(2)}, u32[]{:S(2)}) collective-permute-start(bf16[1,1,2,128,2176]{4,3,2,1,0:T(8,128)(2,1)S(1)} %maximum_bitcast_fusion), channel_id=1, source_target_pairs={{0,8},{4,12},{8,0},{12,4},{16,24},{20,28},{24,16},{28,20},{1,9},{5... | collective-permute-start | bytes 3342344 | tf_op jit(solution)/shard_map/ppermute | solution.py:868
  140.7 27.1 %collective-permute-start.16 = (bf16[1,1,2,128,2176]{4,3,2,1,0:T(8,128)(2,1)}, bf16[1,1,2,128,2176]{4,3,2,1,0:T(8,128)(2,1)}, u32[]{:S(2)}, u32[]{:S(2)}) collective-permute-start(bf16[1,1,2,128,2176]{4,3,2,1,0:T(8,128)(2,1)} %maximum_bitcast_fusion.1), channel_id=1, source_target_pairs={{0,16},{4,20},{8,24},{12,28},{16,0},{20,4},{24,8},{28,12},{1,17},{... | collective-permute-start | bytes 3342344 | tf_op jit(solution)/shard_map/ppermute | solution.py:868
  170.0 54.8 %collective-permute-start.24 = (bf16[1,2,2,128,2176]{4,3,2,1,0:T(8,128)(2,1)}, bf16[1,2,2,128,2176]{4,3,2,1,0:T(8,128)(2,1)}, u32[]{:S(2)}, u32[]{:S(2)}) collective-permute-start(bf16[1,2,2,128,2176]{4,3,2,1,0:T(8,128)(2,1)} %constant_dynamic-update-slice_fusion.28), channel_id=1, source_target_pairs={{0,16},{4,20},{8,24},{12,28},{16,0},{20,4},{24,8},{28,12},{1,17},{... | collective-permute-start | bytes 6684680 | tf_op jit(solution)/shard_map/ppermute | solution.py:868
  171.9 52.9 %collective-permute-start.25 = (bf16[2,1,2,128,2176]{4,3,2,1,0:T(8,128)(2,1)S(1)}, bf16[2,1,2,128,2176]{4,3,2,1,0:T(8,128)(2,1)}, u32[]{:S(2)}, u32[]{:S(2)}) collective-permute-start(bf16[2,1,2,128,2176]{4,3,2,1,0:T(8,128)(2,1)S(1)} %constant_dynamic-update-slice_fusion.30), channel_id=1, source_target_pairs={{0,8},{4,12},{8,0},{12,4},{16,24},{20,28},{24,16},{28,20},{1,9},{5... | collective-permute-start | bytes 6684680 | tf_op jit(solution)/shard_map/ppermute | solution.py:868
  177.7 31.1 %collective-permute-start.28 = (bf16[256,1024]{1,0:T(8,128)(2,1)}, bf16[256,1024]{1,0:T(8,128)(2,1)}, u32[]{:S(2)}, u32[]{:S(2)}) collective-permute-start(bf16[256,1024]{1,0:T(8,128)(2,1)} %shard_map.347.own_ref), channel_id=1, source_target_pairs={{0,4},{4,0},{8,12},{12,8},{16,20},{20,16},{24,28},{28,24},{1,5},{5... | collective-permute-start | bytes 1572872 | tf_op jit(solution)/shard_map/ppermute | solution.py:868
  234.6 30.6 %collective-permute-start.32 = (bf16[4,2,128,2176]{3,2,1,0:T(8,128)(2,1)}, bf16[4,2,128,2176]{3,2,1,0:T(8,128)(2,1)}, u32[]{:S(2)}, u32[]{:S(2)}) collective-permute-start(bf16[4,2,128,2176]{3,2,1,0:T(8,128)(2,1)} %bitcast.62.own_ref), channel_id=1, source_target_pairs={{0,4},{4,0},{8,12},{12,8},{16,20},{20,16},{24,28},{28,24},{1,5},{5... | collective-permute-start | bytes 13369352 | tf_op jit(solution)/shard_map/ppermute | solution.py:868
  264.9 28.0 %collective-permute-start.33 = (bf16[4,2,128,2176]{3,2,1,0:T(8,128)(2,1)}, bf16[4,2,128,2176]{3,2,1,0:T(8,128)(2,1)}, u32[]{:S(2)}, u32[]{:S(2)}) collective-permute-start(bf16[4,2,128,2176]{3,2,1,0:T(8,128)(2,1)} %get-tuple-element.164), channel_id=1, source_target_pairs={{0,4},{4,0},{8,12},{12,8},{16,20},{20,16},{24,28},{28,24},{1,5},{5... | collective-permute-start | bytes 13369352 | tf_op jit(solution)/shard_map/ppermute | solution.py:868
  296.4 77.7 %collective-permute-start.35 = (bf16[1,2,2,128,2176]{4,3,2,1,0:T(8,128)(2,1)}, bf16[1,2,2,128,2176]{4,3,2,1,0:T(8,128)(2,1)}, u32[]{:S(2)}, u32[]{:S(2)}) collective-permute-start(bf16[1,2,2,128,2176]{4,3,2,1,0:T(8,128)(2,1)} %fusion), channel_id=1, source_target_pairs={{0,16},{4,20},{8,24},{12,28},{16,0},{20,4},{24,8},{28,12},{1,17},{... | collective-permute-start | bytes 6684680 | tf_op jit(solution)/shard_map/ppermute | solution.py:868
  312.4 61.7 %collective-permute-start.37 = (bf16[2,1,2,128,2176]{4,3,2,1,0:T(8,128)(2,1)}, bf16[2,1,2,128,2176]{4,3,2,1,0:T(8,128)(2,1)}, u32[]{:S(2)}, u32[]{:S(2)}) collective-permute-start(bf16[2,1,2,128,2176]{4,3,2,1,0:T(8,128)(2,1)} %add_convert_fusion), channel_id=1, source_target_pairs={{0,8},{4,12},{8,0},{12,4},{16,24},{20,28},{24,16},{28,20},{1,9},{5... | collective-permute-start | bytes 6684680 | tf_op jit(solution)/shard_map/ppermute | solution.py:868
  379.9 47.1 %collective-permute-start.41 = (bf16[1,1,2,128,2176]{4,3,2,1,0:T(8,128)(2,1)}, bf16[1,1,2,128,2176]{4,3,2,1,0:T(8,128)(2,1)}, u32[]{:S(2)}, u32[]{:S(2)}) collective-permute-start(bf16[1,1,2,128,2176]{4,3,2,1,0:T(8,128)(2,1)} %add_convert_fusion.4), channel_id=1, source_target_pairs={{0,8},{4,12},{8,0},{12,4},{16,24},{20,28},{24,16},{28,20},{1,9},{5... | collective-permute-start | bytes 3342344 | tf_op jit(solution)/shard_map/ppermute | solution.py:868
  384.7 42.3 %collective-permute-start.42 = (bf16[1,1,2,128,2176]{4,3,2,1,0:T(8,128)(2,1)}, bf16[1,1,2,128,2176]{4,3,2,1,0:T(8,128)(2,1)S(1)}, u32[]{:S(2)}, u32[]{:S(2)}) collective-permute-start(bf16[1,1,2,128,2176]{4,3,2,1,0:T(8,128)(2,1)} %add_convert_fusion.3), channel_id=1, source_target_pairs={{0,16},{4,20},{8,24},{12,28},{16,0},{20,4},{24,8},{28,12},{1,17},{... | collective-permute-start | bytes 3342344 | tf_op jit(solution)/shard_map/ppermute | solution.py:868
  422.9 48.1 %collective-permute-start.48 = (bf16[2,1,4,128,1024]{4,3,2,1,0:T(8,128)(2,1)}, bf16[2,1,4,128,1024]{4,3,2,1,0:T(8,128)(2,1)}, u32[]{:S(2)}, u32[]{:S(2)}) collective-permute-start(bf16[2,1,4,128,1024]{4,3,2,1,0:T(8,128)(2,1)} %add_convert_fusion.2), channel_id=1, source_target_pairs={{0,8},{4,12},{8,0},{12,4},{16,24},{20,28},{24,16},{28,20},{1,9},{5... | collective-permute-start | bytes 6291464 | tf_op jit(solution)/shard_map/ppermute | solution.py:868
  440.1 34.7 %collective-permute-start.44 = (bf16[4,4,128,512]{3,2,1,0:T(8,128)(2,1)}, bf16[4,4,128,512]{3,2,1,0:T(8,128)(2,1)S(1)}, u32[]{:S(2)}, u32[]{:S(2)}) collective-permute-start(bf16[4,4,128,512]{3,2,1,0:T(8,128)(2,1)} %get-tuple-element.196), channel_id=1, source_target_pairs={{0,4},{4,0},{8,12},{12,8},{16,20},{20,16},{24,28},{28,24},{1,5},{5... | collective-permute-start | bytes 6291464 | tf_op jit(solution)/shard_map/ppermute | solution.py:868
  443.9 25.1 %collective-permute-start.47 = (bf16[1,1,128,2176]{3,2,1,0:T(8,128)(2,1)S(1)}, bf16[1,1,128,2176]{3,2,1,0:T(8,128)(2,1)S(1)}, u32[]{:S(2)}, u32[]{:S(2)}) collective-permute-start(bf16[1,1,128,2176]{3,2,1,0:T(8,128)(2,1)S(1)} %add_convert_fusion.8), channel_id=1, source_target_pairs={{0,1},{1,0},{2,3},{3,2},{4,5},{5,4},{6,7},{7,6},{8,9},{9,8},{10,11... | collective-permute-start | bytes 1671176 | tf_op jit(solution)/shard_map/ppermute | solution.py:935
  473.2 31.2 %collective-permute-start.49 = (bf16[1,1,4,128,1024]{4,3,2,1,0:T(8,128)(2,1)S(1)}, bf16[1,1,4,128,1024]{4,3,2,1,0:T(8,128)(2,1)S(1)}, u32[]{:S(2)}, u32[]{:S(2)}) collective-permute-start(bf16[1,1,4,128,1024]{4,3,2,1,0:T(8,128)(2,1)S(1)} %add_convert_fusion.5), channel_id=1, source_target_pairs={{0,16},{4,20},{8,24},{12,28},{16,0},{20,4},{24,8},{28,12},{1,17},{... | collective-permute-start | bytes 3145736 | tf_op jit(solution)/shard_map/ppermute | solution.py:868
  475.1 29.2 %collective-permute-start.45 = (bf16[2,1,4,128,512]{4,3,2,1,0:T(8,128)(2,1)S(1)}, bf16[2,1,4,128,512]{4,3,2,1,0:T(8,128)(2,1)S(1)}, u32[]{:S(2)}, u32[]{:S(2)}) collective-permute-start(bf16[2,1,4,128,512]{4,3,2,1,0:T(8,128)(2,1)S(1)} %add_convert_fusion.6), channel_id=1, source_target_pairs={{0,8},{4,12},{8,0},{12,4},{16,24},{20,28},{24,16},{28,20},{1,9},{5... | collective-permute-start | bytes 3145736 | tf_op jit(solution)/shard_map/ppermute | solution.py:868
  476.1 28.3 %collective-permute-start.50 = (bf16[1,128,2176]{2,1,0:T(8,128)(2,1)S(1)}, bf16[1,128,2176]{2,1,0:T(8,128)(2,1)S(1)}, u32[]{:S(2)}, u32[]{:S(2)}) collective-permute-start(bf16[1,128,2176]{2,1,0:T(8,128)(2,1)S(1)} %fusion.3), channel_id=1, source_target_pairs={{0,2},{1,3},{2,0},{3,1},{4,6},{5,7},{6,4},{7,5},{8,10},{9,11},{10,... | collective-permute-start | bytes 1671176 | tf_op jit(solution)/shard_map/ppermute | solution.py:935
  522.0 25.1 %collective-permute-start.58 = (bf16[1,2,128,2176]{3,2,1,0:T(8,128)(2,1)S(1)}, bf16[1,2,128,2176]{3,2,1,0:T(8,128)(2,1)S(1)}, u32[]{:S(2)}, u32[]{:S(2)}) collective-permute-start(bf16[1,2,128,2176]{3,2,1,0:T(8,128)(2,1)S(1)} %pad_maximum_fusion.11), channel_id=1, source_target_pairs={{0,16},{4,20},{8,24},{12,28},{16,0},{20,4},{24,8},{28,12},{1,17},{... | collective-permute-start | bytes 3342344 | tf_op jit(solution)/shard_map/ppermute | solution.py:868
  530.0 81.0 %collective-permute-start.70 = (bf16[256,1024]{1,0:T(8,128)(2,1)}, bf16[256,1024]{1,0:T(8,128)(2,1)}, u32[]{:S(2)}, u32[]{:S(2)}) collective-permute-start(bf16[256,1024]{1,0:T(8,128)(2,1)} %get-tuple-element.263), channel_id=1, source_target_pairs={{2,0},{6,1},{4,2},{0,3},{3,4},{7,5},{5,6},{1,7},{10,8},{14,9},{12,... | collective-permute-start | bytes 1572872 | tf_op jit(solution)/shard_map/ppermute | solution.py:926
  557.3 54.4 %collective-permute-start.34 = (bf16[256,1024]{1,0:T(8,128)(2,1)}, bf16[256,1024]{1,0:T(8,128)(2,1)}, u32[]{:S(2)}, u32[]{:S(2)}) collective-permute-start(bf16[256,1024]{1,0:T(8,128)(2,1)} %get-tuple-element.262), channel_id=1, source_target_pairs={{0,0},{4,1},{6,2},{2,3},{1,4},{5,5},{7,6},{3,7},{8,8},{12,9},{14,1... | collective-permute-start | bytes 1572872 | tf_op jit(solution)/shard_map/ppermute | solution.py:926
  583.1 32.9 %collective-permute-start.72 = (bf16[256,1024]{1,0:T(8,128)(2,1)}, bf16[256,1024]{1,0:T(8,128)(2,1)}, u32[]{:S(2)}, u32[]{:S(2)}) collective-permute-start(bf16[256,1024]{1,0:T(8,128)(2,1)} %get-tuple-element.261), channel_id=1, source_target_pairs={{2,0},{6,1},{4,2},{0,3},{3,4},{7,5},{5,6},{1,7},{10,8},{14,9},{12,... | collective-permute-start | bytes 1572872 | tf_op jit(solution)/shard_map/ppermute | solution.py:926
  592.9 23.1 %collective-permute-start.71 = (bf16[256,1024]{1,0:T(8,128)(2,1)}, bf16[256,1024]{1,0:T(8,128)(2,1)}, u32[]{:S(2)}, u32[]{:S(2)}) collective-permute-start(bf16[256,1024]{1,0:T(8,128)(2,1)} %get-tuple-element.260), channel_id=1, source_target_pairs={{0,0},{4,1},{6,2},{2,3},{1,4},{5,5},{7,6},{3,7},{8,8},{12,9},{14,1... | collective-permute-start | bytes 1572872 | tf_op jit(solution)/shard_map/ppermute | solution.py:926
  (103 other events, 1124.8 us)

commit v4 on v3

--- a/solution.py
+++ b/solution.py
@@ -1098,7 +1098,7 @@
         far_w.start()
         self_own, self_oth = self_w.finish()
         cross_own, cross_oth = cross_w.finish()
-        cot = to_sequence(after(out_grad, encoder))
+        cot = to_sequence(after(out_grad, encoder, near_w.array))
         stream, encoder = to_relative(stream), to_relative(encoder)
 
         segments = jnp.concatenate([dec_segments, enc_segments], axis=1)
@@ -1126,7 +1126,7 @@
         distance_bias = lax.dot_general(
             all_bias, onehot, (((0,), (1,)), ((), ())), precision=HIGHEST, preferred_element_type=F32
         )
-        slabs = bias_slabs(distance_bias)
+        slabs = bias_slabs(after(distance_bias, *first))
         gain_one, gain_two, gain_three = (
             to_relative(gain.reshape(1, width)) for gain in (self_gain, cross_gain, ffn_gain)
         )

time: 643 us -> 634 us (0.986)
  waiting for transfers between devices: 165 us -> 143 us
  starting transfers between devices: 103 us -> 111 us
    ppermute x42, waiting for transfers between devices: 56.1 us -> 32 us  [swap(): return lax.ppermute(array, 'batch', [(b, b ^ mask) for b in range(batch)])]
    ppermute x6, waiting for transfers between devices: 14.1 us -> 31.8 us  [to_sequence(): received.append(lax.ppermute(part, both, route))]
    ppermute x21, waiting for transfers between devices: 86.6 us -> 70.6 us  [swap_z(): return lax.ppermute(array, 'group', [(z, z ^ mask) for z in range(shards)])]
    ppermute x21, starting transfers between devices: 36.9 us -> 46.7 us  [swap_z(): return lax.ppermute(array, 'group', [(z, z ^ mask) for z in range(shards)])]
    unnamed x214 -> x210, local copies, waits for them, and re-layouts: 23.5 us -> 24.5 us
  transfers between devices with their start and end apart: 75 -> 75, of which waited for: 29 -> 27; matrix products, arithmetic and copies ran while one was open for 16% -> 17% of each run, Pallas kernels for 38% -> 38%
where the time goes in v4:
time: 634 us; the launch traced here: 625 us
  Pallas kernels  242 us (38%)
  waiting for transfers between devices  143 us (23%)
  starting transfers between devices  111 us (18%)
  other arithmetic  67.1 us (11%)
  local copies, waits for them, and re-layouts  58.9 us (9%)
    ppermute x21, waiting for transfers between devices, swap_z(): return lax.ppermute(array, 'group', [(z, z ^ mask) for z in range(shards)])  70.6 us
    ppermute x21, starting transfers between devices, swap_z(): return lax.ppermute(array, 'group', [(z, z ^ mask) for z in range(shards)])  46.7 us
    pallas_call x2, Pallas kernels, feed_forward(): call(functools.partial(ffn_kernel, ff), (shape(rows, width, dtype=F32), s...  44 us
    ppermute x42, starting transfers between devices, swap(): return lax.ppermute(array, 'batch', [(b, b ^ mask) for b in range(batch)])  35 us
    pallas_call x1, Pallas kernels, self_attention_back(): call(self_back_kernel, (shape(*q.shape), shape(*own.shape, dtype=F32), sh...  32.2 us
    ppermute x42, waiting for transfers between devices, swap(): return lax.ppermute(array, 'batch', [(b, b ^ mask) for b in range(batch)])  32 us
    ppermute x6, waiting for transfers between devices, to_sequence(): received.append(lax.ppermute(part, both, route))  31.8 us
    unnamed x210, local copies, waits for them, and re-layouts  24.5 us
  transfers between devices with their start and end apart: 75, of which 27 were waited for; matrix products, arithmetic and copies ran while one was open for 17% of the time, Pallas kernels for 38%

profile of v4, /device:TPU:0, one launch (start us, length us, event | category | flops | bytes accessed | tf_op | source)
XLA Modules:
  0.0 624.8 jit_solution(4933991644917863939)
XLA Ops:
  26.3 5.4 collective-permute-start.2
  43.9 11.9 %collective-permute-done.3 = bf16[256,1024]{1,0:T(8,128)(2,1)} collective-permute-done((bf16[256,1024]{1,0:T(8,128)(2,1)}, bf16[256,1024]{1,0:T(8,128)(2,1)}, u32[]{:S(2)}, u32[]{:S(2)}) %collective-permute-start.3) | collective-permute-done | bytes 524320 | tf_op jit(solution)/shard_map/ppermute | solution.py:919
  57.8 8.3 %collective-permute-start.14 = (bf16[128,2176]{1,0:T(8,128)(2,1)}, bf16[128,2176]{1,0:T(8,128)(2,1)}, u32[]{:S(2)}, u32[]{:S(2)}) collective-permute-start(bf16[128,2176]{1,0:T(8,128)(2,1)} %shard_map.342), channel_id=1, source_target_pairs={{0,2},{1,3},{2,0},{3,1},{4,6},{5,7},{6,4},{7,5},{8,10},{9,11},{10,... | collective-permute-start | bytes 1671176 | tf_op jit(solution)/shard_map/ppermute | solution.py:935
  71.8 11.2 %shard_map.344.slab_ref = f32[16,128,1152]{2,1,0:T(8,128)} custom-call(f32[16,1,1152]{2,1,0:T(1,128)} %reshape.454.base_ref), custom_call_target="tpu_custom_call" | custom-call | flops 11000000512 | bytes 33000000 | tf_op jit(solution)/shard_map/pallas_call | solution.py:339
  83.0 6.6 %collective-permute-done.14 = bf16[128,2176]{1,0:T(8,128)(2,1)} collective-permute-done((bf16[128,2176]{1,0:T(8,128)(2,1)}, bf16[128,2176]{1,0:T(8,128)(2,1)}, u32[]{:S(2)}, u32[]{:S(2)}) %collective-permute-start.14) | collective-permute-done | bytes 557088 | tf_op jit(solution)/shard_map/ppermute | solution.py:935
  98.6 8.3 %collective-permute-done.27 = bf16[128,1024]{1,0:T(8,128)(2,1)S(1)} collective-permute-done((bf16[128,1024]{1,0:T(8,128)(2,1)S(1)}, bf16[128,1024]{1,0:T(8,128)(2,1)S(1)}, u32[]{:S(2)}, u32[]{:S(2)}) %collective-permute-start.27) | collective-permute-done | bytes 262176 | tf_op jit(solution)/shard_map/ppermute | solution.py:919
  111.0 6.2 collective-permute-done.15
  132.1 11.7 %collective-permute-done.30 = bf16[256,1024]{1,0:T(8,128)(2,1)S(1)} collective-permute-done((bf16[256,1024]{1,0:T(8,128)(2,1)S(1)}, bf16[256,1024]{1,0:T(8,128)(2,1)S(1)}, u32[]{:S(2)}, u32[]{:S(2)}) %collective-permute-start.30) | collective-permute-done | bytes 524320 | tf_op jit(solution)/shard_map/ppermute | solution.py:919
  146.1 6.4 %shard_map.343 = (bf16[512,1024]{1,0:T(8,128)(2,1)}, bf16[512,1024]{1,0:T(8,128)(2,1)}, bf16[512,1024]{1,0:T(8,128)(2,1)}) custom-call(bf16[512,1024]{1,0:T(8,128)(2,1)} %copy-done.38, f32[1,1024]{1,0:T(1,128)} %copy-done.50, bf16[4,4,128,768]{3,2,1,0:T(8,128)(2,1)} %bitcast.241, bf16[4,4,128,768]{3,2,1,0:T(8,128)(2,1)} %collective-permute-done.17.oth_ref.wo_oth), custom_call_target="tpu_custom_call" | custom-call | flops 7000000000 | bytes 21000000 | tf_op jit(solution)/shard_map/pallas_call | solution.py:111
  152.6 6.4 %collective-permute-done.16 = bf16[1,1,2,128,2176]{4,3,2,1,0:T(8,128)(2,1)} collective-permute-done((bf16[1,1,2,128,2176]{4,3,2,1,0:T(8,128)(2,1)}, bf16[1,1,2,128,2176]{4,3,2,1,0:T(8,128)(2,1)}, u32[]{:S(2)}, u32[]{:S(2)}) %collective-permute-start.16) | collective-permute-done | bytes 1114144 | tf_op jit(solution)/shard_map/ppermute | solution.py:868
  168.7 20.3 %shard_map.345 = (bf16[512,1024]{1,0:T(8,128)(2,1)}, f32[16,1,512]{2,1,0:T(1,128)}) custom-call(s32[4]{0:T(128)} %pad_add_fusion.2.ids_ref, bf16[512,1024]{1,0:T(8,128)(2,1)} %get-tuple-element.145.q_ref, bf16[512,1024]{1,0:T(8,128)(2,1)} %get-tuple-element.146.own_ref, bf16[512,1024]{1,0:T(8,128)(2,1)} %copy-done.51, f32[16,128,1152]{2,1,0:T(8,128)} %shard_map.344.slab_ref, ...), custom_call_target="tpu_custom_call" | custom-call | flops 20000000000 | bytes 60000000 | tf_op jit(solution)/shard_map/pallas_call | solution.py:446
  189.0 9.9 %shard_map.346 = (f32[512,1024]{1,0:T(8,128)}, bf16[512,1024]{1,0:T(8,128)(2,1)}, bf16[512,1024]{1,0:T(8,128)(2,1)}) custom-call(bf16[512,1024]{1,0:T(8,128)(2,1)} %copy-done.38, bf16[512,1024]{1,0:T(8,128)(2,1)} %get-tuple-element.148.att_ref.att_one_ref, f32[1,1024]{1,0:T(1,128)} %copy-done.49, bf16[4,4,128,768]{3,2,1,0:T(8,128)(2,1)} %bitcast.242, ...), custom_call_target="tpu_custom_call" | custom-call | flops 10000000000 | bytes 30000000 | tf_op jit(solution)/shard_map/pallas_call | solution.py:172
  198.9 16.0 %shard_map.348 = (bf16[512,1024]{1,0:T(8,128)(2,1)}, f32[16,1,512]{2,1,0:T(1,128)}) custom-call(bf16[512,1024]{1,0:T(8,128)(2,1)} %get-tuple-element.152.q_ref, bf16[256,1024]{1,0:T(8,128)(2,1)} %shard_map.347.own_ref, bf16[256,1024]{1,0:T(8,128)(2,1)} %collective-permute-done.28.oth_ref, s32[512,1]{1,0:T(8,128)} %copy.44.kseg_ref, ...), custom_call_target="tpu_custom_call" | custom-call | flops 16000000000 | bytes 48000000 | tf_op jit(solution)/shard_map/pallas_call | solution.py:468
  226.0 6.9 %shard_map.349 = (f32[512,1024]{1,0:T(8,128)}, bf16[512,1024]{1,0:T(8,128)(2,1)}) custom-call(f32[512,1024]{1,0:T(8,128)} %get-tuple-element.149.x_ref.s_ref, bf16[512,1024]{1,0:T(8,128)(2,1)} %get-tuple-element.155.att_ref, f32[1,1024]{1,0:T(1,128)} %copy-done.57, bf16[4,4,128,768]{3,2,1,0:T(8,128)(2,1)} %bitcast.43.wq_own.own_ref.wo_own, ...), custom_call_target="tpu_custom_call" | custom-call | flops 7000000000 | bytes 21000000 | tf_op jit(solution)/shard_map/pallas_call | solution.py:214
  232.9 21.9 %shard_map.350 = (f32[512,1024]{1,0:T(8,128)}, f32[512,1024]{1,0:T(8,128)}, bf16[4,2,128,2176]{3,2,1,0:T(8,128)(2,1)}, bf16[4,2,128,2176]{3,2,1,0:T(8,128)(2,1)}) custom-call(bf16[512,1024]{1,0:T(8,128)(2,1)} %get-tuple-element.162.n_ref, bf16[512,1024]{1,0:T(8,128)(2,1)} %copy-done.37, bf16[4,2,128,2176]{3,2,1,0:T(8,128)(2,1)} %bitcast.61.own_ref, ...), custom_call_target="tpu_custom_call" | custom-call | flops 22000001024 | bytes 66000000 | tf_op jit(solution)/shard_map/pallas_call | solution.py:270
  255.2 22.0 %shard_map.351 = (f32[512,1024]{1,0:T(8,128)}, f32[512,1024]{1,0:T(8,128)}, bf16[4,2,128,2176]{3,2,1,0:T(8,128)(2,1)}, bf16[4,2,128,2176]{3,2,1,0:T(8,128)(2,1)}) custom-call(bf16[512,1024]{1,0:T(8,128)(2,1)} %get-tuple-element.162.n_ref, bf16[512,1024]{1,0:T(8,128)(2,1)} %copy-done.37, bf16[4,2,128,2176]{3,2,1,0:T(8,128)(2,1)} %bitcast.62.own_ref, ...), custom_call_target="tpu_custom_call" | custom-call | flops 22000001024 | bytes 66000000 | tf_op jit(solution)/shard_map/pallas_call | solution.py:270
  288.4 10.3 %shard_map.352 = (bf16[512,1024]{1,0:T(8,128)(2,1)}, f32[512,1024]{1,0:T(8,128)}, bf16[512,1024]{1,0:T(8,128)(2,1)}, f32[1,1024]{1,0:T(1,128)}, bf16[512,1024]{1,0:T(8,128)(2,1)}) custom-call(f32[512,1024]{1,0:T(8,128)} %get-tuple-element.156.s_ref, f32[512,1024]{1,0:T(8,128)} %get-tuple-element.161.ya_ref, f32[512,1024]{1,0:T(8,128)} %get-tuple-element.164.yb_ref, ...), custom_call_target="tpu_custom_call" | custom-call | flops 10000000000 | bytes 30000000 | tf_op jit(solution)/shard_map/pallas_call | solution.py:311
  304.4 21.7 %shard_map.353 = (bf16[512,1024]{1,0:T(8,128)(2,1)}, f32[256,1024]{1,0:T(8,128)}, bf16[256,1024]{1,0:T(8,128)(2,1)}) custom-call(bf16[512,1024]{1,0:T(8,128)(2,1)} %get-tuple-element.152.q_ref, bf16[512,1024]{1,0:T(8,128)(2,1)} %get-tuple-element.176.ga_ref, f32[16,1,512]{2,1,0:T(1,128)} %get-tuple-element.177.lse_ref, ...), custom_call_target="tpu_custom_call" | custom-call | flops 20999999488 | bytes 63000000 | tf_op jit(solution)/shard_map/pallas_call | solution.py:605
  335.0 19.3 %shard_map.354 = (bf16[4,4,128,768]{3,2,1,0:T(8,128)(2,1)}, bf16[4,4,128,768]{3,2,1,0:T(8,128)(2,1)}, bf16[4,4,128,256]{3,2,1,0:T(8,128)(2,1)}, bf16[4,4,128,256...) custom-call(bf16[512,1024]{1,0:T(8,128)(2,1)} %get-tuple-element.178, ...), custom_call_target="tpu_custom_call" | custom-call | flops 17999998976 | bytes 54000000 | tf_op jit(solution)/shard_map/pallas_call | solution.py:684
  375.3 32.2 %shard_map.355 = (bf16[512,1024]{1,0:T(8,128)(2,1)}, f32[512,1024]{1,0:T(8,128)}, bf16[512,1024]{1,0:T(8,128)(2,1)}, f32[16,8,1152]{2,1,0:T(8,128)}) custom-call(s32[4]{0:T(128)} %pad_add_fusion.2.ids_ref, bf16[512,1024]{1,0:T(8,128)(2,1)} %get-tuple-element.145.q_ref, bf16[512,1024]{1,0:T(8,128)(2,1)} %get-tuple-element.189.ga_ref, ...), custom_call_target="tpu_custom_call" | custom-call | flops 32000000000 | bytes 96000000 | tf_op jit(solution)/shard_map/pallas_call | solution.py:555
  419.5 12.0 %shard_map.356 = (bf16[4,4,128,512]{3,2,1,0:T(8,128)(2,1)}, bf16[4,4,128,512]{3,2,1,0:T(8,128)(2,1)}, bf16[512,1024]{1,0:T(8,128)(2,1)}, f32[1,1024]{1,0:T(1,128)}) custom-call(bf16[512,1024]{1,0:T(8,128)(2,1)} %get-tuple-element.192.dq_ref, f32[512,1024]{1,0:T(8,128)} %get-tuple-element.193.dko_ref, bf16[512,1024]{1,0:T(8,128)(2,1)} %collective-permute-done.43.dkr_ref, ...), custom_call_target="tpu_custom_call" | custom-call | flops 14000000000 | bytes 42000000 | tf_op jit(solution)/shard_map/pallas_call | solution.py:755
  437.1 11.9 %collective-permute-done.46 = bf16[1,1,128,2176]{3,2,1,0:T(8,128)(2,1)S(1)} collective-permute-done((bf16[1,1,128,2176]{3,2,1,0:T(8,128)(2,1)S(1)}, bf16[1,1,128,2176]{3,2,1,0:T(8,128)(2,1)S(1)}, u32[]{:S(2)}, u32[]{:S(2)}) %collective-permute-start.46) | collective-permute-done | bytes 557088 | tf_op jit(solution)/shard_map/ppermute | solution.py:935
  449.0 11.4 %collective-permute-done.47 = bf16[1,1,128,2176]{3,2,1,0:T(8,128)(2,1)S(1)} collective-permute-done((bf16[1,1,128,2176]{3,2,1,0:T(8,128)(2,1)S(1)}, bf16[1,1,128,2176]{3,2,1,0:T(8,128)(2,1)S(1)}, u32[]{:S(2)}, u32[]{:S(2)}) %collective-permute-start.47) | collective-permute-done | bytes 557088 | tf_op jit(solution)/shard_map/ppermute | solution.py:935
  483.2 12.3 %collective-permute-done.50 = bf16[1,128,2176]{2,1,0:T(8,128)(2,1)S(1)} collective-permute-done((bf16[1,128,2176]{2,1,0:T(8,128)(2,1)S(1)}, bf16[1,128,2176]{2,1,0:T(8,128)(2,1)S(1)}, u32[]{:S(2)}, u32[]{:S(2)}) %collective-permute-start.50) | collective-permute-done | bytes 557088 | tf_op jit(solution)/shard_map/ppermute | solution.py:935
  503.7 5.2 collective-permute-done.55
  527.3 10.9 %collective-permute-done.58 = bf16[1,2,128,2176]{3,2,1,0:T(8,128)(2,1)S(1)} collective-permute-done((bf16[1,2,128,2176]{3,2,1,0:T(8,128)(2,1)S(1)}, bf16[1,2,128,2176]{3,2,1,0:T(8,128)(2,1)S(1)}, u32[]{:S(2)}, u32[]{:S(2)}) %collective-permute-start.58) | collective-permute-done | bytes 1114144 | tf_op jit(solution)/shard_map/ppermute | solution.py:868
  548.4 5.4 collective-permute-start.34
  563.4 8.8 %shard_map.357 = (f32[704,1024]{1,0:T(8,128)}, f32[704,1024]{1,0:T(8,128)}, f32[704,1024]{1,0:T(8,128)}) custom-call(s32[8]{0:T(128)} %multiply_or_fusion.pos_ref, bf16[8,128,2176]{2,1,0:T(8,128)(2,1)} %pad_maximum_fusion.2.x_ref), custom_call_target="tpu_custom_call" | custom-call | flops 5000000000 | bytes 15000000 | tf_op jit(solution)/shard_map/pallas_call | solution.py:837
  578.5 5.7 collective-permute-done.67
  584.2 5.4 collective-permute-start.71
  593.3 6.9 %shard_map.358 = (f32[1024,256]{1,0:T(8,128)}, f32[1024,128]{1,0:T(8,128)}, f32[1024,128]{1,0:T(8,128)}, f32[256,1024]{1,0:T(8,128)}, f32[256,1024]{1,0:T(8,128)}) custom-call(s32[8]{0:T(128)} %multiply_or_fusion.pos_ref, bf16[8,128,1024]{2,1,0:T(8,128)(2,1)} %pad_maximum_fusion.8.x_ref), custom_call_target="tpu_custom_call" | custom-call | flops 5000000000 | bytes 15000000 | tf_op jit(solution)/shard_map/pallas_call | solution.py:837
  611.5 6.2 shard_map.359
  (474 shorter events, 257.8 us)
Async XLA Ops:
  6.5 25.1 %collective-permute-start.4 = (bf16[128,768]{1,0:T(8,128)(2,1)}, bf16[128,768]{1,0:T(8,128)(2,1)S(1)}, u32[]{:S(2)}, u32[]{:S(2)}) collective-permute-start(bf16[128,768]{1,0:T(8,128)(2,1)} %shard_map.340), channel_id=1, source_target_pairs={{0,1},{1,0},{2,3},{3,2},{4,5},{5,4},{6,7},{7,6},{8,9},{9,8},{10,11... | collective-permute-start | bytes 589832 | tf_op jit(solution)/shard_map/ppermute | solution.py:935
  33.0 23.8 %collective-permute-start.6 = (bf16[1,1,4,128,768]{4,3,2,1,0:T(8,128)(2,1)S(1)}, bf16[1,1,4,128,768]{4,3,2,1,0:T(8,128)(2,1)S(1)}, u32[]{:S(2)}, u32[]{:S(2)}) collective-permute-start(bf16[1,1,4,128,768]{4,3,2,1,0:T(8,128)(2,1)S(1)} %maximum_bitcast_fusion.2), channel_id=1, source_target_pairs={{0,8},{4,12},{8,0},{12,4},{16,24},{20,28},{24,16},{28,20},{1,9},{5... | collective-permute-start | bytes 2359304 | tf_op jit(solution)/shard_map/ppermute | solution.py:868
  57.8 31.8 %collective-permute-start.14 = (bf16[128,2176]{1,0:T(8,128)(2,1)}, bf16[128,2176]{1,0:T(8,128)(2,1)}, u32[]{:S(2)}, u32[]{:S(2)}) collective-permute-start(bf16[128,2176]{1,0:T(8,128)(2,1)} %shard_map.342), channel_id=1, source_target_pairs={{0,2},{1,3},{2,0},{3,1},{4,6},{5,7},{6,4},{7,5},{8,10},{9,11},{10,... | collective-permute-start | bytes 1671176 | tf_op jit(solution)/shard_map/ppermute | solution.py:935
  66.1 27.5 %collective-permute-start.10 = (bf16[128,2176]{1,0:T(8,128)(2,1)}, bf16[128,2176]{1,0:T(8,128)(2,1)}, u32[]{:S(2)}, u32[]{:S(2)}) collective-permute-start(bf16[128,2176]{1,0:T(8,128)(2,1)} %shard_map.342), channel_id=1, source_target_pairs={{0,1},{1,0},{2,3},{3,2},{4,5},{5,4},{6,7},{7,6},{8,9},{9,8},{10,11... | collective-permute-start | bytes 1671176 | tf_op jit(solution)/shard_map/ppermute | solution.py:935
  67.8 39.2 %collective-permute-start.11 = (bf16[1,2,4,128,768]{4,3,2,1,0:T(8,128)(2,1)}, bf16[1,2,4,128,768]{4,3,2,1,0:T(8,128)(2,1)}, u32[]{:S(2)}, u32[]{:S(2)}) collective-permute-start(bf16[1,2,4,128,768]{4,3,2,1,0:T(8,128)(2,1)} %pad_maximum_fusion.9), channel_id=1, source_target_pairs={{0,16},{4,20},{8,24},{12,28},{16,0},{20,4},{24,8},{28,12},{1,17},{... | collective-permute-start | bytes 4718600 | tf_op jit(solution)/shard_map/ppermute | solution.py:868
  69.1 50.4 %collective-permute-start.12 = (bf16[2,1,4,128,768]{4,3,2,1,0:T(8,128)(2,1)}, bf16[2,1,4,128,768]{4,3,2,1,0:T(8,128)(2,1)}, u32[]{:S(2)}, u32[]{:S(2)}) collective-permute-start(bf16[2,1,4,128,768]{4,3,2,1,0:T(8,128)(2,1)} %pad_maximum_fusion.10), channel_id=1, source_target_pairs={{0,8},{4,12},{8,0},{12,4},{16,24},{20,28},{24,16},{28,20},{1,9},{5... | collective-permute-start | bytes 4718600 | tf_op jit(solution)/shard_map/ppermute | solution.py:868
  95.0 22.3 %collective-permute-start.15 = (bf16[128,2176]{1,0:T(8,128)(2,1)}, bf16[128,2176]{1,0:T(8,128)(2,1)S(1)}, u32[]{:S(2)}, u32[]{:S(2)}) collective-permute-start(bf16[128,2176]{1,0:T(8,128)(2,1)} %collective-permute-done.14), channel_id=1, source_target_pairs={{0,1},{1,0},{2,3},{3,2},{4,5},{5,4},{6,7},{7,6},{8,9},{9,8},{10,11... | collective-permute-start | bytes 1671176 | tf_op jit(solution)/shard_map/ppermute | solution.py:935
  108.8 37.4 %collective-permute-start.17 = (bf16[4,4,128,768]{3,2,1,0:T(8,128)(2,1)S(1)}, bf16[4,4,128,768]{3,2,1,0:T(8,128)(2,1)}, u32[]{:S(2)}, u32[]{:S(2)}) collective-permute-start(bf16[4,4,128,768]{3,2,1,0:T(8,128)(2,1)S(1)} %bitcast.240), channel_id=1, source_target_pairs={{0,4},{4,0},{8,12},{12,8},{16,20},{20,16},{24,28},{28,24},{1,5},{5... | collective-permute-start | bytes 9437192 | tf_op jit(solution)/shard_map/ppermute | solution.py:868
  119.5 33.1 %collective-permute-start.13 = (bf16[1,1,2,128,2176]{4,3,2,1,0:T(8,128)(2,1)S(1)}, bf16[1,1,2,128,2176]{4,3,2,1,0:T(8,128)(2,1)}, u32[]{:S(2)}, u32[]{:S(2)}) collective-permute-start(bf16[1,1,2,128,2176]{4,3,2,1,0:T(8,128)(2,1)S(1)} %maximum_bitcast_fusion), channel_id=1, source_target_pairs={{0,8},{4,12},{8,0},{12,4},{16,24},{20,28},{24,16},{28,20},{1,9},{5... | collective-permute-start | bytes 3342344 | tf_op jit(solution)/shard_map/ppermute | solution.py:868
  121.8 22.0 %collective-permute-start.30 = (bf16[256,1024]{1,0:T(8,128)(2,1)S(1)}, bf16[256,1024]{1,0:T(8,128)(2,1)S(1)}, u32[]{:S(2)}, u32[]{:S(2)}) collective-permute-start(bf16[256,1024]{1,0:T(8,128)(2,1)S(1)} %get-tuple-element.266), channel_id=1, source_target_pairs={{0,2},{1,6},{2,4},{3,0},{4,3},{5,7},{6,5},{7,1},{8,10},{9,14},{10,... | collective-permute-start | bytes 1572872 | tf_op jit(solution)/shard_map/ppermute | solution.py:919
  127.5 36.0 %collective-permute-start.23 = (bf16[4,4,128,768]{3,2,1,0:T(8,128)(2,1)}, bf16[4,4,128,768]{3,2,1,0:T(8,128)(2,1)}, u32[]{:S(2)}, u32[]{:S(2)}) collective-permute-start(bf16[4,4,128,768]{3,2,1,0:T(8,128)(2,1)} %bitcast.43.wq_own.own_ref.wo_own), channel_id=1, source_target_pairs={{0,4},{4,0},{8,12},{12,8},{16,20},{20,16},{24,28},{28,24},{1,5},{5... | collective-permute-start | bytes 9437192 | tf_op jit(solution)/shard_map/ppermute | solution.py:868
  131.5 27.5 %collective-permute-start.16 = (bf16[1,1,2,128,2176]{4,3,2,1,0:T(8,128)(2,1)}, bf16[1,1,2,128,2176]{4,3,2,1,0:T(8,128)(2,1)}, u32[]{:S(2)}, u32[]{:S(2)}) collective-permute-start(bf16[1,1,2,128,2176]{4,3,2,1,0:T(8,128)(2,1)} %maximum_bitcast_fusion.1), channel_id=1, source_target_pairs={{0,16},{4,20},{8,24},{12,28},{16,0},{20,4},{24,8},{28,12},{1,17},{... | collective-permute-start | bytes 3342344 | tf_op jit(solution)/shard_map/ppermute | solution.py:868
  161.5 53.4 %collective-permute-start.24 = (bf16[1,2,2,128,2176]{4,3,2,1,0:T(8,128)(2,1)}, bf16[1,2,2,128,2176]{4,3,2,1,0:T(8,128)(2,1)}, u32[]{:S(2)}, u32[]{:S(2)}) collective-permute-start(bf16[1,2,2,128,2176]{4,3,2,1,0:T(8,128)(2,1)} %constant_dynamic-update-slice_fusion.28), channel_id=1, source_target_pairs={{0,16},{4,20},{8,24},{12,28},{16,0},{20,4},{24,8},{28,12},{1,17},{... | collective-permute-start | bytes 6684680 | tf_op jit(solution)/shard_map/ppermute | solution.py:868
  163.4 51.5 %collective-permute-start.25 = (bf16[2,1,2,128,2176]{4,3,2,1,0:T(8,128)(2,1)S(1)}, bf16[2,1,2,128,2176]{4,3,2,1,0:T(8,128)(2,1)}, u32[]{:S(2)}, u32[]{:S(2)}) collective-permute-start(bf16[2,1,2,128,2176]{4,3,2,1,0:T(8,128)(2,1)S(1)} %constant_dynamic-update-slice_fusion.30), channel_id=1, source_target_pairs={{0,8},{4,12},{8,0},{12,4},{16,24},{20,28},{24,16},{28,20},{1,9},{5... | collective-permute-start | bytes 6684680 | tf_op jit(solution)/shard_map/ppermute | solution.py:868
  167.7 31.1 %collective-permute-start.28 = (bf16[256,1024]{1,0:T(8,128)(2,1)}, bf16[256,1024]{1,0:T(8,128)(2,1)}, u32[]{:S(2)}, u32[]{:S(2)}) collective-permute-start(bf16[256,1024]{1,0:T(8,128)(2,1)} %shard_map.347.own_ref), channel_id=1, source_target_pairs={{0,4},{4,0},{8,12},{12,8},{16,20},{20,16},{24,28},{28,24},{1,5},{5... | collective-permute-start | bytes 1572872 | tf_op jit(solution)/shard_map/ppermute | solution.py:868
  224.6 30.6 %collective-permute-start.32 = (bf16[4,2,128,2176]{3,2,1,0:T(8,128)(2,1)}, bf16[4,2,128,2176]{3,2,1,0:T(8,128)(2,1)}, u32[]{:S(2)}, u32[]{:S(2)}) collective-permute-start(bf16[4,2,128,2176]{3,2,1,0:T(8,128)(2,1)} %bitcast.62.own_ref), channel_id=1, source_target_pairs={{0,4},{4,0},{8,12},{12,8},{16,20},{20,16},{24,28},{28,24},{1,5},{5... | collective-permute-start | bytes 13369352 | tf_op jit(solution)/shard_map/ppermute | solution.py:868
  254.9 28.0 %collective-permute-start.33 = (bf16[4,2,128,2176]{3,2,1,0:T(8,128)(2,1)}, bf16[4,2,128,2176]{3,2,1,0:T(8,128)(2,1)}, u32[]{:S(2)}, u32[]{:S(2)}) collective-permute-start(bf16[4,2,128,2176]{3,2,1,0:T(8,128)(2,1)} %get-tuple-element.166), channel_id=1, source_target_pairs={{0,4},{4,0},{8,12},{12,8},{16,20},{20,16},{24,28},{28,24},{1,5},{5... | collective-permute-start | bytes 13369352 | tf_op jit(solution)/shard_map/ppermute | solution.py:868
  286.4 79.2 %collective-permute-start.35 = (bf16[1,2,2,128,2176]{4,3,2,1,0:T(8,128)(2,1)}, bf16[1,2,2,128,2176]{4,3,2,1,0:T(8,128)(2,1)}, u32[]{:S(2)}, u32[]{:S(2)}) collective-permute-start(bf16[1,2,2,128,2176]{4,3,2,1,0:T(8,128)(2,1)} %fusion), channel_id=1, source_target_pairs={{0,16},{4,20},{8,24},{12,28},{16,0},{20,4},{24,8},{28,12},{1,17},{... | collective-permute-start | bytes 6684680 | tf_op jit(solution)/shard_map/ppermute | solution.py:868
  302.9 62.7 %collective-permute-start.37 = (bf16[2,1,2,128,2176]{4,3,2,1,0:T(8,128)(2,1)}, bf16[2,1,2,128,2176]{4,3,2,1,0:T(8,128)(2,1)}, u32[]{:S(2)}, u32[]{:S(2)}) collective-permute-start(bf16[2,1,2,128,2176]{4,3,2,1,0:T(8,128)(2,1)} %add_convert_fusion), channel_id=1, source_target_pairs={{0,8},{4,12},{8,0},{12,4},{16,24},{20,28},{24,16},{28,20},{1,9},{5... | collective-permute-start | bytes 6684680 | tf_op jit(solution)/shard_map/ppermute | solution.py:868
  371.4 47.1 %collective-permute-start.41 = (bf16[1,1,2,128,2176]{4,3,2,1,0:T(8,128)(2,1)}, bf16[1,1,2,128,2176]{4,3,2,1,0:T(8,128)(2,1)}, u32[]{:S(2)}, u32[]{:S(2)}) collective-permute-start(bf16[1,1,2,128,2176]{4,3,2,1,0:T(8,128)(2,1)} %add_convert_fusion.4), channel_id=1, source_target_pairs={{0,8},{4,12},{8,0},{12,4},{16,24},{20,28},{24,16},{28,20},{1,9},{5... | collective-permute-start | bytes 3342344 | tf_op jit(solution)/shard_map/ppermute | solution.py:868
  375.2 43.3 %collective-permute-start.42 = (bf16[1,1,2,128,2176]{4,3,2,1,0:T(8,128)(2,1)}, bf16[1,1,2,128,2176]{4,3,2,1,0:T(8,128)(2,1)S(1)}, u32[]{:S(2)}, u32[]{:S(2)}) collective-permute-start(bf16[1,1,2,128,2176]{4,3,2,1,0:T(8,128)(2,1)} %add_convert_fusion.3), channel_id=1, source_target_pairs={{0,16},{4,20},{8,24},{12,28},{16,0},{20,4},{24,8},{28,12},{1,17},{... | collective-permute-start | bytes 3342344 | tf_op jit(solution)/shard_map/ppermute | solution.py:868
  413.0 48.3 %collective-permute-start.48 = (bf16[2,1,4,128,1024]{4,3,2,1,0:T(8,128)(2,1)}, bf16[2,1,4,128,1024]{4,3,2,1,0:T(8,128)(2,1)}, u32[]{:S(2)}, u32[]{:S(2)}) collective-permute-start(bf16[2,1,4,128,1024]{4,3,2,1,0:T(8,128)(2,1)} %add_convert_fusion.2), channel_id=1, source_target_pairs={{0,8},{4,12},{8,0},{12,4},{16,24},{20,28},{24,16},{28,20},{1,9},{5... | collective-permute-start | bytes 6291464 | tf_op jit(solution)/shard_map/ppermute | solution.py:868
  431.5 33.7 %collective-permute-start.44 = (bf16[4,4,128,512]{3,2,1,0:T(8,128)(2,1)}, bf16[4,4,128,512]{3,2,1,0:T(8,128)(2,1)S(1)}, u32[]{:S(2)}, u32[]{:S(2)}) collective-permute-start(bf16[4,4,128,512]{3,2,1,0:T(8,128)(2,1)} %get-tuple-element.198), channel_id=1, source_target_pairs={{0,4},{4,0},{8,12},{12,8},{16,20},{20,16},{24,28},{28,24},{1,5},{5... | collective-permute-start | bytes 6291464 | tf_op jit(solution)/shard_map/ppermute | solution.py:868
  435.0 25.5 %collective-permute-start.47 = (bf16[1,1,128,2176]{3,2,1,0:T(8,128)(2,1)S(1)}, bf16[1,1,128,2176]{3,2,1,0:T(8,128)(2,1)S(1)}, u32[]{:S(2)}, u32[]{:S(2)}) collective-permute-start(bf16[1,1,128,2176]{3,2,1,0:T(8,128)(2,1)S(1)} %add_convert_fusion.8), channel_id=1, source_target_pairs={{0,1},{1,0},{2,3},{3,2},{4,5},{5,4},{6,7},{7,6},{8,9},{9,8},{10,11... | collective-permute-start | bytes 1671176 | tf_op jit(solution)/shard_map/ppermute | solution.py:935
  463.4 32.1 %collective-permute-start.49 = (bf16[1,1,4,128,1024]{4,3,2,1,0:T(8,128)(2,1)S(1)}, bf16[1,1,4,128,1024]{4,3,2,1,0:T(8,128)(2,1)S(1)}, u32[]{:S(2)}, u32[]{:S(2)}) collective-permute-start(bf16[1,1,4,128,1024]{4,3,2,1,0:T(8,128)(2,1)S(1)} %add_convert_fusion.5), channel_id=1, source_target_pairs={{0,16},{4,20},{8,24},{12,28},{16,0},{20,4},{24,8},{28,12},{1,17},{... | collective-permute-start | bytes 3145736 | tf_op jit(solution)/shard_map/ppermute | solution.py:868
  465.6 29.9 %collective-permute-start.45 = (bf16[2,1,4,128,512]{4,3,2,1,0:T(8,128)(2,1)S(1)}, bf16[2,1,4,128,512]{4,3,2,1,0:T(8,128)(2,1)S(1)}, u32[]{:S(2)}, u32[]{:S(2)}) collective-permute-start(bf16[2,1,4,128,512]{4,3,2,1,0:T(8,128)(2,1)S(1)} %add_convert_fusion.6), channel_id=1, source_target_pairs={{0,8},{4,12},{8,0},{12,4},{16,24},{20,28},{24,16},{28,20},{1,9},{5... | collective-permute-start | bytes 3145736 | tf_op jit(solution)/shard_map/ppermute | solution.py:868
  467.5 28.0 %collective-permute-start.50 = (bf16[1,128,2176]{2,1,0:T(8,128)(2,1)S(1)}, bf16[1,128,2176]{2,1,0:T(8,128)(2,1)S(1)}, u32[]{:S(2)}, u32[]{:S(2)}) collective-permute-start(bf16[1,128,2176]{2,1,0:T(8,128)(2,1)S(1)} %fusion.3), channel_id=1, source_target_pairs={{0,2},{1,3},{2,0},{3,1},{4,6},{5,7},{6,4},{7,5},{8,10},{9,11},{10,... | collective-permute-start | bytes 1671176 | tf_op jit(solution)/shard_map/ppermute | solution.py:935
  513.1 25.1 %collective-permute-start.58 = (bf16[1,2,128,2176]{3,2,1,0:T(8,128)(2,1)S(1)}, bf16[1,2,128,2176]{3,2,1,0:T(8,128)(2,1)S(1)}, u32[]{:S(2)}, u32[]{:S(2)}) collective-permute-start(bf16[1,2,128,2176]{3,2,1,0:T(8,128)(2,1)S(1)} %pad_maximum_fusion.11), channel_id=1, source_target_pairs={{0,16},{4,20},{8,24},{12,28},{16,0},{20,4},{24,8},{28,12},{1,17},{... | collective-permute-start | bytes 3342344 | tf_op jit(solution)/shard_map/ppermute | solution.py:868
  521.2 81.2 %collective-permute-start.70 = (bf16[256,1024]{1,0:T(8,128)(2,1)}, bf16[256,1024]{1,0:T(8,128)(2,1)}, u32[]{:S(2)}, u32[]{:S(2)}) collective-permute-start(bf16[256,1024]{1,0:T(8,128)(2,1)} %get-tuple-element.265), channel_id=1, source_target_pairs={{2,0},{6,1},{4,2},{0,3},{3,4},{7,5},{5,6},{1,7},{10,8},{14,9},{12,... | collective-permute-start | bytes 1572872 | tf_op jit(solution)/shard_map/ppermute | solution.py:926
  548.4 54.6 %collective-permute-start.34 = (bf16[256,1024]{1,0:T(8,128)(2,1)}, bf16[256,1024]{1,0:T(8,128)(2,1)}, u32[]{:S(2)}, u32[]{:S(2)}) collective-permute-start(bf16[256,1024]{1,0:T(8,128)(2,1)} %get-tuple-element.264), channel_id=1, source_target_pairs={{0,0},{4,1},{6,2},{2,3},{1,4},{5,5},{7,6},{3,7},{8,8},{12,9},{14,1... | collective-permute-start | bytes 1572872 | tf_op jit(solution)/shard_map/ppermute | solution.py:926
  574.5 32.9 %collective-permute-start.72 = (bf16[256,1024]{1,0:T(8,128)(2,1)}, bf16[256,1024]{1,0:T(8,128)(2,1)}, u32[]{:S(2)}, u32[]{:S(2)}) collective-permute-start(bf16[256,1024]{1,0:T(8,128)(2,1)} %get-tuple-element.263), channel_id=1, source_target_pairs={{2,0},{6,1},{4,2},{0,3},{3,4},{7,5},{5,6},{1,7},{10,8},{14,9},{12,... | collective-permute-start | bytes 1572872 | tf_op jit(solution)/shard_map/ppermute | solution.py:926
  584.2 23.1 %collective-permute-start.71 = (bf16[256,1024]{1,0:T(8,128)(2,1)}, bf16[256,1024]{1,0:T(8,128)(2,1)}, u32[]{:S(2)}, u32[]{:S(2)}) collective-permute-start(bf16[256,1024]{1,0:T(8,128)(2,1)} %get-tuple-element.262), channel_id=1, source_target_pairs={{0,0},{4,1},{6,2},{2,3},{1,4},{5,5},{7,6},{3,7},{8,8},{12,9},{14,1... | collective-permute-start | bytes 1572872 | tf_op jit(solution)/shard_map/ppermute | solution.py:926
  (101 other events, 1025.4 us)
